TPU v7x, 32 devices: a whole 2x2x4 slice. The times are simulated.
32 devices in a mesh: seq: 8 (over z, y), tensor: 4 (over x, core).
Axes of the slice: x: 2, y: 2, z: 4, core: 2. Of those that a mesh axis runs over, the one named last changes fastest.
Arguments:
- tokens_in: bfloat16 [8192, 2048], P(('seq', 'tensor')), may hold values from -6 to 6
- w_query: bfloat16 [2048, 256], P(None, 'tensor'), may hold values from -0.125 to 0.125
- w_key: bfloat16 [2048, 256], P(None, 'tensor'), may hold values from -0.125 to 0.125
- w_value: bfloat16 [2048, 2048], P(None, 'tensor'), may hold values from -0.125 to 0.125
- w_output: bfloat16 [2048, 2048], P('tensor'), may hold values from -0.125 to 0.125
- conv_taps: float32 [3, 2048], P(None, 'tensor'), may hold values from -3 to 3
- norm_gain: float32 [2048], P('tensor'), may hold values from 0.1 to 1.9
- grad_out: bfloat16 [8192, 2048], P(('seq', 'tensor')), may hold values from -6 to 6
Outputs:
- layer_out: bfloat16 [8192, 2048], P(('seq', 'tensor'))
- grad_in: bfloat16 [8192, 2048], P(('seq', 'tensor'))
- grad_wq: bfloat16 [2048, 256], P('seq', 'tensor')
- grad_wk: bfloat16 [2048, 256], P('seq', 'tensor')
- grad_wv: bfloat16 [2048, 2048], P('seq', 'tensor')
- grad_wo: bfloat16 [2048, 2048], P('tensor', 'seq')
- grad_taps: float32 [3, 2048], P(None, 'tensor')
- grad_gain: float32 [2048], P('tensor')
All inputs are finite; a program needn't handle non-finite values.
Results may differ from a plain program's by a relative error of at most 0.018.
Values may be sent and summed in bfloat16 or wider, within the bound.
No kernel may reach another device: no remote copies, remote signals or barrier semaphores. Data moves between devices by JAX's collectives and lax.ppermute only.
A program may use at most 192 MiB of HBM per device.

v0:
```python
import functools

import jax
import jax.numpy as jnp
import numpy as np
from jax import lax
from jax.experimental import pallas as pl
from jax.experimental.pallas import tpu as pltpu
from jax.sharding import PartitionSpec as P

VD = 128
FK = 16
FEATS = 153
STATE_ROWS = 160
LANES = 256
EPS = 1e-6

bf16 = jnp.bfloat16
f32 = jnp.float32
CONTRACT_COLS = (((1,), (1,)), ((), ()))
CONTRACT_ROWS = (((0,), (0,)), ((), ()))


def mm(a, b):
    return jnp.dot(a, b, preferred_element_type=f32)


def mm_nt(a, b):
    return lax.dot_general(a, b, CONTRACT_COLS, preferred_element_type=f32)


def mm_tn(a, b):
    return lax.dot_general(a, b, CONTRACT_ROWS, preferred_element_type=f32)


def feature_tables(heads):
    e1 = np.zeros((FK, LANES), np.float32)
    e2 = np.zeros((FK, LANES), np.float32)
    weight = np.zeros((LANES,), np.float32)
    bias = np.zeros((8, LANES), np.float32)
    bias[0, 0] = bias[1, 0] = weight[0] = 1.0
    for i in range(FK):
        e1[i, 1 + i] = 1.0
        bias[1, 1 + i] = 1.0
        weight[1 + i] = FK ** -0.5
    column = 1 + FK
    for i in range(FK):
        for j in range(i, FK):
            e1[i, column] = 1.0
            e2[j, column] = 1.0
            weight[column] = 1.0 / FK if i < j else 0.5 / FK
            column += 1
    def spread(table):
        out = np.zeros((heads, FK, heads, LANES), np.float32)
        for h in range(heads):
            out[h, :, h] = table
        return jnp.asarray(out.reshape(heads * FK, heads * LANES), bf16)
    return spread(e1), spread(e1 * weight), spread(e2), jnp.asarray(bias)


def features(rows, e1_ref, e2_ref, bias_ref, head):
    cols = slice(head * LANES, (head + 1) * LANES)
    first = mm(rows, e1_ref[:, cols]) + bias_ref[0:1, :]
    second = mm(rows, e2_ref[:, cols]) + bias_ref[1:2, :]
    return first, second


def features_pull(grad, first, second, e1_ref, e2_ref, head):
    cols = slice(head * LANES, (head + 1) * LANES)
    return mm_nt((grad * second).astype(bf16), e1_ref[:, cols]) + mm_nt(
        (grad * first).astype(bf16), e2_ref[:, cols]
    )


def head_only(rows, head, scale):
    lane = lax.broadcasted_iota(jnp.int32, rows.shape, 1)
    keep = (lane >= head * FK) & (lane < (head + 1) * FK)
    return jnp.where(keep, rows.astype(f32) * scale, 0.0).astype(bf16)


def full_state(state):
    return jnp.concatenate(
        [state.astype(bf16), jnp.zeros((LANES - STATE_ROWS, VD), bf16)], axis=0
    )


def conv_kernel(heads, parts, *refs):
    place_ref = refs[0]
    pieces = refs[1 : 1 + parts]
    halo_ref, taps_ref, e1_ref, e2_ref, bias_ref = refs[1 + parts : 6 + parts]
    q_ref, k_ref, v_ref, mixed_ref, state_ref, total_ref = refs[6 + parts : 12 + parts]
    piece_scr, prev_scr, total_scr = refs[12 + parts :]
    chunk = pl.program_id(0)
    relative = chunk ^ place_ref[0]
    for j in range(parts):
        @pl.when(relative == j)
        def _(j=j):
            piece_scr[...] = pieces[j][...]

    @pl.when(chunk == 0)
    def _():
        prev_scr[...] = halo_ref[...].astype(f32)
        total_scr[...] = jnp.zeros_like(total_scr)

    vw = heads * VD
    kw = heads * FK
    values = piece_scr[:, :vw]
    q = piece_scr[:, vw : vw + kw]
    k = piece_scr[:, vw + kw : vw + 2 * kw]
    q_ref[...] = q
    k_ref[...] = k
    v_ref[...] = values
    wide = values.astype(f32)
    rows = wide.shape[0]
    at = lax.broadcasted_iota(jnp.int32, wide.shape, 0)
    before1 = prev_scr[7:8, :]
    before2 = prev_scr[6:7, :]
    lag1 = jnp.where(at == 0, before1, pltpu.roll(wide, 1, 0))
    lag2 = jnp.where(at == 0, before2, jnp.where(at == 1, before1, pltpu.roll(wide, 2, 0)))
    prev_scr[...] = wide[rows - 8 :, :]
    mixed = (taps_ref[0:1, :] * wide + taps_ref[1:2, :] * lag1 + taps_ref[2:3, :] * lag2).astype(
        bf16
    )
    mixed_ref[...] = mixed
    for h in range(heads):
        first, second = features(k, e1_ref, e2_ref, bias_ref, h)
        phi = (first * second).astype(bf16)
        state = mm_tn(phi, mixed[:, h * VD : (h + 1) * VD])[:STATE_ROWS]
        state_ref[0, h] = state.astype(bf16)
        total_scr[h] += state

    @pl.when(chunk == pl.num_programs(0) - 1)
    def _():
        total_ref[...] = total_scr[...].astype(bf16)


def attend_kernel(heads, *refs):
    (
        place_ref, q_ref, k_ref, mixed_ref, state_ref, carried_ref, ga_ref, gain_ref,
        e1q_ref, e1k_ref, e2_ref, bias_ref,
        attn_ref, gq_ref, dk_ref, dv_ref, gstate_ref, gtotal_ref, gain_sum_ref, halo_ref,
        run_scr, gtotal_scr,
    ) = refs
    chunk = pl.program_id(0)

    @pl.when(chunk == 0)
    def _():
        run_scr[...] = carried_ref[...].astype(f32)
        gtotal_scr[...] = jnp.zeros_like(gtotal_scr)
        gain_sum_ref[...] = jnp.zeros_like(gain_sum_ref)

    q = q_ref[...]
    k = k_ref[...]
    rows = q.shape[0]
    row = lax.broadcasted_iota(jnp.int32, (rows, rows), 0)
    col = lax.broadcasted_iota(jnp.int32, (rows, rows), 1)
    causal = row >= col
    dq = jnp.zeros(q.shape, f32)
    dk = jnp.zeros(q.shape, f32)
    for h in range(heads):
        lanes = slice(h * VD, (h + 1) * VD)
        v = mixed_ref[:, lanes]
        first, second = features(q, e1q_ref, e2_ref, bias_ref, h)
        phi = (first * second).astype(bf16)
        state = full_state(run_scr[h])
        kh = head_only(k, h, FK ** -0.5)
        qh = head_only(q, h, FK ** -0.5)
        u = mm_nt(q, kh)
        weight = jnp.where(causal, 1.0 + u + 0.5 * u * u, 0.0).astype(bf16)
        summed = mm(weight, v) + mm(phi, state)
        scale = lax.rsqrt(jnp.mean(summed * summed, axis=-1, keepdims=True) + EPS)
        unit = summed * scale
        gain = gain_ref[0:1, lanes]
        attn_ref[0, :, lanes] = (unit * gain).astype(bf16)
        ga = ga_ref[0, :, lanes].astype(f32)
        gu = ga * unit
        gain_sum_ref[0:1, lanes] += jnp.sum(gu, axis=0, keepdims=True)
        ds = scale * (ga * gain - unit * jnp.mean(gu * gain, axis=-1, keepdims=True))
        ds = ds.astype(bf16)
        dw = mm_nt(ds, v).astype(bf16).astype(f32)
        du = jnp.where(causal, dw * (1.0 + u), 0.0).astype(bf16)
        dq += mm(du, kh)
        dk += mm_tn(du, qh)
        dv_ref[:, lanes] = mm_tn(weight, ds).astype(bf16)
        gstate = mm_tn(phi, ds)[:STATE_ROWS]
        gstate_ref[0, h] = gstate.astype(bf16)
        gtotal_scr[h] += gstate
        dphi = mm_nt(ds, state)
        dq += features_pull(dphi, first, second, e1q_ref, e2_ref, h)
        run_scr[h] += state_ref[0, h].astype(f32)

        @pl.when(chunk == 0)
        def _(h=h, lanes=lanes, gstate=gstate):
            kfirst, ksecond = features(k[0:16, :], e1k_ref, e2_ref, bias_ref, h)
            kphi = (kfirst * ksecond).astype(bf16)
            own = mm(kphi, full_state(gstate))
            halo_ref[:, lanes] = (dv_ref[0:16, lanes].astype(f32) - own)[0:8]

    gq_ref[...] = dq.astype(bf16)
    dk_ref[...] = dk

    @pl.when(chunk == pl.num_programs(0) - 1)
    def _():
        gtotal_ref[...] = gtotal_scr[...].astype(bf16)


def finish_kernel(heads, *refs):
    (
        place_ref, q_grad_ref, k_ref, v_ref, mixed_ref, dk_ref, dv_ref, gstate_ref, gin_ref,
        taps_ref, hk_ref, hv_ref, gain_ref, e1_ref, e2_ref, bias_ref,
        cols_ref, sums_ref,
        run_scr, next_scr, mixed_scr,
    ) = refs
    step = pl.program_id(0)

    @pl.when(step == 0)
    def _():
        run_scr[...] = gin_ref[...].astype(f32)
        sums_ref[...] = jnp.zeros_like(sums_ref)
        sums_ref[3:4, :] = gain_ref[0:1, :]
        hk = hk_ref[...]
        for h in range(heads):
            lanes = slice(h * VD, (h + 1) * VD)
            first, second = features(hk, e1_ref, e2_ref, bias_ref, h)
            phi = (first * second).astype(bf16)
            next_scr[:, lanes] = hv_ref[:, lanes] + mm(phi, full_state(gin_ref[h]))[0:8]

    k = k_ref[...]
    dk = dk_ref[...]
    for h in range(heads):
        lanes = slice(h * VD, (h + 1) * VD)
        first, second = features(k, e1_ref, e2_ref, bias_ref, h)
        phi = (first * second).astype(bf16)
        state = full_state(run_scr[h])
        mixed_scr[:, lanes] = dv_ref[:, lanes].astype(f32) + mm(phi, state)
        dphi = mm_nt(mixed_ref[:, lanes], state)
        dk += features_pull(dphi, first, second, e1_ref, e2_ref, h)
        run_scr[h] += gstate_ref[0, h].astype(f32)
    gm = mixed_scr[...]
    rows = gm.shape[0]
    at = lax.broadcasted_iota(jnp.int32, gm.shape, 0)
    after0 = next_scr[0:1, :]
    after1 = next_scr[1:2, :]
    lead1 = jnp.where(at == rows - 1, after0, pltpu.roll(gm, rows - 1, 0))
    lead2 = jnp.where(
        at == rows - 1, after1, jnp.where(at == rows - 2, after0, pltpu.roll(gm, rows - 2, 0))
    )
    next_scr[...] = gm[0:8, :]
    gv = taps_ref[0:1, :] * gm + taps_ref[1:2, :] * lead1 + taps_ref[2:3, :] * lead2
    values = v_ref[...].astype(f32)
    sums_ref[0:1, :] += jnp.sum(gm * values, axis=0, keepdims=True)
    sums_ref[1:2, :] += jnp.sum(lead1 * values, axis=0, keepdims=True)
    sums_ref[2:3, :] += jnp.sum(lead2 * values, axis=0, keepdims=True)
    vw = heads * VD
    kw = heads * FK
    cols_ref[0, :, :vw] = gv.astype(bf16)
    cols_ref[0, :, vw : vw + kw] = q_grad_ref[...]
    cols_ref[0, :, vw + kw :] = dk.astype(bf16)


def whole(shape):
    return pl.BlockSpec(shape, lambda *a, n=len(shape): (0,) * n)


def call(kernel, place, inputs, in_specs, out_shapes, out_specs, scratch, steps, flops):
    moved = sum(int(np.prod(x.shape)) * x.dtype.itemsize for x in inputs) + sum(
        int(np.prod(x.shape)) * x.dtype.itemsize for x in out_shapes
    )
    return pl.pallas_call(
        kernel,
        out_shape=out_shapes,
        grid_spec=pltpu.PrefetchScalarGridSpec(
            num_scalar_prefetch=1,
            grid=(steps,),
            in_specs=in_specs,
            out_specs=out_specs,
            scratch_shapes=scratch,
        ),
        compiler_params=pltpu.CompilerParams(
            dimension_semantics=("arbitrary",), vmem_limit_bytes=48 << 20
        ),
        cost_estimate=pl.CostEstimate(flops=flops, bytes_accessed=moved, transcendentals=0),
    )(place, *inputs)


def flip(x, axis, mask):
    n = lax.axis_size(axis)
    return lax.ppermute(x, axis, [(i, i ^ mask) for i in range(n)])


def gathered(x, after=None):
    n = lax.axis_size("tensor")
    if after is not None:
        x, _ = lax.optimization_barrier((x, after))
    pieces = [x, flip(x, "tensor", 1)]
    for j in range(2, n, 2):
        far = flip(x, "tensor", j)
        pieces += [far, flip(far, "tensor", 1)]
    return pieces


def scattered(partial_of):
    n = lax.axis_size("tensor")
    odd = partial_of(list(range(1, n, 2))).astype(bf16)
    got = flip(odd, "tensor", 1)
    rows = got.shape[0] // (n // 2)
    total = None
    for i, j in list(enumerate(range(0, n, 2)))[::-1]:
        part = partial_of([j]) + got[i * rows : (i + 1) * rows].astype(f32)
        if j:
            part = flip(part.astype(bf16), "tensor", j).astype(f32)
        total = part if total is None else total + part
    return total.astype(bf16)


def running(state, reverse):
    n, place = lax.axis_size("seq"), lax.axis_index("seq")
    before = jnp.zeros(state.shape, f32)
    total = state
    mask = 1
    while mask < n:
        got = flip(total.astype(bf16), "seq", mask).astype(f32)
        upper = (place & mask) != 0
        before += jnp.where(upper != reverse, got, 0.0)
        total = total.astype(f32) + got
        mask *= 2
    return before.astype(bf16)


def halved(blocks):
    n = lax.axis_size("seq")
    mask = 1
    while mask < n:
        pairs = blocks.reshape((blocks.shape[0] // 2, 2) + blocks.shape[1:])
        got = flip(pairs[:, 1], "seq", mask)
        blocks = (pairs[:, 0].astype(f32) + got.astype(f32)).astype(bf16)
        mask *= 2
    return blocks[0]


def summed_over(x, axis):
    mask = 1
    while mask < lax.axis_size(axis):
        x = x + flip(x, axis, mask)
        mask *= 2
    return x


def tn_kernel(scale, parts, relative, *refs):
    left = refs[1 : 1 + parts]
    right = refs[1 + parts : 1 + 2 * parts]
    out_ref = refs[1 + 2 * parts]
    total = mm_tn(left[0][...], right[0][...])
    for a, b in zip(left[1:], right[1:]):
        total += mm_tn(a[...], b[...])
    out_ref[0] = (total * scale).astype(bf16)


def out_blocks(attn, cotangent, scale):
    n, place = lax.axis_size("seq"), lax.axis_index("seq")
    parts, rows, vw = attn.shape
    width = cotangent[0].shape[1] // n
    if width % 128:
        full = sum(mm_tn(attn[j], cotangent[j]) for j in range(parts)) * scale
        full = full.astype(bf16).reshape(vw, n, width).transpose(1, 0, 2)
        return jnp.take(full, jnp.arange(n) ^ place, axis=0)
    return call(
        functools.partial(tn_kernel, scale, parts, True),
        place.reshape(1).astype(jnp.int32),
        [attn[j] for j in range(parts)] + list(cotangent),
        [whole((rows, vw))] * parts
        + [pl.BlockSpec((rows, width), lambda i, p: (0, i ^ p[0]))] * parts,
        [jax.ShapeDtypeStruct((n, vw, width), bf16)],
        [pl.BlockSpec((1, vw, width), lambda i, p: (i, 0, 0))],
        [], n, 2 * parts * rows * vw * width * n,
    )[0]


def in_blocks(pieces, cols, scale):
    n, place = lax.axis_size("seq"), lax.axis_index("seq")
    parts, rows, cw = cols.shape
    width = pieces[0].shape[1] // n
    if width % 128:
        full = sum(mm_tn(pieces[j], cols[j]) for j in range(parts)) * scale
        full = full.astype(bf16).reshape(n, width, cw)
        return jnp.take(full, jnp.arange(n) ^ place, axis=0)
    return call(
        functools.partial(tn_kernel, scale, parts, True),
        place.reshape(1).astype(jnp.int32),
        list(pieces) + [cols[j] for j in range(parts)],
        [pl.BlockSpec((rows, width), lambda i, p: (0, i ^ p[0]))] * parts
        + [whole((rows, cw))] * parts,
        [jax.ShapeDtypeStruct((n, width, cw), bf16)],
        [pl.BlockSpec((1, width, cw), lambda i, p: (i, 0, 0))],
        [], n, 2 * parts * rows * cw * width * n,
    )[0]


def per_device(tokens_in, w_query, w_key, w_value, w_output, conv_taps, norm_gain, grad_out):
    nt, ns = lax.axis_size("tensor"), lax.axis_size("seq")
    rows, depth = tokens_in.shape
    length = rows * nt
    kw, vw = w_query.shape[1], w_value.shape[1]
    heads = vw // VD
    grad_scale = float(length * ns) ** -0.5
    place = lax.axis_index("tensor").reshape(1).astype(jnp.int32)
    e1q, e1k, e2, bias = feature_tables(heads)

    tail = tokens_in[rows - 2 :]
    above = sum(
        lax.ppermute(
            tail, ("seq", "tensor"), [(s * nt + nt - 1, (s + 1) * nt + i) for s in range(ns - 1)]
        )
        for i in range(nt)
    )
    tokens = gathered(tokens_in)
    weights = jnp.concatenate([w_value, w_query, w_key], axis=1)
    cw = vw + 2 * kw
    projected = [mm(piece, weights).astype(bf16) for piece in tokens]
    halo = jnp.pad(mm(above, w_value).astype(bf16), ((6, 0), (0, 0)))

    state_shape = (heads, STATE_ROWS, VD)
    at_chunk = lambda i, p: (i, 0)
    at_state = lambda i, p: (i, 0, 0, 0)
    at_piece = lambda i, p: (i ^ p[0], 0, 0)
    tables = [whole(e1q.shape), whole(e2.shape), whole(bias.shape)]
    q, k, values, mixed, states, total = call(
        functools.partial(conv_kernel, heads, nt),
        place,
        projected + [halo, conv_taps, e1k, e2, bias],
        [whole((rows, cw))] * nt + [whole((8, vw)), whole((3, vw))] + tables,
        [
            jax.ShapeDtypeStruct((length, kw), bf16),
            jax.ShapeDtypeStruct((length, kw), bf16),
            jax.ShapeDtypeStruct((length, vw), bf16),
            jax.ShapeDtypeStruct((length, vw), bf16),
            jax.ShapeDtypeStruct((nt,) + state_shape, bf16),
            jax.ShapeDtypeStruct(state_shape, bf16),
        ],
        [
            pl.BlockSpec((rows, kw), at_chunk),
            pl.BlockSpec((rows, kw), at_chunk),
            pl.BlockSpec((rows, vw), at_chunk),
            pl.BlockSpec((rows, vw), at_chunk),
            pl.BlockSpec((1,) + state_shape, at_state),
            whole(state_shape),
        ],
        [
            pltpu.VMEM((rows, cw), bf16),
            pltpu.VMEM((8, vw), f32),
            pltpu.VMEM(state_shape, f32),
        ],
        nt, 2 * length * vw * 256 * 3,
    )
    carried = running(total, False)

    cotangent = gathered(grad_out, after=tokens[2])
    grad_attn = jnp.stack([mm_nt(piece, w_output).astype(bf16) for piece in cotangent])

    attn, gq, dk, dv, gstates, gtotal, gain_sum, hv = call(
        functools.partial(attend_kernel, heads),
        place,
        [q, k, mixed, states, carried, grad_attn, norm_gain.reshape(1, vw), e1q, e1k, e2, bias],
        [
            pl.BlockSpec((rows, kw), at_chunk),
            pl.BlockSpec((rows, kw), at_chunk),
            pl.BlockSpec((rows, vw), at_chunk),
            pl.BlockSpec((1,) + state_shape, at_state),
            whole(state_shape),
            pl.BlockSpec((1, rows, vw), at_piece),
            whole((1, vw)),
            whole(e1q.shape),
        ]
        + tables,
        [
            jax.ShapeDtypeStruct((nt, rows, vw), bf16),
            jax.ShapeDtypeStruct((length, kw), bf16),
            jax.ShapeDtypeStruct((length, kw), f32),
            jax.ShapeDtypeStruct((length, vw), bf16),
            jax.ShapeDtypeStruct((nt,) + state_shape, bf16),
            jax.ShapeDtypeStruct(state_shape, bf16),
            jax.ShapeDtypeStruct((8, vw), f32),
            jax.ShapeDtypeStruct((8, vw), f32),
        ],
        [
            pl.BlockSpec((1, rows, vw), at_piece),
            pl.BlockSpec((rows, kw), at_chunk),
            pl.BlockSpec((rows, kw), at_chunk),
            pl.BlockSpec((rows, vw), at_chunk),
            pl.BlockSpec((1,) + state_shape, at_state),
            whole(state_shape),
            whole((8, vw)),
            whole((8, vw)),
        ],
        [pltpu.VMEM(state_shape, f32), pltpu.VMEM(state_shape, f32)],
        nt, 2 * length * vw * 256 * 9,
    )
    gin = running(gtotal, True)
    down = [(i + 1, i) for i in range(ns - 1)]
    next_v = lax.ppermute(hv, "seq", down)
    next_k = lax.ppermute(k[0:16], "seq", down)

    layer_out = scattered(
        lambda which: mm(jnp.concatenate([attn[j] for j in which], axis=0), w_output)
    )
    grad_wo = halved(out_blocks(attn, cotangent, grad_scale))

    last = lambda i, p: (nt - 1 - i, 0)
    last_state = lambda i, p: (nt - 1 - i, 0, 0, 0)
    cols, sums = call(
        functools.partial(finish_kernel, heads),
        place,
        [gq, k, values, mixed, dk, dv, gstates, gin, conv_taps, next_k, next_v, gain_sum, e1k, e2, bias],
        [
            pl.BlockSpec((rows, kw), last),
            pl.BlockSpec((rows, kw), last),
            pl.BlockSpec((rows, vw), last),
            pl.BlockSpec((rows, vw), last),
            pl.BlockSpec((rows, kw), last),
            pl.BlockSpec((rows, vw), last),
            pl.BlockSpec((1,) + state_shape, last_state),
            whole(state_shape),
            whole((3, vw)),
            whole((16, kw)),
            whole((8, vw)),
            whole((8, vw)),
        ]
        + tables,
        [
            jax.ShapeDtypeStruct((nt, rows, cw), bf16),
            jax.ShapeDtypeStruct((8, vw), f32),
        ],
        [
            pl.BlockSpec((1, rows, cw), lambda i, p: ((nt - 1 - i) ^ p[0], 0, 0)),
            whole((8, vw)),
        ],
        [
            pltpu.VMEM(state_shape, f32),
            pltpu.VMEM((8, vw), f32),
            pltpu.VMEM((rows, vw), f32),
        ],
        nt, 2 * length * vw * 256 * 6,
    )
    grad_in = scattered(
        lambda which: mm_nt(jnp.concatenate([cols[j] for j in which], axis=0), weights)
    )
    in_share = halved(in_blocks(tokens, cols, grad_scale))
    sums = summed_over(sums, "seq") * grad_scale
    grad_wv = in_share[:, :vw]
    grad_wq = in_share[:, vw : vw + kw]
    grad_wk = in_share[:, vw + kw :]
    return (layer_out, grad_in, grad_wq, grad_wk, grad_wv, grad_wo, sums[0:3], sums[3])


def solution(mesh):
    return jax.shard_map(
        per_device,
        mesh=mesh,
        in_specs=(
            P(("seq", "tensor"), None),
            P(None, "tensor"),
            P(None, "tensor"),
            P(None, "tensor"),
            P("tensor", None),
            P(None, "tensor"),
            P("tensor"),
            P(("seq", "tensor"), None),
        ),
        out_specs=(
            P(("seq", "tensor"), None),
            P(("seq", "tensor"), None),
            P("seq", "tensor"),
            P("seq", "tensor"),
            P("seq", "tensor"),
            P("tensor", "seq"),
            P(None, "tensor"),
            P("tensor"),
        ),
        check_vma=False,
    )
```

profile of v0, /device:TPU:0, one launch (start us, length us, event | category | flops | bytes accessed | tf_op | source)
XLA Modules:
  0.0 223.8 jit_solution(3507308195127478443)
XLA Ops:
  0.6 3.0 %collective-permute-start.1 = (bf16[256,2048]{1,0:T(8,128)(2,1)}, bf16[256,2048]{1,0:T(8,128)(2,1)}, u32[]{:S(2)}, u32[]{:S(2)}) collective-permute-start(bf16[256,2048]{1,0:T(8,128)(2,1)} %refs_1_.1), channel_id=1, source_target_pairs={{0,2},{1,3},{2,0},{3,1},{4,6},{5,7},{6,4},{7,5},{8,10},{9,11},{10,... | collective-permute-start | bytes 3145736 | tf_op jit(solution)/shard_map/ppermute | solution.py:288
  9.8 17.5 %collective-permute-done.1.refs_3_ = bf16[256,2048]{1,0:T(8,128)(2,1)} collective-permute-done((bf16[256,2048]{1,0:T(8,128)(2,1)}, bf16[256,2048]{1,0:T(8,128)(2,1)}, u32[]{:S(2)}, u32[]{:S(2)}) %collective-permute-start.1) | collective-permute-done | bytes 1048608 | tf_op jit(solution)/shard_map/ppermute | solution.py:288
  27.3 2.9 %fusion.4.refs_1_ = bf16[256,640]{1,0:T(8,128)(2,1)S(1)} fusion(bf16[256,2048]{1,0:T(8,128)(2,1)} %refs_1_.1, bf16[2048,64]{1,0:T(8,128)(2,1)S(1)} %copy.31, bf16[2048,64]{1,0:T(8,128)(2,1)S(1)} %copy.30, bf16[2048,512]{1,0:T(8,128)(2,1)} %param.15), kind=kOutput, calls=%fused_computation.25 | convolution fusion | flops 679116800 | bytes 3997696 | tf_op jit(solution)/shard_map/dot_general | solution.py:25
  30.3 2.1 convolution_convert_fusion.10
  34.3 2.9 %fusion.6.refs_3_ = bf16[256,640]{1,0:T(8,128)(2,1)S(1)} fusion(bf16[256,2048]{1,0:T(8,128)(2,1)} %collective-permute-done.1.refs_3_, bf16[2048,64]{1,0:T(8,128)(2,1)S(1)} %copy-done.21, bf16[2048,64]{1,0:T(8,128)(2,1)S(1)} %copy-done.17, bf16[2048,512]{1,0:T(8,128)(2,1)} %param.15), kind=kOutput, calls=%fused_computation.27 | convolution fusion | flops 679116800 | bytes 3997696 | tf_op jit(solution)/shard_map/dot_general | solution.py:25
  37.2 2.2 fusion.5.refs_2_
  39.5 2.3 %fusion.7.refs_4_ = bf16[256,640]{1,0:T(8,128)(2,1)S(1)} fusion(bf16[256,2048]{1,0:T(8,128)(2,1)} %collective-permute-done.2.refs_4_, bf16[2048,64]{1,0:T(8,128)(2,1)S(1)} %copy-done.21, bf16[2048,64]{1,0:T(8,128)(2,1)S(1)} %copy-done.17, bf16[2048,512]{1,0:T(8,128)(2,1)S(1)} %copy-done.14), kind=kOutput, calls=%fused_computation.28 | convolution fusion | flops 679116800 | bytes 3997696 | tf_op jit(solution)/shard_map/dot_general | solution.py:25
  41.8 5.7 %shard_map.179 = (bf16[1024,64]{1,0:T(8,128)(2,1)S(1)}, bf16[1024,64]{1,0:T(8,128)(2,1)S(1)}, bf16[1024,512]{1,0:T(8,128)(2,1)S(1)}, bf16[1024,512]{1,0:T(8,128)...) custom-call(s32[1]{0:T(128)} %bitcast.refs_0_, bf16[256,640]{1,0:T(8,128)(2,1)S(1)} %fusion.4.refs_1_, ...), custom_call_target="tpu_custom_call" | custom-call | flops 805306368 | bytes 4773888 | tf_op jit(solution)/shard_map/pallas_call | solution.py:269
  51.5 6.6 %collective-permute-done.11.refs_7_ = bf16[256,2048]{1,0:T(8,128)(2,1)S(1)} collective-permute-done((bf16[256,2048]{1,0:T(8,128)(2,1)S(1)}, bf16[256,2048]{1,0:T(8,128)(2,1)S(1)}, u32[]{:S(2)}, u32[]{:S(2)}) %collective-permute-start.11) | collective-permute-done | bytes 1048608 | tf_op jit(solution)/shard_map/ppermute | solution.py:288
  58.1 1.9 collective-permute-start.8
  60.9 4.0 %collective-permute-done.8 = bf16[4,160,128]{2,1,0:T(8,128)(2,1)S(1)} collective-permute-done((bf16[4,160,128]{2,1,0:T(8,128)(2,1)S(1)}, bf16[4,160,128]{2,1,0:T(8,128)(2,1)S(1)}, u32[]{:S(2)}, u32[]{:S(2)}) %collective-permute-start.8) | collective-permute-done | bytes 163872 | tf_op jit(solution)/shard_map/ppermute | solution.py:288
  65.0 2.8 %collective-permute-start.9 = (bf16[4,160,128]{2,1,0:T(8,128)(2,1)S(1)}, bf16[4,160,128]{2,1,0:T(8,128)(2,1)S(1)}, u32[]{:S(2)}, u32[]{:S(2)}) collective-permute-start(bf16[4,160,128]{2,1,0:T(8,128)(2,1)S(1)} %fusion.26), channel_id=1, source_target_pairs={{0,16},{4,20},{8,24},{12,28},{16,0},{20,4},{24,8},{28,12},{1,17},{... | collective-permute-start | bytes 491528 | tf_op jit(solution)/shard_map/ppermute | solution.py:288
  68.7 6.7 %collective-permute-done.9 = bf16[4,160,128]{2,1,0:T(8,128)(2,1)S(1)} collective-permute-done((bf16[4,160,128]{2,1,0:T(8,128)(2,1)S(1)}, bf16[4,160,128]{2,1,0:T(8,128)(2,1)S(1)}, u32[]{:S(2)}, u32[]{:S(2)}) %collective-permute-start.9) | collective-permute-done | bytes 163872 | tf_op jit(solution)/shard_map/ppermute | solution.py:288
  77.4 20.5 %shard_map.180 = (bf16[4,256,512]{2,1,0:T(8,128)(2,1)S(1)}, bf16[1024,64]{1,0:T(8,128)(2,1)S(1)}, f32[1024,64]{1,0:T(8,128)S(1)}, bf16[1024,512]{1,0:T(8,128)(2,...) custom-call(s32[1]{0:T(128)} %bitcast.refs_0_, ...), custom_call_target="tpu_custom_call" | custom-call | flops 2415919104 | bytes 6924288 | tf_op jit(solution)/shard_map/pallas_call | solution.py:269
  101.1 2.4 %collective-permute-done.15 = bf16[4,160,128]{2,1,0:T(8,128)(2,1)S(1)} collective-permute-done((bf16[4,160,128]{2,1,0:T(8,128)(2,1)S(1)}, bf16[4,160,128]{2,1,0:T(8,128)(2,1)S(1)}, u32[]{:S(2)}, u32[]{:S(2)}) %collective-permute-start.15) | collective-permute-done | bytes 163872 | tf_op jit(solution)/shard_map/ppermute | solution.py:288
  105.2 5.8 %shard_map.183 = bf16[8,512,256]{2,1,0:T(8,128)(2,1)} custom-call(s32[1]{0:T(128)} %bitcast.18.refs_0_, bf16[256,512]{1,0:T(8,128)(2,1)S(1)} %get-tuple-element.63.refs_1_, bf16[256,512]{1,0:T(8,128)(2,1)S(1)} %get-tuple-element.65.refs_2_, bf16[256,512]{1,0:T(8,128)(2,1)S(1)} %get-tuple-element.62.refs_3_, bf16[256,512]{1,0:T(8,128)(2,1)S(1)} %get-tuple-element.64.refs_4_, ...), custom_call_target="tpu_custom_call" | custom-call | flops 2147483648 | bytes 7340032 | tf_op jit(solution)/shard_map/pallas_call | solution.py:269
  111.0 3.4 %collective-permute-start.17 = (bf16[4,160,128]{2,1,0:T(8,128)(2,1)S(1)}, bf16[4,160,128]{2,1,0:T(8,128)(2,1)S(1)}, u32[]{:S(2)}, u32[]{:S(2)}) collective-permute-start(bf16[4,160,128]{2,1,0:T(8,128)(2,1)S(1)} %fusion.30), channel_id=1, source_target_pairs={{0,16},{4,20},{8,24},{12,28},{16,0},{20,4},{24,8},{28,12},{1,17},{... | collective-permute-start | bytes 491528 | tf_op jit(solution)/shard_map/ppermute | solution.py:288
  114.5 2.3 %slice_bitcast_fusion.2 = bf16[4,512,256]{2,1,0:T(8,128)(2,1)} fusion(bf16[4,2,512,256]{3,2,1,0:T(8,128)(2,1)} %bitcast.133), kind=kLoop, calls=%fused_computation.34 | loop fusion | bytes 2097152 | tf_op jit(solution)/shard_map/squeeze | solution.py:335
  118.1 2.7 %collective-permute-done.17 = bf16[4,160,128]{2,1,0:T(8,128)(2,1)S(1)} collective-permute-done((bf16[4,160,128]{2,1,0:T(8,128)(2,1)S(1)}, bf16[4,160,128]{2,1,0:T(8,128)(2,1)S(1)}, u32[]{:S(2)}, u32[]{:S(2)}) %collective-permute-start.17) | collective-permute-done | bytes 163872 | tf_op jit(solution)/shard_map/ppermute | solution.py:288
  120.9 6.6 %shard_map.181 = (bf16[4,256,640]{2,1,0:T(8,128)(2,1)}, f32[8,512]{1,0:T(8,128)S(1)}) custom-call(s32[1]{0:T(128)} %bitcast.refs_0_, bf16[1024,64]{1,0:T(8,128)(2,1)S(1)} %get-tuple-element.32.refs_1_, bf16[1024,64]{1,0:T(8,128)(2,1)S(1)} %get-tuple-element.26.refs_2_, bf16[1024,512]{1,0:T(8,128)(2,1)S(1)} %get-tuple-element.33.refs_3_, ...), custom_call_target="tpu_custom_call" | custom-call | flops 1610612736 | bytes 6127616 | tf_op jit(solution)/shard_map/pallas_call | solution.py:269
  130.4 8.5 %shard_map.182 = bf16[8,256,640]{2,1,0:T(8,128)(2,1)} custom-call(s32[1]{0:T(128)} %bitcast.18.refs_0_, bf16[256,2048]{1,0:T(8,128)(2,1)S(1)} %copy-done.1, bf16[256,2048]{1,0:T(8,128)(2,1)} %collective-permute-done.refs_2_, bf16[256,2048]{1,0:T(8,128)(2,1)} %collective-permute-done.1.refs_3_, bf16[256,2048]{1,0:T(8,128)(2,1)} %collective-permute-done.2.refs_4_, ...), custom_call_target="tpu_custom_call" | custom-call | flops 2684354560 | bytes 8126464 | tf_op jit(solution)/shard_map/pallas_call | solution.py:269
  142.5 2.3 %collective-permute-done.29 = f32[8,512]{1,0:T(8,128)S(1)} collective-permute-done((f32[8,512]{1,0:T(8,128)S(1)}, f32[8,512]{1,0:T(8,128)S(1)}, u32[]{:S(2)}, u32[]{:S(2)}) %collective-permute-start.29) | collective-permute-done | bytes 16416 | tf_op jit(solution)/shard_map/ppermute | solution.py:288
  146.0 1.8 convolution_convert_fusion.1
  151.6 19.3 %collective-permute-done.22 = bf16[4,256,640]{2,1,0:T(8,128)(2,1)S(1)} collective-permute-done((bf16[4,256,640]{2,1,0:T(8,128)(2,1)S(1)}, bf16[4,256,640]{2,1,0:T(8,128)(2,1)S(1)}, u32[]{:S(2)}, u32[]{:S(2)}) %collective-permute-start.22) | collective-permute-done | bytes 1310752 | tf_op jit(solution)/shard_map/ppermute | solution.py:288
  171.5 2.1 collective-permute-start.27
  173.6 1.7 add_convert_fusion.2
  176.6 15.8 %collective-permute-done.23 = bf16[2,256,640]{2,1,0:T(8,128)(2,1)S(1)} collective-permute-done((bf16[2,256,640]{2,1,0:T(8,128)(2,1)S(1)}, bf16[2,256,640]{2,1,0:T(8,128)(2,1)S(1)}, u32[]{:S(2)}, u32[]{:S(2)}) %collective-permute-start.23) | collective-permute-done | bytes 655392 | tf_op jit(solution)/shard_map/ppermute | solution.py:288
  192.7 3.3 %fusion.1 = bf16[256,2048]{1,0:T(8,128)(2,1)} fusion(bf16[512,2048]{1,0:T(8,128)(2,1)S(1)} %collective-permute-done.20, bf16[4,256,640]{2,1,0:T(8,128)(2,1)} %get-tuple-element.40, bf16[2048,64]{1,0:T(8,128)(2,1)S(1)} %copy-done.22, bf16[2048,64]{1,0:T(8,128)(2,1)S(1)} %copy-done.18, bf16[2048,512]{1,0:T(8,128)(2,1)S(1)} %copy-done.14), kind=kOutput, calls=%fused_computation.7 | convolution fusion | flops 680525824 | bytes 5046272 | tf_op jit(solution)/shard_map/dot_general | solution.py:29
  198.2 9.8 %collective-permute-done.24 = bf16[1,256,640]{2,1,0:T(8,128)(2,1)S(1)} collective-permute-done((bf16[1,256,640]{2,1,0:T(8,128)(2,1)S(1)}, bf16[1,256,640]{2,1,0:T(8,128)(2,1)S(1)}, u32[]{:S(2)}, u32[]{:S(2)}) %collective-permute-start.24) | collective-permute-done | bytes 327712 | tf_op jit(solution)/shard_map/ppermute | solution.py:288
  210.3 3.5 %add_convert_fusion.1 = bf16[256,2048]{1,0:T(8,128)(2,1)} fusion(bf16[256,2048]{1,0:T(8,128)(2,1)} %collective-permute-done.14, bf16[512,2048]{1,0:T(8,128)(2,1)} %copy-done.24, bf16[512,2048]{1,0:T(8,128)(2,1)S(1)} %copy-done, bf16[4,256,512]{2,1,0:T(8,128)(2,1)S(1)} %get-tuple-element.31), kind=kOutput, calls=%fused_computation.11 | convolution fusion | flops 539492352 | bytes 5505024 | tf_op jit(solution)/shard_map/dot_general | solution.py:25
  213.8 6.5 %collective-permute-done.21 = bf16[256,2048]{1,0:T(8,128)(2,1)} collective-permute-done((bf16[256,2048]{1,0:T(8,128)(2,1)}, bf16[256,2048]{1,0:T(8,128)(2,1)}, u32[]{:S(2)}, u32[]{:S(2)}) %collective-permute-start.21) | collective-permute-done | bytes 1048608 | tf_op jit(solution)/shard_map/ppermute | solution.py:288
  220.3 3.5 %add_convert_fusion = bf16[256,2048]{1,0:T(8,128)(2,1)} fusion(bf16[256,2048]{1,0:T(8,128)(2,1)} %collective-permute-done.21, bf16[512,2048]{1,0:T(8,128)(2,1)S(1)} %copy-done.26, bf16[4,256,640]{2,1,0:T(8,128)(2,1)} %get-tuple-element.40, bf16[2048,64]{1,0:T(8,128)(2,1)S(1)} %copy-done.23, bf16[2048,64]{1,0:T(8,128)(2,1)S(1)} %copy-done.19, ...), kind=kOutput, calls=%fused_computation.10 | convolution fusion | flops 681574400 | bytes 6094848 | tf_op jit(solution)/shard_map/dot_general | solution.py:29
  (139 shorter events, 40.2 us)
Async XLA Ops:
  0.6 48.6 %copy-start = (bf16[512,2048]{1,0:T(8,128)(2,1)S(1)}, bf16[512,2048]{1,0:T(8,128)(2,1)}, u32[]{:S(2)}) copy-start(bf16[512,2048]{1,0:T(8,128)(2,1)} %param.16) | copy-start | bytes 6291460
  0.6 26.7 %collective-permute-start.1 = (bf16[256,2048]{1,0:T(8,128)(2,1)}, bf16[256,2048]{1,0:T(8,128)(2,1)}, u32[]{:S(2)}, u32[]{:S(2)}) collective-permute-start(bf16[256,2048]{1,0:T(8,128)(2,1)} %refs_1_.1), channel_id=1, source_target_pairs={{0,2},{1,3},{2,0},{3,1},{4,6},{5,7},{6,4},{7,5},{8,10},{9,11},{10,... | collective-permute-start | bytes 3145736 | tf_op jit(solution)/shard_map/ppermute | solution.py:288
  3.7 33.6 %collective-permute-start = (bf16[256,2048]{1,0:T(8,128)(2,1)}, bf16[256,2048]{1,0:T(8,128)(2,1)}, u32[]{:S(2)}, u32[]{:S(2)}) collective-permute-start(bf16[256,2048]{1,0:T(8,128)(2,1)} %refs_1_.1), channel_id=1, source_target_pairs={{0,1},{1,0},{2,3},{3,2},{4,5},{5,4},{6,7},{7,6},{8,9},{9,8},{10,11... | collective-permute-start | bytes 3145736 | tf_op jit(solution)/shard_map/ppermute | solution.py:288
  4.5 4.7 %collective-permute-start.3 = (bf16[2,2048]{1,0:T(2,128)(2,1)S(1)}, bf16[2,2048]{1,0:T(2,128)(2,1)S(1)}, u32[]{:S(2)}, u32[]{:S(2)}) collective-permute-start(bf16[2,2048]{1,0:T(2,128)(2,1)S(1)} %slice.101), channel_id=1, source_target_pairs={{3,4},{7,8},{11,12},{15,16},{19,20},{23,24},{27,28}} | collective-permute-start | bytes 24584 | tf_op jit(solution)/shard_map/ppermute | solution.py:411
  5.1 25.2 %collective-permute-start.4 = (bf16[2,2048]{1,0:T(2,128)(2,1)S(1)}, bf16[2,2048]{1,0:T(2,128)(2,1)S(1)}, u32[]{:S(2)}, u32[]{:S(2)}) collective-permute-start(bf16[2,2048]{1,0:T(2,128)(2,1)S(1)} %slice.101), channel_id=1, source_target_pairs={{3,5},{7,9},{11,13},{15,17},{19,21},{23,25},{27,29}} | collective-permute-start | bytes 24584 | tf_op jit(solution)/shard_map/ppermute | solution.py:411
  5.8 24.5 %collective-permute-start.5 = (bf16[2,2048]{1,0:T(2,128)(2,1)S(1)}, bf16[2,2048]{1,0:T(2,128)(2,1)S(1)}, u32[]{:S(2)}, u32[]{:S(2)}) collective-permute-start(bf16[2,2048]{1,0:T(2,128)(2,1)S(1)} %slice.101), channel_id=1, source_target_pairs={{3,6},{7,10},{11,14},{15,18},{19,22},{23,26},{27,30}} | collective-permute-start | bytes 24584 | tf_op jit(solution)/shard_map/ppermute | solution.py:411
  9.1 21.2 %collective-permute-start.6 = (bf16[2,2048]{1,0:T(2,128)(2,1)S(1)}, bf16[2,2048]{1,0:T(2,128)(2,1)S(1)}, u32[]{:S(2)}, u32[]{:S(2)}) collective-permute-start(bf16[2,2048]{1,0:T(2,128)(2,1)S(1)} %slice.101), channel_id=1, source_target_pairs={{3,7},{7,11},{11,15},{15,19},{19,23},{23,27},{27,31}} | collective-permute-start | bytes 24584 | tf_op jit(solution)/shard_map/ppermute | solution.py:411
  27.3 12.2 %collective-permute-start.2 = (bf16[256,2048]{1,0:T(8,128)(2,1)}, bf16[256,2048]{1,0:T(8,128)(2,1)}, u32[]{:S(2)}, u32[]{:S(2)}) collective-permute-start(bf16[256,2048]{1,0:T(8,128)(2,1)} %collective-permute-done.1.refs_3_), channel_id=1, source_target_pairs={{0,1},{1,0},{2,3},{3,2},{4,5},{5,4},{6,7},{7,6},{8,9},{9,8},{10,11... | collective-permute-start | bytes 3145736 | tf_op jit(solution)/shard_map/ppermute | solution.py:288
  32.5 25.6 %collective-permute-start.11 = (bf16[256,2048]{1,0:T(8,128)(2,1)S(1)}, bf16[256,2048]{1,0:T(8,128)(2,1)S(1)}, u32[]{:S(2)}, u32[]{:S(2)}) collective-permute-start(bf16[256,2048]{1,0:T(8,128)(2,1)S(1)} %copy-done.2), channel_id=1, source_target_pairs={{0,2},{1,3},{2,0},{3,1},{4,6},{5,7},{6,4},{7,5},{8,10},{9,11},{10,... | collective-permute-start | bytes 3145736 | tf_op jit(solution)/shard_map/ppermute | solution.py:288
  34.1 33.7 %collective-permute-start.10 = (bf16[256,2048]{1,0:T(8,128)(2,1)S(1)}, bf16[256,2048]{1,0:T(8,128)(2,1)S(1)}, u32[]{:S(2)}, u32[]{:S(2)}) collective-permute-start(bf16[256,2048]{1,0:T(8,128)(2,1)S(1)} %copy-done.2), channel_id=1, source_target_pairs={{0,1},{1,0},{2,3},{3,2},{4,5},{5,4},{6,7},{7,6},{8,9},{9,8},{10,11... | collective-permute-start | bytes 3145736 | tf_op jit(solution)/shard_map/ppermute | solution.py:288
  47.6 10.5 %collective-permute-start.7 = (bf16[4,160,128]{2,1,0:T(8,128)(2,1)S(1)}, bf16[4,160,128]{2,1,0:T(8,128)(2,1)S(1)}, u32[]{:S(2)}, u32[]{:S(2)}) collective-permute-start(bf16[4,160,128]{2,1,0:T(8,128)(2,1)S(1)} %get-tuple-element.29), channel_id=1, source_target_pairs={{0,4},{4,0},{8,12},{12,8},{16,20},{20,16},{24,28},{28,24},{1,5},{5... | collective-permute-start | bytes 491528 | tf_op jit(solution)/shard_map/ppermute | solution.py:288
  50.0 70.9 %collective-permute-start.18 = (bf16[16,64]{1,0:T(8,128)(2,1)S(1)}, bf16[16,64]{1,0:T(8,128)(2,1)S(1)}, u32[]{:S(2)}, u32[]{:S(2)}) collective-permute-start(bf16[16,64]{1,0:T(8,128)(2,1)S(1)} %slice.108), channel_id=1, source_target_pairs={{4,0},{8,4},{12,8},{16,12},{20,16},{24,20},{28,24},{5,1},{9,5},{13... | collective-permute-start | bytes 6152 | tf_op jit(solution)/shard_map/ppermute | solution.py:501
  58.1 17.4 %collective-permute-start.12 = (bf16[256,2048]{1,0:T(8,128)(2,1)S(1)}, bf16[256,2048]{1,0:T(8,128)(2,1)S(1)}, u32[]{:S(2)}, u32[]{:S(2)}) collective-permute-start(bf16[256,2048]{1,0:T(8,128)(2,1)S(1)} %collective-permute-done.11.refs_7_), channel_id=1, source_target_pairs={{0,1},{1,0},{2,3},{3,2},{4,5},{5,4},{6,7},{7,6},{8,9},{9,8},{10,11... | collective-permute-start | bytes 3145736 | tf_op jit(solution)/shard_map/ppermute | solution.py:288
  58.1 6.8 %collective-permute-start.8 = (bf16[4,160,128]{2,1,0:T(8,128)(2,1)S(1)}, bf16[4,160,128]{2,1,0:T(8,128)(2,1)S(1)}, u32[]{:S(2)}, u32[]{:S(2)}) collective-permute-start(bf16[4,160,128]{2,1,0:T(8,128)(2,1)S(1)} %fusion.32), channel_id=1, source_target_pairs={{0,8},{4,12},{8,0},{12,4},{16,24},{20,28},{24,16},{28,20},{1,9},{5... | collective-permute-start | bytes 491528 | tf_op jit(solution)/shard_map/ppermute | solution.py:288
  65.0 10.4 %collective-permute-start.9 = (bf16[4,160,128]{2,1,0:T(8,128)(2,1)S(1)}, bf16[4,160,128]{2,1,0:T(8,128)(2,1)S(1)}, u32[]{:S(2)}, u32[]{:S(2)}) collective-permute-start(bf16[4,160,128]{2,1,0:T(8,128)(2,1)S(1)} %fusion.26), channel_id=1, source_target_pairs={{0,16},{4,20},{8,24},{12,28},{16,0},{20,4},{24,8},{28,12},{1,17},{... | collective-permute-start | bytes 491528 | tf_op jit(solution)/shard_map/ppermute | solution.py:288
  98.0 5.6 %collective-permute-start.15 = (bf16[4,160,128]{2,1,0:T(8,128)(2,1)S(1)}, bf16[4,160,128]{2,1,0:T(8,128)(2,1)S(1)}, u32[]{:S(2)}, u32[]{:S(2)}) collective-permute-start(bf16[4,160,128]{2,1,0:T(8,128)(2,1)S(1)} %get-tuple-element.37), channel_id=1, source_target_pairs={{0,4},{4,0},{8,12},{12,8},{16,20},{20,16},{24,28},{28,24},{1,5},{5... | collective-permute-start | bytes 491528 | tf_op jit(solution)/shard_map/ppermute | solution.py:288
  99.5 21.4 %collective-permute-start.19 = (f32[8,512]{1,0:T(8,128)S(1)}, f32[8,512]{1,0:T(8,128)S(1)}, u32[]{:S(2)}, u32[]{:S(2)}) collective-permute-start(f32[8,512]{1,0:T(8,128)S(1)} %get-tuple-element.38), channel_id=1, source_target_pairs={{4,0},{8,4},{12,8},{16,12},{20,16},{24,20},{28,24},{5,1},{9,5},{13... | collective-permute-start | bytes 49160 | tf_op jit(solution)/shard_map/ppermute | solution.py:500
  103.6 7.4 %collective-permute-start.16 = (bf16[4,160,128]{2,1,0:T(8,128)(2,1)S(1)}, bf16[4,160,128]{2,1,0:T(8,128)(2,1)S(1)}, u32[]{:S(2)}, u32[]{:S(2)}) collective-permute-start(bf16[4,160,128]{2,1,0:T(8,128)(2,1)S(1)} %fusion.33), channel_id=1, source_target_pairs={{0,8},{4,12},{8,0},{12,4},{16,24},{20,28},{24,16},{28,20},{1,9},{5... | collective-permute-start | bytes 491528 | tf_op jit(solution)/shard_map/ppermute | solution.py:288
  111.0 9.8 %collective-permute-start.17 = (bf16[4,160,128]{2,1,0:T(8,128)(2,1)S(1)}, bf16[4,160,128]{2,1,0:T(8,128)(2,1)S(1)}, u32[]{:S(2)}, u32[]{:S(2)}) collective-permute-start(bf16[4,160,128]{2,1,0:T(8,128)(2,1)S(1)} %fusion.30), channel_id=1, source_target_pairs={{0,16},{4,20},{8,24},{12,28},{16,0},{20,4},{24,8},{28,12},{1,17},{... | collective-permute-start | bytes 491528 | tf_op jit(solution)/shard_map/ppermute | solution.py:288
  116.7 33.9 %collective-permute-start.25 = (bf16[4,512,256]{2,1,0:T(8,128)(2,1)}, bf16[4,512,256]{2,1,0:T(8,128)(2,1)S(1)}, u32[]{:S(2)}, u32[]{:S(2)}) collective-permute-start(bf16[4,512,256]{2,1,0:T(8,128)(2,1)} %slice_bitcast_fusion.2), channel_id=1, source_target_pairs={{0,4},{4,0},{8,12},{12,8},{16,20},{20,16},{24,28},{28,24},{1,5},{5... | collective-permute-start | bytes 3145736 | tf_op jit(solution)/shard_map/ppermute | solution.py:288
  127.5 13.4 %collective-permute-start.28 = (f32[8,512]{1,0:T(8,128)S(1)}, f32[8,512]{1,0:T(8,128)S(1)}, u32[]{:S(2)}, u32[]{:S(2)}) collective-permute-start(f32[8,512]{1,0:T(8,128)S(1)} %get-tuple-element.41), channel_id=1, source_target_pairs={{0,4},{4,0},{8,12},{12,8},{16,20},{20,16},{24,28},{28,24},{1,5},{5... | collective-permute-start | bytes 49160 | tf_op jit(solution)/shard_map/ppermute | solution.py:288
  140.4 30.5 %collective-permute-start.22 = (bf16[4,256,640]{2,1,0:T(8,128)(2,1)S(1)}, bf16[4,256,640]{2,1,0:T(8,128)(2,1)S(1)}, u32[]{:S(2)}, u32[]{:S(2)}) collective-permute-start(bf16[4,256,640]{2,1,0:T(8,128)(2,1)S(1)} %slice_bitcast_fusion), channel_id=1, source_target_pairs={{0,4},{4,0},{8,12},{12,8},{16,20},{20,16},{24,28},{28,24},{1,5},{5... | collective-permute-start | bytes 3932168 | tf_op jit(solution)/shard_map/ppermute | solution.py:288
  141.0 3.8 %collective-permute-start.29 = (f32[8,512]{1,0:T(8,128)S(1)}, f32[8,512]{1,0:T(8,128)S(1)}, u32[]{:S(2)}, u32[]{:S(2)}) collective-permute-start(f32[8,512]{1,0:T(8,128)S(1)} %add.103), channel_id=1, source_target_pairs={{0,8},{4,12},{8,0},{12,4},{16,24},{20,28},{24,16},{28,20},{1,9},{5... | collective-permute-start | bytes 49160 | tf_op jit(solution)/shard_map/ppermute | solution.py:288
  142.4 31.1 %collective-permute-start.13 = (bf16[512,2048]{1,0:T(8,128)(2,1)S(1)}, bf16[512,2048]{1,0:T(8,128)(2,1)S(1)}, u32[]{:S(2)}, u32[]{:S(2)}) collective-permute-start(bf16[512,2048]{1,0:T(8,128)(2,1)S(1)} %convolution_convert_fusion), channel_id=1, source_target_pairs={{0,1},{1,0},{2,3},{3,2},{4,5},{5,4},{6,7},{7,6},{8,9},{9,8},{10,11... | collective-permute-start | bytes 6291464 | tf_op jit(solution)/shard_map/ppermute | solution.py:288
  144.8 4.6 %collective-permute-start.30 = (f32[8,512]{1,0:T(8,128)S(1)}, f32[8,512]{1,0:T(8,128)S(1)}, u32[]{:S(2)}, u32[]{:S(2)}) collective-permute-start(f32[8,512]{1,0:T(8,128)S(1)} %add.104), channel_id=1, source_target_pairs={{0,16},{4,20},{8,24},{12,28},{16,0},{20,4},{24,8},{28,12},{1,17},{... | collective-permute-start | bytes 49160 | tf_op jit(solution)/shard_map/ppermute | solution.py:288
  147.8 44.9 %collective-permute-start.20 = (bf16[512,2048]{1,0:T(8,128)(2,1)S(1)}, bf16[512,2048]{1,0:T(8,128)(2,1)S(1)}, u32[]{:S(2)}, u32[]{:S(2)}) collective-permute-start(bf16[512,2048]{1,0:T(8,128)(2,1)S(1)} %convolution_convert_fusion.1), channel_id=1, source_target_pairs={{0,1},{1,0},{2,3},{3,2},{4,5},{5,4},{6,7},{7,6},{8,9},{9,8},{10,11... | collective-permute-start | bytes 6291464 | tf_op jit(solution)/shard_map/ppermute | solution.py:288
  151.0 20.4 %collective-permute-start.26 = (bf16[2,512,256]{2,1,0:T(8,128)(2,1)S(1)}, bf16[2,512,256]{2,1,0:T(8,128)(2,1)S(1)}, u32[]{:S(2)}, u32[]{:S(2)}) collective-permute-start(bf16[2,512,256]{2,1,0:T(8,128)(2,1)S(1)} %slice_bitcast_fusion.6), channel_id=1, source_target_pairs={{0,8},{4,12},{8,0},{12,4},{16,24},{20,28},{24,16},{28,20},{1,9},{5... | collective-permute-start | bytes 1572872 | tf_op jit(solution)/shard_map/ppermute | solution.py:288
  171.3 21.1 %collective-permute-start.23 = (bf16[2,256,640]{2,1,0:T(8,128)(2,1)S(1)}, bf16[2,256,640]{2,1,0:T(8,128)(2,1)S(1)}, u32[]{:S(2)}, u32[]{:S(2)}) collective-permute-start(bf16[2,256,640]{2,1,0:T(8,128)(2,1)S(1)} %slice_bitcast_fusion.4), channel_id=1, source_target_pairs={{0,8},{4,12},{8,0},{12,4},{16,24},{20,28},{24,16},{28,20},{1,9},{5... | collective-permute-start | bytes 1966088 | tf_op jit(solution)/shard_map/ppermute | solution.py:288
  171.5 25.9 %collective-permute-start.27 = (bf16[1,512,256]{2,1,0:T(8,128)(2,1)S(1)}, bf16[1,512,256]{2,1,0:T(8,128)(2,1)S(1)}, u32[]{:S(2)}, u32[]{:S(2)}) collective-permute-start(bf16[1,512,256]{2,1,0:T(8,128)(2,1)S(1)} %slice_bitcast_fusion.14), channel_id=1, source_target_pairs={{0,16},{4,20},{8,24},{12,28},{16,0},{20,4},{24,8},{28,12},{1,17},{... | collective-permute-start | bytes 786440 | tf_op jit(solution)/shard_map/ppermute | solution.py:288
  175.3 35.1 %collective-permute-start.14 = (bf16[256,2048]{1,0:T(8,128)(2,1)}, bf16[256,2048]{1,0:T(8,128)(2,1)}, u32[]{:S(2)}, u32[]{:S(2)}) collective-permute-start(bf16[256,2048]{1,0:T(8,128)(2,1)} %add_convert_fusion.2), channel_id=1, source_target_pairs={{0,2},{1,3},{2,0},{3,1},{4,6},{5,7},{6,4},{7,5},{8,10},{9,11},{10,... | collective-permute-start | bytes 3145736 | tf_op jit(solution)/shard_map/ppermute | solution.py:288
  192.6 15.4 %collective-permute-start.24 = (bf16[1,256,640]{2,1,0:T(8,128)(2,1)S(1)}, bf16[1,256,640]{2,1,0:T(8,128)(2,1)S(1)}, u32[]{:S(2)}, u32[]{:S(2)}) collective-permute-start(bf16[1,256,640]{2,1,0:T(8,128)(2,1)S(1)} %slice_bitcast_fusion.8), channel_id=1, source_target_pairs={{0,16},{4,20},{8,24},{12,28},{16,0},{20,4},{24,8},{28,12},{1,17},{... | collective-permute-start | bytes 983048 | tf_op jit(solution)/shard_map/ppermute | solution.py:288
  196.0 24.3 %collective-permute-start.21 = (bf16[256,2048]{1,0:T(8,128)(2,1)}, bf16[256,2048]{1,0:T(8,128)(2,1)}, u32[]{:S(2)}, u32[]{:S(2)}) collective-permute-start(bf16[256,2048]{1,0:T(8,128)(2,1)} %fusion.1), channel_id=1, source_target_pairs={{0,2},{1,3},{2,0},{3,1},{4,6},{5,7},{6,4},{7,5},{8,10},{9,11},{10,... | collective-permute-start | bytes 3145736 | tf_op jit(solution)/shard_map/ppermute | solution.py:288
  (26 other events, 171.1 us)
where the time goes:
time: 225 us; the launch traced here: 224 us
  waiting for transfers between devices  95.1 us (42%)
  Pallas kernels  47.1 us (21%)
  starting transfers between devices  34 us (15%)
  matrix products  30.7 us (14%)
  local copies, waits for them, and re-layouts  12.3 us (5%)
  other arithmetic  3.36 us (1%)
    ppermute x25, waiting for transfers between devices, flip(): return lax.ppermute(x, axis, [(i, i ^ mask) for i in range(n)])  95.1 us
    pallas_call x5, Pallas kernels, call(): pl.pallas_call(kernel, out_shape=out_shapes, grid_spec=pltpu.PrefetchScal...  47.1 us
    ppermute x25, starting transfers between devices, flip(): return lax.ppermute(x, axis, [(i, i ^ mask) for i in range(n)])  28.3 us
    dot_general x8, matrix products, mm(): return jnp.dot(a, b, preferred_element_type=f32)  18.8 us
    dot_general x7, matrix products, mm_nt(): return lax.dot_general(a, b, CONTRACT_COLS, preferred_element_type=f32)  11.9 us
  transfers between devices with their start and end apart: 31, of which 12 were waited for; matrix products, arithmetic and copies ran while one was open for 19% of the time, Pallas kernels for 21%

commit v1 on v0

v1 whole, which is shorter than its diff:
```python
import functools

import jax
import jax.numpy as jnp
import numpy as np
from jax import lax
from jax.experimental import pallas as pl
from jax.experimental.pallas import tpu as pltpu
from jax.sharding import PartitionSpec as P

VD = 128
FK = 16
FEATS = 153
STATE_ROWS = 160
LANES = 256
EPS = 1e-6

bf16 = jnp.bfloat16
f32 = jnp.float32
CONTRACT_COLS = (((1,), (1,)), ((), ()))
CONTRACT_ROWS = (((0,), (0,)), ((), ()))


def mm(a, b):
    return jnp.dot(a, b, preferred_element_type=f32)


def mm_nt(a, b):
    return lax.dot_general(a, b, CONTRACT_COLS, preferred_element_type=f32)


def mm_tn(a, b):
    return lax.dot_general(a, b, CONTRACT_ROWS, preferred_element_type=f32)


def feature_tables(heads):
    e1 = np.zeros((FK, LANES), np.float32)
    e2 = np.zeros((FK, LANES), np.float32)
    weight = np.zeros((LANES,), np.float32)
    bias = np.zeros((8, LANES), np.float32)
    bias[0, 0] = bias[1, 0] = weight[0] = 1.0
    for i in range(FK):
        e1[i, 1 + i] = 1.0
        bias[1, 1 + i] = 1.0
        weight[1 + i] = FK ** -0.5
    column = 1 + FK
    for i in range(FK):
        for j in range(i, FK):
            e1[i, column] = 1.0
            e2[j, column] = 1.0
            weight[column] = 1.0 / FK if i < j else 0.5 / FK
            column += 1
    def spread(table):
        out = np.zeros((heads, FK, heads, LANES), np.float32)
        for h in range(heads):
            out[h, :, h] = table
        return jnp.asarray(out.reshape(heads * FK, heads * LANES), bf16)
    return spread(e1), spread(e1 * weight), spread(e2), jnp.asarray(bias)


def features_t(rows, e1_ref, e2_ref, bias_ref, head):
    at = slice(head * LANES, (head + 1) * LANES)
    first = mm_nt(e1_ref[at, :], rows) + bias_ref[:, 0:1]
    second = mm_nt(e2_ref[at, :], rows) + bias_ref[:, 1:2]
    return (first * second).astype(bf16)


def features(rows, e1_ref, e2_ref, bias_ref, head):
    cols = slice(head * LANES, (head + 1) * LANES)
    first = mm(rows, e1_ref[:, cols]) + bias_ref[0:1, :]
    second = mm(rows, e2_ref[:, cols]) + bias_ref[1:2, :]
    return first, second


def features_pull(grad, first, second, e1_ref, e2_ref, head):
    cols = slice(head * LANES, (head + 1) * LANES)
    return mm_nt((grad * second).astype(bf16), e1_ref[:, cols]) + mm_nt(
        (grad * first).astype(bf16), e2_ref[:, cols]
    )


def head_only(rows, head, scale):
    lane = lax.broadcasted_iota(jnp.int32, rows.shape, 1)
    keep = (lane >= head * FK) & (lane < (head + 1) * FK)
    return jnp.where(keep, rows.astype(f32) * scale, 0.0).astype(bf16)


def full_state(state):
    return jnp.concatenate(
        [state.astype(bf16), jnp.zeros((LANES - STATE_ROWS, VD), bf16)], axis=0
    )


def conv_kernel(heads, group, parts, *refs):
    place_ref = refs[0]
    pieces = refs[1 : 1 + parts]
    halo_ref, taps_ref, e1_ref, e2_ref, bias_ref = refs[1 + parts : 6 + parts]
    qk_ref, v_ref, mixed_ref, state_ref, total_ref = refs[6 + parts : 11 + parts]
    piece_scr, prev_scr, total_scr = refs[11 + parts :]
    chunk = pl.program_id(0)
    relative = chunk ^ place_ref[0]
    for j in range(parts):
        @pl.when(relative == j)
        def _(j=j):
            piece_scr[...] = pieces[j][...]

    first_lane, last_lane = group[0] * VD, (group[-1] + 1) * VD

    @pl.when(chunk == 0)
    def _():
        prev_scr[...] = halo_ref[:, first_lane:last_lane].astype(f32)
        total_scr[...] = jnp.zeros_like(total_scr)

    vw = heads * VD
    kw = heads * FK
    values = piece_scr[:, first_lane:last_lane]
    qk = piece_scr[:, vw : vw + 2 * kw]
    k = qk[:, kw:]
    qk_ref[...] = qk
    v_ref[...] = values
    wide = values.astype(f32)
    rows = wide.shape[0]
    at = lax.broadcasted_iota(jnp.int32, wide.shape, 0)
    before1 = prev_scr[7:8, :]
    before2 = prev_scr[6:7, :]
    lag1 = jnp.where(at == 0, before1, pltpu.roll(wide, 1, 0))
    lag2 = jnp.where(at == 0, before2, jnp.where(at == 1, before1, pltpu.roll(wide, 2, 0)))
    prev_scr[...] = wide[rows - 8 :, :]
    taps = taps_ref[:, first_lane:last_lane]
    mixed = (taps[0:1, :] * wide + taps[1:2, :] * lag1 + taps[2:3, :] * lag2).astype(bf16)
    mixed_ref[...] = mixed
    for i, h in enumerate(group):
        phi_t = features_t(k, e1_ref, e2_ref, bias_ref, h)
        state = mm(phi_t, mixed[:, i * VD : (i + 1) * VD])[:STATE_ROWS]
        state_ref[0, i] = state.astype(bf16)
        total_scr[i] += state

    @pl.when(chunk == pl.num_programs(0) - 1)
    def _():
        total_ref[...] = total_scr[...].astype(bf16)


def pre_kernel(heads, *refs):
    (
        _, qk_ref, mixed_ref, state_ref, e1_ref, e2_ref, bias_ref, e1t_ref, e2t_ref, biast_ref,
        local_ref, phi_ref, turned_ref, weight_ref, slope_ref, prefix_ref,
        run_scr,
    ) = refs

    @pl.when(pl.program_id(0) == 0)
    def _():
        run_scr[...] = jnp.zeros_like(run_scr)

    kw = heads * FK
    q = qk_ref[:, :kw]
    k = qk_ref[:, kw:]
    rows = q.shape[0]
    row = lax.broadcasted_iota(jnp.int32, (rows, rows), 0)
    col = lax.broadcasted_iota(jnp.int32, (rows, rows), 1)
    causal = row >= col
    for h in range(heads):
        lanes = slice(h * VD, (h + 1) * VD)
        first, second = features(q, e1_ref, e2_ref, bias_ref, h)
        phi = (first * second).astype(bf16)
        phi_ref[:, h * LANES : (h + 1) * LANES] = phi
        turned_ref[h] = features_t(q, e1t_ref, e2t_ref, biast_ref, h)
        u = mm_nt(q, head_only(k, h, FK ** -0.5))
        slope = 1.0 + u
        weight = jnp.where(causal, slope + 0.5 * u * u, 0.0).astype(bf16)
        weight_ref[h] = weight
        slope_ref[h] = jnp.where(causal, slope, 0.0).astype(bf16)
        prefix = run_scr[h].astype(bf16)
        prefix_ref[0, h] = prefix
        local = mm(weight, mixed_ref[:, lanes]) + mm(phi, full_state(prefix))
        local_ref[:, lanes] = local.astype(bf16)
        run_scr[h] += state_ref[0, h].astype(f32)


def mid_kernel(heads, parts, *refs):
    (
        place_ref, local_ref, phi_ref, turned_ref, carried_ref, ga_ref, gain_ref,
        qk_ref, weight_ref, e1k_ref, e2_ref, bias_ref,
        even_ref, odd_ref, ds_ref, gstate_ref, gtotal_ref, gain_sum_ref, halo_ref,
        gtotal_scr, attn_scr,
    ) = refs
    chunk = pl.program_id(0)
    relative = chunk ^ place_ref[0]

    @pl.when(chunk == 0)
    def _():
        gtotal_scr[...] = jnp.zeros_like(gtotal_scr)
        gain_sum_ref[...] = jnp.zeros_like(gain_sum_ref)

    for h in range(heads):
        lanes = slice(h * VD, (h + 1) * VD)
        phi = phi_ref[:, h * LANES : (h + 1) * LANES]
        summed = local_ref[:, lanes].astype(f32) + mm(phi, full_state(carried_ref[h]))
        scale = lax.rsqrt(jnp.mean(summed * summed, axis=-1, keepdims=True) + EPS)
        unit = summed * scale
        gain = gain_ref[0:1, lanes]
        attn_scr[:, lanes] = (unit * gain).astype(bf16)
        ga = ga_ref[0, :, lanes].astype(f32)
        gu = ga * unit
        gain_sum_ref[0:1, lanes] += jnp.sum(gu, axis=0, keepdims=True)
        ds = scale * (ga * gain - unit * jnp.mean(gu * gain, axis=-1, keepdims=True))
        ds = ds.astype(bf16)
        ds_ref[:, lanes] = ds
        gstate = mm(turned_ref[h], ds)[:STATE_ROWS]
        gstate_ref[0, h] = gstate.astype(bf16)
        gtotal_scr[h] += gstate

    @pl.when(chunk == 0)
    def _():
        kw = heads * FK
        vw = heads * VD
        qk = qk_ref[...]
        for h in range(heads):
            lanes = slice(h * VD, (h + 1) * VD)
            kfirst, ksecond = features(qk[:, kw:], e1k_ref, e2_ref, bias_ref, h)
            kphi = (kfirst * ksecond).astype(bf16)
            own = mm(kphi, full_state(gstate_ref[0, h]))
            top = mm_tn(weight_ref[h], ds_ref[:, lanes])
            halo_ref[:, lanes] = top[0:8] - own[0:8]
        halo_ref[:, vw:] = qk[0:8, :].astype(f32)

    @pl.when(relative % 2 == 0)
    def _():
        even_ref[relative // 2] = attn_scr[...]

    @pl.when(relative % 2 == 1)
    def _():
        odd_ref[relative // 2] = attn_scr[...]

    @pl.when(chunk == pl.num_programs(0) - 1)
    def _():
        gtotal_ref[...] = gtotal_scr[...].astype(bf16)


def post_kernel(heads, *refs):
    (
        _, qk_ref, mixed_ref, ds_ref, weight_ref, slope_ref, prefix_ref, carried_ref,
        e1q_ref, e2_ref, bias_ref,
        dqk_ref, dv_ref,
    ) = refs
    kw = heads * FK
    qk = qk_ref[...]
    q = qk[:, :kw]
    k = qk[:, kw:]
    dq = jnp.zeros(q.shape, f32)
    dk = jnp.zeros(q.shape, f32)
    for h in range(heads):
        lanes = slice(h * VD, (h + 1) * VD)
        ds = ds_ref[:, lanes]
        dw = mm_nt(ds, mixed_ref[:, lanes]).astype(bf16).astype(f32)
        du = (dw * slope_ref[h].astype(f32)).astype(bf16)
        dq += mm(du, head_only(k, h, FK ** -0.5))
        dk += mm_tn(du, head_only(q, h, FK ** -0.5))
        dv_ref[:, lanes] = mm_tn(weight_ref[h], ds).astype(bf16)
        state = full_state(prefix_ref[0, h].astype(f32) + carried_ref[h].astype(f32))
        first, second = features(q, e1q_ref, e2_ref, bias_ref, h)
        dq += features_pull(mm_nt(ds, state), first, second, e1q_ref, e2_ref, h)
    dqk_ref[:, :kw] = dq
    dqk_ref[:, kw:] = dk


def finish_kernel(heads, cut, parts, *refs):
    (
        place_ref, dqk_ref, qk_ref, v_ref, mixed_ref, dv_ref, gstate_ref, gin_ref,
        taps_ref, halo_ref, gain_ref, e1_ref, e2_ref, bias_ref,
        early_ref, late_ref, even_ref, odd_ref, sums_ref,
        run_scr, next_scr, mixed_scr, cols_scr,
    ) = refs
    step = pl.program_id(0)
    chunk = pl.num_programs(0) - 1 - step
    relative = chunk ^ place_ref[0]
    kw = heads * FK
    vw = heads * VD

    @pl.when(step == 0)
    def _():
        run_scr[...] = gin_ref[...].astype(f32)
        sums_ref[...] = jnp.zeros_like(sums_ref)
        sums_ref[3:4, :] = gain_ref[0:1, :]
        hk = jnp.concatenate([halo_ref[:, vw + kw :]] * 2, axis=0).astype(bf16)
        for h in range(heads):
            lanes = slice(h * VD, (h + 1) * VD)
            first, second = features(hk, e1_ref, e2_ref, bias_ref, h)
            phi = (first * second).astype(bf16)
            next_scr[:, lanes] = halo_ref[:, lanes] + mm(phi, full_state(gin_ref[h]))[0:8]

    k = qk_ref[:, kw:]
    dk = dqk_ref[:, kw:]
    for h in range(heads):
        lanes = slice(h * VD, (h + 1) * VD)
        first, second = features(k, e1_ref, e2_ref, bias_ref, h)
        phi = (first * second).astype(bf16)
        state = full_state(run_scr[h])
        mixed_scr[:, lanes] = dv_ref[:, lanes].astype(f32) + mm(phi, state)
        dphi = mm_nt(mixed_ref[:, lanes], state)
        dk += features_pull(dphi, first, second, e1_ref, e2_ref, h)
        run_scr[h] += gstate_ref[0, h].astype(f32)
    gm = mixed_scr[...]
    rows = gm.shape[0]
    at = lax.broadcasted_iota(jnp.int32, gm.shape, 0)
    after0 = next_scr[0:1, :]
    after1 = next_scr[1:2, :]
    lead1 = jnp.where(at == rows - 1, after0, pltpu.roll(gm, rows - 1, 0))
    lead2 = jnp.where(
        at == rows - 1, after1, jnp.where(at == rows - 2, after0, pltpu.roll(gm, rows - 2, 0))
    )
    next_scr[...] = gm[0:8, :]
    gv = taps_ref[0:1, :] * gm + taps_ref[1:2, :] * lead1 + taps_ref[2:3, :] * lead2
    values = v_ref[...].astype(f32)
    sums_ref[0:1, :] += jnp.sum(gm * values, axis=0, keepdims=True)
    sums_ref[1:2, :] += jnp.sum(lead1 * values, axis=0, keepdims=True)
    sums_ref[2:3, :] += jnp.sum(lead2 * values, axis=0, keepdims=True)
    cols_scr[:, :vw] = gv.astype(bf16)
    cols_scr[:, vw : vw + kw] = dqk_ref[:, :kw].astype(bf16)
    cols_scr[:, vw + kw :] = dk.astype(bf16)
    at_piece = relative // 2 + (relative % 2) * (parts // 2)
    early_ref[at_piece] = cols_scr[:, :cut]
    late_ref[at_piece] = cols_scr[:, cut:]

    @pl.when(relative % 2 == 0)
    def _():
        even_ref[relative // 2] = cols_scr[...]

    @pl.when(relative % 2 == 1)
    def _():
        odd_ref[relative // 2] = cols_scr[...]


def whole(shape):
    return pl.BlockSpec(shape, lambda *a, n=len(shape): (0,) * n)


def call(kernel, place, inputs, in_specs, out_shapes, out_specs, scratch, steps, flops, alias=None):
    return pl.pallas_call(
        kernel,
        out_shape=out_shapes,
        grid_spec=pltpu.PrefetchScalarGridSpec(
            num_scalar_prefetch=1,
            grid=(steps,),
            in_specs=in_specs,
            out_specs=out_specs,
            scratch_shapes=scratch,
        ),
        input_output_aliases=alias or {},
        compiler_params=pltpu.CompilerParams(
            dimension_semantics=("arbitrary",), vmem_limit_bytes=16 << 20
        ),
        cost_estimate=pl.CostEstimate(flops=0, bytes_accessed=0, transcendentals=0),
    )(place, *inputs)


def in_hbm(x):
    return pltpu.with_memory_space_constraint(x, pltpu.HBM)


def flip(x, axis, mask):
    n = lax.axis_size(axis)
    return lax.ppermute(x, axis, [(i, i ^ mask) for i in range(n)])


def held(x, *others):
    return lax.optimization_barrier((x,) + others)[0]


def scan_send(total, mask):
    return flip(total.astype(bf16), "seq", mask) if mask < lax.axis_size("seq") else None


def scan_take(before, total, got, mask, reverse):
    got = got.astype(f32)
    upper = (lax.axis_index("seq") & mask) != 0
    return before + jnp.where(upper != reverse, got, 0.0), total.astype(f32) + got


def arrange_kernel(parts, *refs):
    pieces = refs[1 : 1 + parts]
    kept_ref, sent_ref = refs[1 + parts :]
    rows = pieces[0].shape[0]
    step = pl.program_id(0)
    half = pl.num_programs(0) // 2
    for target, on in ((kept_ref, step < half), (sent_ref, step >= half)):
        @pl.when(on)
        def _(target=target):
            for j in range(parts):
                target[j * rows : (j + 1) * rows, :] = pieces[j][...]


def arranged(pieces, masks):
    n, place = lax.axis_size("seq"), lax.axis_index("seq")
    order = [0]
    for mask in masks[::-1]:
        order = order + [j | mask for j in order]
    order = jnp.asarray(np.array(order, np.int32)) ^ place.astype(jnp.int32)
    parts = len(pieces)
    rows, depth = pieces[0].shape
    length, width, half = parts * rows, depth // n, depth // 2
    if width % 128:
        full = jnp.concatenate(pieces, axis=0).reshape(length, n, width)
        full = jnp.take(full, order, axis=1).reshape(length, depth)
        return full[:, :half], full[:, half:]
    out = pltpu.HBM((length, half), bf16)
    mid = n // 2
    return call(
        functools.partial(arrange_kernel, parts),
        order,
        list(pieces),
        [pl.BlockSpec((rows, width), lambda i, o: (0, o[i]))] * parts,
        [out, out],
        [
            pl.BlockSpec((length, width), lambda i, o: (0, jnp.minimum(i, mid - 1))),
            pl.BlockSpec((length, width), lambda i, o: (0, jnp.maximum(i - mid, 0))),
        ],
        [], n, 0,
    )


class Halve:
    def __init__(self, turn, left, right, scale, extra=None):
        n = lax.axis_size("seq")
        self.masks = [1 << b for b in range(n.bit_length() - 1)]
        self.turn = turn and n > 2
        if self.turn:
            self.masks = self.masks[1:] + self.masks[:1]
        self.left, self.right, self.scale, self.extra = left, right, scale, extra

    def product(self, side, *others):
        left = held(self.left, *others) if others else self.left
        n = lax.axis_size("seq")
        width = 2 * self.right[0].shape[1] // n
        if self.turn:
            half = self.right[0].shape[1] // 2
            pair = [
                (mm_tn(left, right[:, side * half : (side + 1) * half]) * self.scale).astype(bf16)
                for right in self.right
            ]
            out = jnp.concatenate(
                [p[:, i * width : (i + 1) * width] for i in range(n // 4) for p in pair], axis=1
            )
        else:
            out = (mm_tn(left, self.right[side]) * self.scale).astype(bf16)
        if self.extra is not None:
            tail = (self.extra[:4] * self.scale).astype(bf16).reshape(4, -1, width)
            tail = tail.transpose(1, 0, 2).reshape(-1, width)
            out = jnp.concatenate([out, jnp.tile(tail, (1, n // 2))], axis=0)
        return out

    def begin(self, *others):
        self.first = self.product(1, *others)
        self.got = flip(self.first, "seq", self.masks[0])
        self.at = 1

    def keep(self, *others):
        self.kept = [self.product(0, *others)]
        return self.kept[0]

    def step(self, *others):
        got = held(self.got, *others)
        self.kept.append(got)
        if self.at == len(self.masks):
            self.out = sum(t.astype(f32) for t in self.kept)
            return self.out
        half = got.shape[1] // 2
        send = sum(t[:, half:].astype(f32) for t in self.kept).astype(bf16)
        self.got = flip(send, "seq", self.masks[self.at])
        self.at += 1
        self.kept = [t[:, :half] for t in self.kept]
        return send


def masks_of(first):
    n = lax.axis_size("seq")
    masks = [1 << b for b in range(n.bit_length() - 1)]
    return masks[first:] + masks[:first]


def per_device(tokens_in, w_query, w_key, w_value, w_output, conv_taps, norm_gain, grad_out):
    nt, ns = lax.axis_size("tensor"), lax.axis_size("seq")
    rows, depth = tokens_in.shape
    length = rows * nt
    kw, vw = w_query.shape[1], w_value.shape[1]
    heads = vw // VD
    grad_scale = float(length * ns) ** -0.5
    place = lax.axis_index("tensor").reshape(1).astype(jnp.int32)
    e1q, e1k, e2, bias = feature_tables(heads)
    turned_q, turned_k, turned2 = e1q.T, e1k.T, e2.T
    turned_bias = jnp.pad(bias[:2].T, ((0, 0), (0, 126)))
    (
        e1q, e1k, e2, bias, turned_q, turned_k, turned2, turned_bias, conv_taps, norm_gain
    ) = (
        pltpu.with_memory_space_constraint(x, pltpu.HBM)
        for x in (
            e1q, e1k, e2, bias, turned_q, turned_k, turned2, turned_bias, conv_taps,
            norm_gain.reshape(1, -1),
        )
    )
    evens, odds = list(range(0, nt, 2)), list(range(1, nt, 2))

    far = {j: flip(tokens_in, "tensor", j) for j in evens[1:]}
    near = flip(tokens_in, "tensor", 1)
    near_cot = flip(grad_out, "tensor", 1)
    tail = held(tokens_in, near)[rows - 2 :]
    above = sum(
        lax.ppermute(
            tail, ("seq", "tensor"), [(s * nt + nt - 1, (s + 1) * nt + i) for s in range(ns - 1)]
        )
        for i in range(nt)
    )
    cw = vw + 2 * kw
    joined = [held(w, near) for w in (w_value, w_query, w_key)]
    weights = lax.optimization_barrier(jnp.concatenate(joined, axis=1))
    project = lambda piece: mm(piece, weights).astype(bf16)
    pull = lambda piece: mm_nt(piece, w_output).astype(bf16)
    halo = jnp.pad(mm(above, w_value).astype(bf16), ((6, 0), (0, 0)))
    tokens, cotangent = [tokens_in, near], [grad_out, near_cot]
    projected = [project(tokens_in), project(near)]
    pulled = [pull(grad_out), pull(near_cot)]
    for j in evens[1:]:
        piece = held(far[j], halo, *projected, *pulled)
        tokens += [piece, flip(piece, "tensor", 1)]
    projected += [project(piece) for piece in tokens[2:]]
    cot_from = held(grad_out, projected[2])
    far_cot = {j: flip(cot_from, "tensor", j) for j in evens[1:]}

    state_shape = (heads, STATE_ROWS, VD)
    at_chunk = lambda i, p: (i, 0)
    at_state = lambda i, p: (i, 0, 0, 0)
    on_chunk = lambda width: pl.BlockSpec((rows, width), at_chunk)
    state_spec = pl.BlockSpec((1,) + state_shape, at_state)
    square_spec = pl.BlockSpec((heads, rows, rows), lambda i, p: (0, i, 0))
    tables = [whole(e1q.shape), whole(e2.shape), whole(bias.shape)]
    turned_tables = [whole(turned_q.shape), whole(turned2.shape), whole(turned_bias.shape)]
    turned_spec = pl.BlockSpec((heads, LANES, rows), lambda i, p: (0, 0, i))
    shape = jax.ShapeDtypeStruct
    states_shape = shape((nt,) + state_shape, bf16)
    qk, values, mixed, states, total = call(
        functools.partial(conv_kernel, heads, list(range(heads)), nt),
        place,
        projected + [halo, conv_taps, turned_k, turned2, turned_bias],
        [whole((rows, cw))] * nt + [whole((8, vw)), whole((3, vw))] + turned_tables,
        [
            shape((length, 2 * kw), bf16),
            shape((length, vw), bf16),
            shape((length, vw), bf16),
            states_shape,
            shape(state_shape, bf16),
        ],
        [on_chunk(2 * kw), on_chunk(vw), on_chunk(vw), state_spec, whole(state_shape)],
        [pltpu.VMEM((rows, cw), bf16), pltpu.VMEM((8, vw), f32), pltpu.VMEM(state_shape, f32)],
        nt, 2 * length * vw * 256 * 3,
    )

    before = jnp.zeros(state_shape, f32)
    mask = 1
    got = scan_send(total, mask)
    pinned = lambda dims, kind: pltpu.HBM(dims, kind)
    local, phi, phi_t, weight, slope, prefix = call(
        functools.partial(pre_kernel, heads),
        place,
        [qk, mixed, states, e1q, e2, bias, turned_q, turned2, turned_bias],
        [on_chunk(2 * kw), on_chunk(vw), state_spec] + tables + turned_tables,
        [
            pinned((length, vw), bf16),
            pinned((length, heads * LANES), bf16),
            pinned((heads, LANES, length), bf16),
            pinned((heads, length, rows), bf16),
            pinned((heads, length, rows), bf16),
            states_shape,
        ],
        [
            on_chunk(vw), on_chunk(heads * LANES), turned_spec, square_spec, square_spec,
            state_spec,
        ],
        [pltpu.VMEM(state_shape, f32)],
        nt, 2 * length * vw * 256 * 5,
    )
    got = held(got, local)
    ordered = lambda pieces: [pieces[j] for j in evens + odds]
    tokens_for = None
    while got is not None:
        before, total = scan_take(before, total, got, mask, False)
        mask *= 2
        got = scan_send(total, mask)
        if tokens_for is None:
            ready = ordered(tokens)
            ready[0] = held(ready[0], total)
            tokens_for = arranged(ready, masks_of(0))
            got = held(got, *tokens_for) if got is not None else None
        if mask * 2 == ns:
            for j in evens[1:]:
                piece = held(far_cot[j], total)
                cotangent += [piece, flip(piece, "tensor", 1)]
            pulled += [pull(piece) for piece in cotangent[2:]]
            by_place = [pulled[j] for j in evens + odds]
            grad_attn = jnp.stack(by_place)
            got = held(got, grad_attn)
    carried = before.astype(bf16)

    half_shape = shape((nt // 2, rows, vw), bf16)
    slot = lambda j: (j >> 1) + (j & 1) * (nt // 2)
    attn_even, attn_odd, ds, gstates, gtotal, gain_sum, halo_out = call(
        functools.partial(mid_kernel, heads, nt),
        place,
        [
            local, phi, phi_t, carried, grad_attn, norm_gain, qk, weight, e1k, e2,
            bias,
        ],
        [
            on_chunk(vw),
            on_chunk(heads * LANES),
            turned_spec,
            whole(state_shape),
            pl.BlockSpec((1, rows, vw), lambda i, p: (slot(i ^ p[0]), 0, 0)),
            whole((1, vw)),
            whole((16, 2 * kw)),
            whole((heads, rows, 128)),
        ]
        + tables,
        [
            half_shape, half_shape, shape((length, vw), bf16), states_shape,
            shape(state_shape, bf16), shape((8, vw), f32), shape((8, vw + 2 * kw), f32),
        ],
        [
            whole(half_shape.shape), whole(half_shape.shape), on_chunk(vw), state_spec,
            whole(state_shape), whole((8, vw)), whole((8, vw + 2 * kw)),
        ],
        [pltpu.VMEM(state_shape, f32), pltpu.VMEM((rows, vw), bf16)],
        nt, 2 * length * vw * 256 * 2,
    )

    attn_all = jnp.concatenate([attn_even.reshape(-1, vw), attn_odd.reshape(-1, vw)], axis=0)
    ready = ordered(cotangent)
    ready[0] = held(ready[0], gtotal)
    cot_for = arranged(ready, masks_of(0))
    out_halve = Halve(False, attn_all, cot_for, grad_scale)
    after = jnp.zeros(state_shape, f32)
    got = scan_send(gtotal, 1)
    halo_in = lax.ppermute(halo_out, "seq", [(i + 1, i) for i in range(ns - 1)])
    out_odd = mm(attn_odd.reshape(-1, vw), w_output).astype(bf16)
    out_got = flip(out_odd, "tensor", 1)
    mask = 1
    while got is not None:
        cover = [out_odd, *cot_for] if mask == 1 else [kept] if mask == 2 else [dv]
        after, gtotal = scan_take(after, gtotal, held(got, *cover), mask, True)
        mask *= 2
        got = scan_send(gtotal, mask)
        if mask == 2:
            out_flips = []
            out_rows = mm(attn_even.reshape(-1, vw), w_output) + held(out_got, gtotal).astype(f32)
            out_rows = out_rows.astype(bf16)
            for i in range(1, nt // 2):
                out_flips.append(flip(out_rows[i * rows : (i + 1) * rows], "tensor", 2 * i))
            out_halve.begin(out_rows)
            kept = out_halve.keep(out_halve.first)
        if mask == 4 or (mask == 2 and ns == 2):
            dqk, dv = call(
                functools.partial(post_kernel, heads),
                place,
                [
                    held(qk, gtotal), in_hbm(mixed), ds, in_hbm(weight), in_hbm(slope),
                    in_hbm(prefix), carried, e1q, e2, bias,
                ],
                [
                    on_chunk(2 * kw), on_chunk(vw), on_chunk(vw), square_spec, square_spec,
                    state_spec, whole(state_shape),
                ]
                + tables,
                [shape((length, 2 * kw), f32), shape((length, vw), bf16)],
                [on_chunk(2 * kw), on_chunk(vw)],
                [],
                nt, 2 * length * vw * 256 * 8,
            )
    gin = after.astype(bf16)
    dqk = held(dqk, out_halve.step(gin))

    last = lambda i, p: (nt - 1 - i, 0)
    from_last = lambda width: pl.BlockSpec((rows, width), last)
    cut = cw * 6 // 10 // 128 * 128
    early, late, cols_even, cols_odd, sums = call(
        functools.partial(finish_kernel, heads, cut, nt),
        place,
        [dqk, qk, values, mixed, dv, gstates, gin, conv_taps, halo_in, gain_sum, e1k, e2, bias],
        [
            from_last(2 * kw), from_last(2 * kw), from_last(vw), from_last(vw), from_last(vw),
            pl.BlockSpec((1,) + state_shape, lambda i, p: (nt - 1 - i, 0, 0, 0)),
            whole(state_shape), whole((3, vw)), whole((8, vw + 2 * kw)), whole((8, vw)),
        ]
        + tables,
        [
            shape((nt, rows, cut), bf16), shape((nt, rows, cw - cut), bf16),
            shape((nt // 2, rows, cw), bf16), shape((nt // 2, rows, cw), bf16),
            shape((8, vw), f32),
        ],
        [
            whole((nt, rows, cut)), whole((nt, rows, cw - cut)),
            whole((nt // 2, rows, cw)), whole((nt // 2, rows, cw)), whole((8, vw)),
        ],
        [
            pltpu.VMEM(state_shape, f32), pltpu.VMEM((8, vw), f32),
            pltpu.VMEM((rows, vw), f32), pltpu.VMEM((rows, cw), bf16),
        ],
        nt, 2 * length * vw * 256 * 6,
    )
    first = Halve(False, early.reshape(length, cut), tokens_for, grad_scale)
    out_flips = [held(got, early) for got in out_flips]
    steps = len(out_halve.masks)
    first = Halve(False, early.reshape(length, cut), tokens_for, grad_scale)
    first.begin(*out_flips)
    second = Halve(True, late.reshape(length, cw - cut), tokens_for, grad_scale, sums)
    done = out_halve.step(first.first) if steps > 2 else first.first
    second.begin(done)
    in_odd = mm_nt(held(cols_odd, second.first).reshape(-1, cw), weights).astype(bf16)
    in_got = held(flip(in_odd, "tensor", 1), in_odd)
    in_rows = mm_nt(cols_even.reshape(-1, cw), weights) + in_got.astype(f32)
    in_rows = in_rows.astype(bf16)
    in_flips = []
    for i in range(1, nt // 2):
        in_flips.append(flip(in_rows[i * rows : (i + 1) * rows], "tensor", 2 * i))
    done = first.keep(in_rows)
    done = first.step(done)
    done = second.keep(done)
    done = second.step(done)
    layer_out = held(out_rows, done)[:rows].astype(f32)
    for got in out_flips:
        layer_out += got.astype(f32)
    done = layer_out = layer_out.astype(bf16)
    for k in range(1, steps):
        if k < steps - 1 or steps == 2:
            done = out_halve.step(done)
        done = first.step(done) if k < steps - 1 else done
        done = second.step(done)
        if k == steps - 2 or steps == 2:
            grad_in = in_rows[:rows].astype(f32)
            for got in in_flips:
                grad_in += held(got, done).astype(f32)
            done = grad_in = grad_in.astype(bf16)
    first.step(done)
    while not hasattr(out_halve, "out"):
        out_halve.step(done)
    grad_wo = out_halve.out.astype(bf16)
    low, high = first.out.astype(bf16), second.out[: cw - cut].astype(bf16)
    sums = second.out[cw - cut :]
    sums = jnp.concatenate(jnp.split(sums, sums.shape[0] // 4, axis=0), axis=1)
    more = vw - cut
    grad_wv = jnp.concatenate([low.T, high[:more].T], axis=1)
    grad_wq = high[more : more + kw].T
    grad_wk = high[more + kw :].T
    return (layer_out, grad_in, grad_wq, grad_wk, grad_wv, grad_wo, sums[0:3], sums[3])


def solution(mesh):
    return jax.shard_map(
        per_device,
        mesh=mesh,
        in_specs=(
            P(("seq", "tensor"), None),
            P(None, "tensor"),
            P(None, "tensor"),
            P(None, "tensor"),
            P("tensor", None),
            P(None, "tensor"),
            P("tensor"),
            P(("seq", "tensor"), None),
        ),
        out_specs=(
            P(("seq", "tensor"), None),
            P(("seq", "tensor"), None),
            P("seq", "tensor"),
            P("seq", "tensor"),
            P("seq", "tensor"),
            P("tensor", "seq"),
            P(None, "tensor"),
            P("tensor"),
        ),
        check_vma=False,
    )
```

time: 225 us -> 200 us (0.89)
  waiting for transfers between devices: 95.1 us -> 48.5 us
  other arithmetic: 3.36 us -> 20.2 us
  Pallas kernels: 47.1 us -> 53.3 us
  starting transfers between devices: 34 us -> 28.9 us
  matrix products: 30.7 us -> 33.8 us
    ppermute x25, waiting for transfers between devices: 95.1 us -> 48.5 us  [flip(): return lax.ppermute(x, axis, [(i, i ^ mask) for i in range(n)])]
    convert_element_type x8 -> x14, other arithmetic: 1.08 us -> 11.6 us  [the longest x6 3.65 us: step(): send = sum((t[:, half:].astype(f32) for t in self.kept)).astype(bf16)]
    dot_general x0 -> x8, matrix products: none -> 10.1 us  [mm_tn(): return lax.dot_general(a, b, CONTRACT_ROWS, preferred_element_type=f32)]
    dot_general x8 -> x7, matrix products: 18.8 us -> 11.8 us  [mm(): return jnp.dot(a, b, preferred_element_type=f32)]
    pallas_call x5 -> x7, Pallas kernels: 47.1 us -> 53.3 us  [call(): pl.pallas_call(kernel, out_shape=out_shapes, grid_spec=pltpu.PrefetchScal...]
    squeeze x8 -> x0, local copies, waits for them, and re-layouts: 5.29 us -> none  [the longest x6 3.83 us: halved(): got = flip(pairs[:, 1], 'seq', mask)]
    add x2 -> x3, other arithmetic: 0.01 us -> 4.47 us  [the longest x2 2.53 us: scan_take(): total.astype(f32) + got]
    concatenate x0 -> x7, other arithmetic: none -> 3.7 us  [the longest x1 2.31 us: per_device(): weights = lax.optimization_barrier(jnp.concatenate(joined, axis=1))]
  transfers between devices with their start and end apart: 31 -> 30, of which waited for: 12 -> 9; matrix products, arithmetic and copies ran while one was open for 19% -> 25% of each run, Pallas kernels for 21% -> 23%
where the time goes in v1:
time: 200 us; the launch traced here: 199 us
  Pallas kernels  53.3 us (27%)
  waiting for transfers between devices  48.5 us (24%)
  matrix products  33.8 us (17%)
  starting transfers between devices  28.9 us (14%)
  other arithmetic  20.2 us (10%)
  local copies, waits for them, and re-layouts  12.6 us (6%)
    pallas_call x7, Pallas kernels, call(): pl.pallas_call(kernel, out_shape=out_shapes, grid_spec=pltpu.PrefetchScal...  53.3 us
    ppermute x25, waiting for transfers between devices, flip(): return lax.ppermute(x, axis, [(i, i ^ mask) for i in range(n)])  48.5 us
    ppermute x25, starting transfers between devices, flip(): return lax.ppermute(x, axis, [(i, i ^ mask) for i in range(n)])  24.9 us
    dot_general x6, matrix products, mm_nt(): return lax.dot_general(a, b, CONTRACT_COLS, preferred_element_type=f32)  11.8 us
    dot_general x7, matrix products, mm(): return jnp.dot(a, b, preferred_element_type=f32)  11.8 us
    dot_general x8, matrix products, mm_tn(): return lax.dot_general(a, b, CONTRACT_ROWS, preferred_element_type=f32)  10.1 us
    unnamed x93, local copies, waits for them, and re-layouts  7.73 us
  transfers between devices with their start and end apart: 30, of which 9 were waited for; matrix products, arithmetic and copies ran while one was open for 25% of the time, Pallas kernels for 23%

profile of v1, /device:TPU:0, one launch (start us, length us, event | category | flops | bytes accessed | tf_op | source)
XLA Modules:
  0.0 198.7 jit_solution(7287549509143015683)
XLA Ops:
  1.2 2.6 %collective-permute-start.1 = (bf16[256,2048]{1,0:T(8,128)(2,1)}, bf16[256,2048]{1,0:T(8,128)(2,1)}, u32[]{:S(2)}, u32[]{:S(2)}) collective-permute-start(bf16[256,2048]{1,0:T(8,128)(2,1)} %refs_1_), channel_id=1, source_target_pairs={{0,2},{1,3},{2,0},{3,1},{4,6},{5,7},{6,4},{7,5},{8,10},{9,11},{10,... | collective-permute-start | bytes 3145736 | tf_op jit(solution)/shard_map/ppermute | solution.py:362
  3.9 2.7 %convolution_convert_fusion.9 = bf16[256,512]{1,0:T(8,128)(2,1)} fusion(bf16[256,2048]{1,0:T(8,128)(2,1)} %refs_1_.1, bf16[512,2048]{1,0:T(8,128)(2,1)S(1)} %copy-done), kind=kOutput, calls=%fused_computation.26 | convolution fusion | flops 537001984 | bytes 3407872 | tf_op jit(solution)/shard_map/dot_general | solution.py:29
  9.6 2.0 copy.28
  11.6 2.3 %pad_maximum_fusion = bf16[2048,640]{1,0:T(8,128)(2,1)S(1)} fusion(bf16[2048,64]{1,0:T(8,128)(2,1)} %copy.28, bf16[2048,64]{1,0:T(8,128)(2,1)} %copy.27, bf16[2048,512]{1,0:T(8,128)(2,1)} %param.17), kind=kLoop, calls=%fused_computation.4 | loop fusion | flops 7864320 | bytes 5242880 | tf_op jit(solution)/shard_map/concatenate | solution.py:514
  15.6 2.9 %fusion.5.refs_2_ = bf16[256,640]{1,0:T(8,128)(2,1)} fusion(bf16[256,2048]{1,0:T(8,128)(2,1)} %collective-permute-done.refs_3_, bf16[2048,640]{1,0:T(8,128)(2,1)S(1)} %pad_maximum_fusion), kind=kOutput, calls=%fused_computation.28 | convolution fusion | flops 671252480 | bytes 3997696 | tf_op jit(solution)/shard_map/dot_general | solution.py:25
  19.4 2.7 %convolution_convert_fusion.8 = bf16[256,512]{1,0:T(8,128)(2,1)} fusion(bf16[256,2048]{1,0:T(8,128)(2,1)} %collective-permute-done.6.refs_3_, bf16[512,2048]{1,0:T(8,128)(2,1)S(1)} %copy-done), kind=kOutput, calls=%fused_computation.25 | convolution fusion | flops 537001984 | bytes 3407872 | tf_op jit(solution)/shard_map/dot_general | solution.py:29
  22.5 5.5 %collective-permute-done.1.refs_2_ = bf16[256,2048]{1,0:T(8,128)(2,1)} collective-permute-done((bf16[256,2048]{1,0:T(8,128)(2,1)}, bf16[256,2048]{1,0:T(8,128)(2,1)}, u32[]{:S(2)}, u32[]{:S(2)}) %collective-permute-start.1) | collective-permute-done | bytes 1048608 | tf_op jit(solution)/shard_map/ppermute | solution.py:362
  28.0 3.2 %convolution_convert_fusion.5.refs_3_ = bf16[256,640]{1,0:T(8,128)(2,1)S(1)} fusion(bf16[256,2048]{1,0:T(8,128)(2,1)} %collective-permute-done.1.refs_2_, bf16[2048,640]{1,0:T(8,128)(2,1)} %copy-done.29), kind=kOutput, calls=%fused_computation.18 | convolution fusion | flops 671252480 | bytes 3997696 | tf_op jit(solution)/shard_map/dot_general | solution.py:25
  33.9 6.2 %shard_map.197 = (bf16[1024,128]{1,0:T(8,128)(2,1)S(1)}, bf16[1024,512]{1,0:T(8,128)(2,1)S(1)}, bf16[1024,512]{1,0:T(8,128)(2,1)S(1)}, bf16[4,4,160,128]{3,2,1,0:T(8,128)(2,1)S(1)}, bf16[4,160,128]{2,1,0:T(8,128)(2,1)}) custom-call(s32[1]{0:T(128)} %bitcast.refs_0_, bf16[256,640]{1,0:T(8,128)(2,1)S(1)} %copy-done.21, bf16[256,640]{1,0:T(8,128)(2,1)S(1)} %copy-done.22, ...), custom_call_target="tpu_custom_call" | custom-call | tf_op jit(solution)/shard_map/pallas_call | solution.py:338
  44.7 7.6 %shard_map.198 = (bf16[1024,512]{1,0:T(8,128)(2,1)}, bf16[1024,1024]{1,0:T(8,128)(2,1)}, bf16[4,256,1024]{2,1,0:T(8,128)(2,1)}, bf16[4,1024,256]{2,1,0:T(8,128)(...) custom-call(s32[1]{0:T(128)} %bitcast.refs_0_, ...), custom_call_target="tpu_custom_call" | custom-call | tf_op jit(solution)/shard_map/pallas_call | solution.py:338
  55.9 7.2 %shard_map.199 = (bf16[1024,1024]{1,0:T(8,128)(2,1)}, bf16[1024,1024]{1,0:T(8,128)(2,1)}) custom-call(s32[8]{0:T(128)S(1)} %broadcast_xor_fusion.refs_0_, bf16[256,2048]{1,0:T(8,128)(2,1)S(1)} %copy-done.8, bf16[256,2048]{1,0:T(8,128)(2,1)} %collective-permute-done.1.refs_2_, bf16[256,2048]{1,0:T(8,128)(2,1)} %collective-permute-done.refs_3_, ...), custom_call_target="tpu_custom_call" | custom-call | tf_op jit(solution)/shard_map/pallas_call | solution.py:338
  65.0 2.6 %collective-permute-start.10 = (bf16[4,160,128]{2,1,0:T(8,128)(2,1)}, bf16[4,160,128]{2,1,0:T(8,128)(2,1)S(1)}, u32[]{:S(2)}, u32[]{:S(2)}) collective-permute-start(bf16[4,160,128]{2,1,0:T(8,128)(2,1)} %convert_add_fusion.3), channel_id=1, source_target_pairs={{0,16},{4,20},{8,24},{12,28},{16,0},{20,4},{24,8},{28,12},{1,17},{... | collective-permute-start | bytes 491528 | tf_op jit(solution)/shard_map/ppermute | solution.py:362
  67.6 2.1 %fusion.6 = bf16[1,256,512]{2,1,0:T(8,128)(2,1)S(1)} fusion(bf16[256,2048]{1,0:T(8,128)(2,1)} %collective-permute-done.11.refs_2_, bf16[512,2048]{1,0:T(8,128)(2,1)S(1)} %copy-done), kind=kOutput, calls=%fused_computation.29 | convolution fusion | flops 537001984 | bytes 3407872 | tf_op jit(solution)/shard_map/dot_general | solution.py:29
  70.7 5.4 %collective-permute-done.10 = bf16[4,160,128]{2,1,0:T(8,128)(2,1)S(1)} collective-permute-done((bf16[4,160,128]{2,1,0:T(8,128)(2,1)}, bf16[4,160,128]{2,1,0:T(8,128)(2,1)S(1)}, u32[]{:S(2)}, u32[]{:S(2)}) %collective-permute-start.10) | collective-permute-done | bytes 163872 | tf_op jit(solution)/shard_map/ppermute | solution.py:362
  77.1 7.2 %shard_map.200 = (bf16[2,256,512]{2,1,0:T(8,128)(2,1)S(1)}, bf16[2,256,512]{2,1,0:T(8,128)(2,1)S(1)}, bf16[1024,512]{1,0:T(8,128)(2,1)S(1)}, bf16[4,4,160,128]{3...) custom-call(s32[1]{0:T(128)} %bitcast.refs_0_, ...), custom_call_target="tpu_custom_call" | custom-call | tf_op jit(solution)/shard_map/pallas_call | solution.py:338
  87.7 7.4 %shard_map.201 = (bf16[1024,1024]{1,0:T(8,128)(2,1)}, bf16[1024,1024]{1,0:T(8,128)(2,1)}) custom-call(s32[8]{0:T(128)S(1)} %broadcast_xor_fusion.refs_0_, bf16[256,2048]{1,0:T(8,128)(2,1)} %refs_1_.1, bf16[256,2048]{1,0:T(8,128)(2,1)} %collective-permute-done.11.refs_2_, bf16[256,2048]{1,0:T(8,128)(2,1)} %collective-permute-done.6.refs_3_, ...), custom_call_target="tpu_custom_call" | custom-call | tf_op jit(solution)/shard_map/pallas_call | solution.py:338
  96.8 2.3 %multiply_convert_fusion.1 = bf16[512,1024]{1,0:T(8,128)(2,1)} fusion(bf16[1024,512]{1,0:T(8,128)(2,1)S(1)} %pad_maximum_fusion.2, bf16[1024,1024]{1,0:T(8,128)(2,1)S(1)} %copy-done.35), kind=kOutput, calls=%fused_computation.8 | convolution fusion | flops 1074790400 | bytes 4194304 | tf_op jit(solution)/shard_map/dot_general | solution.py:33
  102.5 2.3 %multiply_convert_fusion = bf16[512,1024]{1,0:T(8,128)(2,1)} fusion(bf16[1024,512]{1,0:T(8,128)(2,1)S(1)} %pad_maximum_fusion.2, bf16[1024,1024]{1,0:T(8,128)(2,1)S(1)} %copy-done.34), kind=kOutput, calls=%fused_computation.7 | convolution fusion | flops 1074790400 | bytes 4194304 | tf_op jit(solution)/shard_map/dot_general | solution.py:33
  104.8 1.9 collective-permute-done.15
  110.2 10.1 %shard_map.202 = (f32[1024,128]{1,0:T(8,128)S(1)}, bf16[1024,512]{1,0:T(8,128)(2,1)S(1)}) custom-call(s32[1]{0:T(128)} %bitcast.refs_0_, bf16[1024,128]{1,0:T(8,128)(2,1)S(1)} %get-tuple-element.107.refs_1_.refs_7_.refs_2_, bf16[1024,512]{1,0:T(8,128)(2,1)} %copy-done.2, bf16[1024,512]{1,0:T(8,128)(2,1)S(1)} %copy-done.10, ...), custom_call_target="tpu_custom_call" | custom-call | tf_op jit(solution)/shard_map/pallas_call | solution.py:338
  121.5 3.3 %collective-permute-done.16 = bf16[512,1024]{1,0:T(8,128)(2,1)} collective-permute-done((bf16[512,1024]{1,0:T(8,128)(2,1)}, bf16[512,1024]{1,0:T(8,128)(2,1)}, u32[]{:S(2)}, u32[]{:S(2)}) %collective-permute-start.16) | collective-permute-done | bytes 1048608 | tf_op jit(solution)/shard_map/ppermute | solution.py:362
  124.9 2.0 %add_convert_fusion.4 = bf16[512,512]{1,0:T(8,128)(2,1)} fusion(bf16[512,1024]{1,0:T(8,128)(2,1)S(1)} %copy-done.28, bf16[512,1024]{1,0:T(8,128)(2,1)} %collective-permute-done.16), kind=kLoop, calls=%fused_computation.38 | loop fusion | flops 1048576 | bytes 1572864 | tf_op jit(solution)/shard_map/convert_element_type | solution.py:467
  126.9 7.5 %shard_map.203 = (bf16[4,256,384]{2,1,0:T(8,128)(2,1)S(1)}, bf16[4,256,256]{2,1,0:T(8,128)(2,1)S(1)}, bf16[2,256,640]{2,1,0:T(8,128)(2,1)S(1)}, bf16[2,256,640]{2,1,0:T(8,128)(2,1)S(1)}, f32[8,512]{1,0:T(8,128)S(1)}) custom-call(s32[1]{0:T(128)} %bitcast.refs_0_, f32[1024,128]{1,0:T(8,128)S(1)} %get-tuple-element.115.refs_1_, ...), custom_call_target="tpu_custom_call" | custom-call | tf_op jit(solution)/shard_map/pallas_call | solution.py:338
  135.3 2.7 %multiply_convert_fusion.3 = bf16[384,1024]{1,0:T(8,128)(2,1)S(1)} fusion(bf16[1024,384]{1,0:T(8,128)(2,1)S(1)} %bitcast.68, bf16[1024,1024]{1,0:T(8,128)(2,1)} %get-tuple-element.90), kind=kOutput, calls=%fused_computation.10 | convolution fusion | flops 806092800 | bytes 3670016 | tf_op jit(solution)/shard_map/dot_general | solution.py:33
  138.0 2.1 %collective-permute-done.19 = bf16[512,512]{1,0:T(8,128)(2,1)} collective-permute-done((bf16[512,512]{1,0:T(8,128)(2,1)}, bf16[512,512]{1,0:T(8,128)(2,1)}, u32[]{:S(2)}, u32[]{:S(2)}) %collective-permute-start.19) | collective-permute-done | bytes 524320 | tf_op jit(solution)/shard_map/ppermute | solution.py:362
  145.5 2.0 %collective-permute-start.22 = (bf16[384,1024]{1,0:T(8,128)(2,1)S(1)}, bf16[384,1024]{1,0:T(8,128)(2,1)S(1)}, u32[]{:S(2)}, u32[]{:S(2)}) collective-permute-start(bf16[384,1024]{1,0:T(8,128)(2,1)S(1)} %multiply_convert_fusion.3), channel_id=1, source_target_pairs={{0,4},{4,0},{8,12},{12,8},{16,20},{20,16},{24,28},{28,24},{1,5},{5... | collective-permute-start | bytes 2359304 | tf_op jit(solution)/shard_map/ppermute | solution.py:362
  150.3 1.8 add_convert_fusion
  153.1 12.6 %collective-permute-done.22 = bf16[384,1024]{1,0:T(8,128)(2,1)S(1)} collective-permute-done((bf16[384,1024]{1,0:T(8,128)(2,1)S(1)}, bf16[384,1024]{1,0:T(8,128)(2,1)S(1)}, u32[]{:S(2)}, u32[]{:S(2)}) %collective-permute-start.22) | collective-permute-done | bytes 786464 | tf_op jit(solution)/shard_map/ppermute | solution.py:362
  171.5 2.6 %add_convert_fusion.3 = bf16[256,2048]{1,0:T(8,128)(2,1)} fusion(bf16[256,2048]{1,0:T(8,128)(2,1)} %collective-permute-done.20, bf16[512,2048]{1,0:T(8,128)(2,1)S(1)} %copy-done.26), kind=kLoop, calls=%fused_computation.6 | loop fusion | flops 2097152 | bytes 3145728 | tf_op jit(solution)/shard_map/convert_element_type | solution.py:729
  174.0 1.9 convert_add_fusion
  176.0 8.8 %collective-permute-done.26 = bf16[384,512]{1,0:T(8,128)(2,1)S(1)} collective-permute-done((bf16[384,512]{1,0:T(8,128)(2,1)S(1)}, bf16[384,512]{1,0:T(8,128)(2,1)S(1)}, u32[]{:S(2)}, u32[]{:S(2)}) %collective-permute-start.26) | collective-permute-done | bytes 393248 | tf_op jit(solution)/shard_map/ppermute | solution.py:362
  186.9 7.4 %collective-permute-done.24 = bf16[256,2048]{1,0:T(8,128)(2,1)S(1)} collective-permute-done((bf16[256,2048]{1,0:T(8,128)(2,1)S(1)}, bf16[256,2048]{1,0:T(8,128)(2,1)S(1)}, u32[]{:S(2)}, u32[]{:S(2)}) %collective-permute-start.24) | collective-permute-done | bytes 1048608 | tf_op jit(solution)/shard_map/ppermute | solution.py:362
  (192 shorter events, 56.1 us)
Async XLA Ops:
  0.7 5.9 %collective-permute-start = (bf16[256,2048]{1,0:T(8,128)(2,1)}, bf16[256,2048]{1,0:T(8,128)(2,1)}, u32[]{:S(2)}, u32[]{:S(2)}) collective-permute-start(bf16[256,2048]{1,0:T(8,128)(2,1)} %refs_1_), channel_id=1, source_target_pairs={{0,1},{1,0},{2,3},{3,2},{4,5},{5,4},{6,7},{7,6},{8,9},{9,8},{10,11... | collective-permute-start | bytes 3145736 | tf_op jit(solution)/shard_map/ppermute | solution.py:362
  1.2 26.8 %collective-permute-start.1 = (bf16[256,2048]{1,0:T(8,128)(2,1)}, bf16[256,2048]{1,0:T(8,128)(2,1)}, u32[]{:S(2)}, u32[]{:S(2)}) collective-permute-start(bf16[256,2048]{1,0:T(8,128)(2,1)} %refs_1_), channel_id=1, source_target_pairs={{0,2},{1,3},{2,0},{3,1},{4,6},{5,7},{6,4},{7,5},{8,10},{9,11},{10,... | collective-permute-start | bytes 3145736 | tf_op jit(solution)/shard_map/ppermute | solution.py:362
  3.8 14.8 %collective-permute-start.6 = (bf16[256,2048]{1,0:T(8,128)(2,1)}, bf16[256,2048]{1,0:T(8,128)(2,1)}, u32[]{:S(2)}, u32[]{:S(2)}) collective-permute-start(bf16[256,2048]{1,0:T(8,128)(2,1)} %refs_1_.1), channel_id=1, source_target_pairs={{0,1},{1,0},{2,3},{3,2},{4,5},{5,4},{6,7},{7,6},{8,9},{9,8},{10,11... | collective-permute-start | bytes 3145736 | tf_op jit(solution)/shard_map/ppermute | solution.py:362
  6.6 15.4 %collective-permute-start.5 = (bf16[2,2048]{1,0:T(2,128)(2,1)S(1)}, bf16[2,2048]{1,0:T(2,128)(2,1)S(1)}, u32[]{:S(2)}, u32[]{:S(2)}) collective-permute-start(bf16[2,2048]{1,0:T(2,128)(2,1)S(1)} %slice.171), channel_id=1, source_target_pairs={{3,7},{7,11},{11,15},{15,19},{19,23},{23,27},{27,31}} | collective-permute-start | bytes 24584 | tf_op jit(solution)/shard_map/ppermute | solution.py:507
  7.3 14.8 %collective-permute-start.4 = (bf16[2,2048]{1,0:T(2,128)(2,1)S(1)}, bf16[2,2048]{1,0:T(2,128)(2,1)S(1)}, u32[]{:S(2)}, u32[]{:S(2)}) collective-permute-start(bf16[2,2048]{1,0:T(2,128)(2,1)S(1)} %slice.171), channel_id=1, source_target_pairs={{3,6},{7,10},{11,14},{15,18},{19,22},{23,26},{27,30}} | collective-permute-start | bytes 24584 | tf_op jit(solution)/shard_map/ppermute | solution.py:507
  8.0 14.1 %collective-permute-start.3 = (bf16[2,2048]{1,0:T(2,128)(2,1)S(1)}, bf16[2,2048]{1,0:T(2,128)(2,1)S(1)}, u32[]{:S(2)}, u32[]{:S(2)}) collective-permute-start(bf16[2,2048]{1,0:T(2,128)(2,1)S(1)} %slice.171), channel_id=1, source_target_pairs={{3,5},{7,9},{11,13},{15,17},{19,21},{23,25},{27,29}} | collective-permute-start | bytes 24584 | tf_op jit(solution)/shard_map/ppermute | solution.py:507
  18.6 3.5 %collective-permute-start.2 = (bf16[2,2048]{1,0:T(2,128)(2,1)S(1)}, bf16[2,2048]{1,0:T(2,128)(2,1)S(1)}, u32[]{:S(2)}, u32[]{:S(2)}) collective-permute-start(bf16[2,2048]{1,0:T(2,128)(2,1)S(1)} %slice.171), channel_id=1, source_target_pairs={{3,4},{7,8},{11,12},{15,16},{19,20},{23,24},{27,28}} | collective-permute-start | bytes 24584 | tf_op jit(solution)/shard_map/ppermute | solution.py:507
  28.0 4.9 %collective-permute-start.7 = (bf16[256,2048]{1,0:T(8,128)(2,1)}, bf16[256,2048]{1,0:T(8,128)(2,1)S(1)}, u32[]{:S(2)}, u32[]{:S(2)}) collective-permute-start(bf16[256,2048]{1,0:T(8,128)(2,1)} %collective-permute-done.1.refs_2_), channel_id=1, source_target_pairs={{0,1},{1,0},{2,3},{3,2},{4,5},{5,4},{6,7},{7,6},{8,9},{9,8},{10,11... | collective-permute-start | bytes 3145736 | tf_op jit(solution)/shard_map/ppermute | solution.py:362
  31.2 33.7 %collective-permute-start.11 = (bf16[256,2048]{1,0:T(8,128)(2,1)}, bf16[256,2048]{1,0:T(8,128)(2,1)}, u32[]{:S(2)}, u32[]{:S(2)}) collective-permute-start(bf16[256,2048]{1,0:T(8,128)(2,1)} %refs_1_.1), channel_id=1, source_target_pairs={{0,2},{1,3},{2,0},{3,1},{4,6},{5,7},{6,4},{7,5},{8,10},{9,11},{10,... | collective-permute-start | bytes 3145736 | tf_op jit(solution)/shard_map/ppermute | solution.py:362
  41.9 21.2 %copy-start.2 = (bf16[1024,512]{1,0:T(8,128)(2,1)}, bf16[1024,512]{1,0:T(8,128)(2,1)S(1)}, u32[]{:S(2)}) copy-start(bf16[1024,512]{1,0:T(8,128)(2,1)S(1)} %get-tuple-element.81.refs_2_.refs_4_) | copy-start | bytes 3145732
  41.9 11.3 %collective-permute-start.8 = (bf16[4,160,128]{2,1,0:T(8,128)(2,1)}, bf16[4,160,128]{2,1,0:T(8,128)(2,1)}, u32[]{:S(2)}, u32[]{:S(2)}) collective-permute-start(bf16[4,160,128]{2,1,0:T(8,128)(2,1)} %get-tuple-element.86), channel_id=1, source_target_pairs={{0,4},{4,0},{8,12},{12,8},{16,20},{20,16},{24,28},{28,24},{1,5},{5... | collective-permute-start | bytes 491528 | tf_op jit(solution)/shard_map/ppermute | solution.py:362
  54.2 8.9 %collective-permute-start.9 = (bf16[4,160,128]{2,1,0:T(8,128)(2,1)S(1)}, bf16[4,160,128]{2,1,0:T(8,128)(2,1)S(1)}, u32[]{:S(2)}, u32[]{:S(2)}) collective-permute-start(bf16[4,160,128]{2,1,0:T(8,128)(2,1)S(1)} %fusion.22), channel_id=1, source_target_pairs={{0,8},{4,12},{8,0},{12,4},{16,24},{20,28},{24,16},{28,20},{1,9},{5... | collective-permute-start | bytes 491528 | tf_op jit(solution)/shard_map/ppermute | solution.py:362
  65.0 4.8 %collective-permute-start.12 = (bf16[256,2048]{1,0:T(8,128)(2,1)}, bf16[256,2048]{1,0:T(8,128)(2,1)S(1)}, u32[]{:S(2)}, u32[]{:S(2)}) collective-permute-start(bf16[256,2048]{1,0:T(8,128)(2,1)} %collective-permute-done.11.refs_2_), channel_id=1, source_target_pairs={{0,1},{1,0},{2,3},{3,2},{4,5},{5,4},{6,7},{7,6},{8,9},{9,8},{10,11... | collective-permute-start | bytes 3145736 | tf_op jit(solution)/shard_map/ppermute | solution.py:362
  65.0 11.1 %collective-permute-start.10 = (bf16[4,160,128]{2,1,0:T(8,128)(2,1)}, bf16[4,160,128]{2,1,0:T(8,128)(2,1)S(1)}, u32[]{:S(2)}, u32[]{:S(2)}) collective-permute-start(bf16[4,160,128]{2,1,0:T(8,128)(2,1)} %convert_add_fusion.3), channel_id=1, source_target_pairs={{0,16},{4,20},{8,24},{12,28},{16,0},{20,4},{24,8},{28,12},{1,17},{... | collective-permute-start | bytes 491528 | tf_op jit(solution)/shard_map/ppermute | solution.py:362
  85.7 9.5 %collective-permute-start.13 = (bf16[512,2048]{1,0:T(8,128)(2,1)S(1)}, bf16[512,2048]{1,0:T(8,128)(2,1)S(1)}, u32[]{:S(2)}, u32[]{:S(2)}) collective-permute-start(bf16[512,2048]{1,0:T(8,128)(2,1)S(1)} %convolution_convert_fusion), channel_id=1, source_target_pairs={{0,1},{1,0},{2,3},{3,2},{4,5},{5,4},{6,7},{7,6},{8,9},{9,8},{10,11... | collective-permute-start | bytes 6291464 | tf_op jit(solution)/shard_map/ppermute | solution.py:362
  85.8 9.3 %collective-permute-start.14 = (bf16[4,160,128]{2,1,0:T(8,128)(2,1)S(1)}, bf16[4,160,128]{2,1,0:T(8,128)(2,1)S(1)}, u32[]{:S(2)}, u32[]{:S(2)}) collective-permute-start(bf16[4,160,128]{2,1,0:T(8,128)(2,1)S(1)} %get-tuple-element.98), channel_id=1, source_target_pairs={{0,4},{4,0},{8,12},{12,8},{16,20},{20,16},{24,28},{28,24},{1,5},{5... | collective-permute-start | bytes 491528 | tf_op jit(solution)/shard_map/ppermute | solution.py:362
  99.1 25.8 %collective-permute-start.16 = (bf16[512,1024]{1,0:T(8,128)(2,1)}, bf16[512,1024]{1,0:T(8,128)(2,1)}, u32[]{:S(2)}, u32[]{:S(2)}) collective-permute-start(bf16[512,1024]{1,0:T(8,128)(2,1)} %multiply_convert_fusion.1), channel_id=1, source_target_pairs={{0,4},{4,0},{8,12},{12,8},{16,20},{20,16},{24,28},{28,24},{1,5},{5... | collective-permute-start | bytes 3145736 | tf_op jit(solution)/shard_map/ppermute | solution.py:362
  100.7 6.1 %collective-permute-start.15 = (bf16[4,160,128]{2,1,0:T(8,128)(2,1)S(1)}, bf16[4,160,128]{2,1,0:T(8,128)(2,1)S(1)}, u32[]{:S(2)}, u32[]{:S(2)}) collective-permute-start(bf16[4,160,128]{2,1,0:T(8,128)(2,1)S(1)} %fusion.23), channel_id=1, source_target_pairs={{0,8},{4,12},{8,0},{12,4},{16,24},{20,28},{24,16},{28,20},{1,9},{5... | collective-permute-start | bytes 491528 | tf_op jit(solution)/shard_map/ppermute | solution.py:362
  101.8 33.4 %collective-permute-start.20 = (bf16[256,2048]{1,0:T(8,128)(2,1)}, bf16[256,2048]{1,0:T(8,128)(2,1)}, u32[]{:S(2)}, u32[]{:S(2)}) collective-permute-start(bf16[256,2048]{1,0:T(8,128)(2,1)} %slice.221), channel_id=1, source_target_pairs={{0,2},{1,3},{2,0},{3,1},{4,6},{5,7},{6,4},{7,5},{8,10},{9,11},{10,... | collective-permute-start | bytes 3145736 | tf_op jit(solution)/shard_map/ppermute | solution.py:362
  107.5 12.8 %collective-permute-start.17 = (bf16[4,160,128]{2,1,0:T(8,128)(2,1)}, bf16[4,160,128]{2,1,0:T(8,128)(2,1)}, u32[]{:S(2)}, u32[]{:S(2)}) collective-permute-start(bf16[4,160,128]{2,1,0:T(8,128)(2,1)} %convert_add_fusion.1), channel_id=1, source_target_pairs={{0,16},{4,20},{8,24},{12,28},{16,0},{20,4},{24,8},{28,12},{1,17},{... | collective-permute-start | bytes 491528 | tf_op jit(solution)/shard_map/ppermute | solution.py:362
  108.9 18.0 %collective-permute-start.18 = (f32[8,640]{1,0:T(8,128)S(1)}, f32[8,640]{1,0:T(8,128)S(1)}, u32[]{:S(2)}, u32[]{:S(2)}) collective-permute-start(f32[8,640]{1,0:T(8,128)S(1)} %get-tuple-element.118), channel_id=1, source_target_pairs={{4,0},{8,4},{12,8},{16,12},{20,16},{24,20},{28,24},{5,1},{9,5},{13... | collective-permute-start | bytes 61448 | tf_op jit(solution)/shard_map/ppermute | solution.py:641
  110.2 14.6 %copy-start.28 = (bf16[512,1024]{1,0:T(8,128)(2,1)S(1)}, bf16[512,1024]{1,0:T(8,128)(2,1)}, u32[]{:S(2)}) copy-start(bf16[512,1024]{1,0:T(8,128)(2,1)} %multiply_convert_fusion) | copy-start | bytes 3145732
  126.9 13.3 %collective-permute-start.19 = (bf16[512,512]{1,0:T(8,128)(2,1)}, bf16[512,512]{1,0:T(8,128)(2,1)}, u32[]{:S(2)}, u32[]{:S(2)}) collective-permute-start(bf16[512,512]{1,0:T(8,128)(2,1)} %add_convert_fusion.4), channel_id=1, source_target_pairs={{0,8},{4,12},{8,0},{12,4},{16,24},{20,28},{24,16},{28,20},{1,9},{5... | collective-permute-start | bytes 1572872 | tf_op jit(solution)/shard_map/ppermute | solution.py:362
  145.4 4.8 %collective-permute-start.21 = (bf16[512,2048]{1,0:T(8,128)(2,1)S(1)}, bf16[512,2048]{1,0:T(8,128)(2,1)S(1)}, u32[]{:S(2)}, u32[]{:S(2)}) collective-permute-start(bf16[512,2048]{1,0:T(8,128)(2,1)S(1)} %convolution_convert_fusion.1), channel_id=1, source_target_pairs={{0,1},{1,0},{2,3},{3,2},{4,5},{5,4},{6,7},{7,6},{8,9},{9,8},{10,11... | collective-permute-start | bytes 6291464 | tf_op jit(solution)/shard_map/ppermute | solution.py:362
  145.5 20.2 %collective-permute-start.22 = (bf16[384,1024]{1,0:T(8,128)(2,1)S(1)}, bf16[384,1024]{1,0:T(8,128)(2,1)S(1)}, u32[]{:S(2)}, u32[]{:S(2)}) collective-permute-start(bf16[384,1024]{1,0:T(8,128)(2,1)S(1)} %multiply_convert_fusion.3), channel_id=1, source_target_pairs={{0,4},{4,0},{8,12},{12,8},{16,20},{20,16},{24,28},{28,24},{1,5},{5... | collective-permute-start | bytes 2359304 | tf_op jit(solution)/shard_map/ppermute | solution.py:362
  147.5 26.5 %collective-permute-start.27 = (bf16[512,256]{1,0:T(8,128)(2,1)S(1)}, bf16[512,256]{1,0:T(8,128)(2,1)S(1)}, u32[]{:S(2)}, u32[]{:S(2)}) collective-permute-start(bf16[512,256]{1,0:T(8,128)(2,1)S(1)} %add_convert_fusion.7), channel_id=1, source_target_pairs={{0,16},{4,20},{8,24},{12,28},{16,0},{20,4},{24,8},{28,12},{1,17},{... | collective-permute-start | bytes 786440 | tf_op jit(solution)/shard_map/ppermute | solution.py:362
  148.6 19.7 %collective-permute-start.23 = (bf16[264,1024]{1,0:T(8,128)(2,1)S(1)}, bf16[264,1024]{1,0:T(8,128)(2,1)S(1)}, u32[]{:S(2)}, u32[]{:S(2)}) collective-permute-start(bf16[264,1024]{1,0:T(8,128)(2,1)S(1)} %pad_maximum_fusion.4), channel_id=1, source_target_pairs={{0,8},{4,12},{8,0},{12,4},{16,24},{20,28},{24,16},{28,20},{1,9},{5... | collective-permute-start | bytes 1622024 | tf_op jit(solution)/shard_map/ppermute | solution.py:362
  168.3 17.7 %collective-permute-start.25 = (bf16[264,512]{1,0:T(8,128)(2,1)S(1)}, bf16[264,512]{1,0:T(8,128)(2,1)S(1)}, u32[]{:S(2)}, u32[]{:S(2)}) collective-permute-start(bf16[264,512]{1,0:T(8,128)(2,1)S(1)} %add_convert_fusion.6), channel_id=1, source_target_pairs={{0,16},{4,20},{8,24},{12,28},{16,0},{20,4},{24,8},{28,12},{1,17},{... | collective-permute-start | bytes 811016 | tf_op jit(solution)/shard_map/ppermute | solution.py:362
  168.9 15.9 %collective-permute-start.26 = (bf16[384,512]{1,0:T(8,128)(2,1)S(1)}, bf16[384,512]{1,0:T(8,128)(2,1)S(1)}, u32[]{:S(2)}, u32[]{:S(2)}) collective-permute-start(bf16[384,512]{1,0:T(8,128)(2,1)S(1)} %add_convert_fusion.5), channel_id=1, source_target_pairs={{0,8},{4,12},{8,0},{12,4},{16,24},{20,28},{24,16},{28,20},{1,9},{5... | collective-permute-start | bytes 1179656 | tf_op jit(solution)/shard_map/ppermute | solution.py:362
  170.7 23.6 %collective-permute-start.24 = (bf16[256,2048]{1,0:T(8,128)(2,1)S(1)}, bf16[256,2048]{1,0:T(8,128)(2,1)S(1)}, u32[]{:S(2)}, u32[]{:S(2)}) collective-permute-start(bf16[256,2048]{1,0:T(8,128)(2,1)S(1)} %slice.233), channel_id=1, source_target_pairs={{0,2},{1,3},{2,0},{3,1},{4,6},{5,7},{6,4},{7,5},{8,10},{9,11},{10,... | collective-permute-start | bytes 3145736 | tf_op jit(solution)/shard_map/ppermute | solution.py:362
  184.9 12.7 %collective-permute-start.29 = (bf16[384,256]{1,0:T(8,128)(2,1)S(1)}, bf16[384,256]{1,0:T(8,128)(2,1)S(1)}, u32[]{:S(2)}, u32[]{:S(2)}) collective-permute-start(bf16[384,256]{1,0:T(8,128)(2,1)S(1)} %add_convert_fusion.9), channel_id=1, source_target_pairs={{0,16},{4,20},{8,24},{12,28},{16,0},{20,4},{24,8},{28,12},{1,17},{... | collective-permute-start | bytes 589832 | tf_op jit(solution)/shard_map/ppermute | solution.py:362
  186.1 9.6 %collective-permute-start.28 = (bf16[264,256]{1,0:T(8,128)(2,1)S(1)}, bf16[264,256]{1,0:T(8,128)(2,1)S(1)}, u32[]{:S(2)}, u32[]{:S(2)}) collective-permute-start(bf16[264,256]{1,0:T(8,128)(2,1)S(1)} %add_convert_fusion.10), channel_id=1, source_target_pairs={{0,4},{4,0},{8,12},{12,8},{16,20},{20,16},{24,28},{28,24},{1,5},{5... | collective-permute-start | bytes 405512 | tf_op jit(solution)/shard_map/ppermute | solution.py:362
  (44 other events, 222.0 us)

commit v2 on v1

--- a/solution.py
+++ b/solution.py
@@ -579,16 +579,10 @@
     )
     got = held(got, local)
     ordered = lambda pieces: [pieces[j] for j in evens + odds]
-    tokens_for = None
     while got is not None:
         before, total = scan_take(before, total, got, mask, False)
         mask *= 2
         got = scan_send(total, mask)
-        if tokens_for is None:
-            ready = ordered(tokens)
-            ready[0] = held(ready[0], total)
-            tokens_for = arranged(ready, masks_of(0))
-            got = held(got, *tokens_for) if got is not None else None
         if mask * 2 == ns:
             for j in evens[1:]:
                 piece = held(far_cot[j], total)
@@ -596,7 +590,10 @@
             pulled += [pull(piece) for piece in cotangent[2:]]
             by_place = [pulled[j] for j in evens + odds]
             grad_attn = jnp.stack(by_place)
-            got = held(got, grad_attn)
+            ready = ordered(cotangent)
+            ready[0] = held(ready[0], grad_attn)
+            cot_for = arranged(ready, masks_of(0))
+            got = held(got, *cot_for)
     carried = before.astype(bf16)
 
     half_shape = shape((nt // 2, rows, vw), bf16)
@@ -632,9 +629,9 @@
     )
 
     attn_all = jnp.concatenate([attn_even.reshape(-1, vw), attn_odd.reshape(-1, vw)], axis=0)
-    ready = ordered(cotangent)
+    ready = ordered(tokens)
     ready[0] = held(ready[0], gtotal)
-    cot_for = arranged(ready, masks_of(0))
+    tokens_for = arranged(ready, masks_of(0))
     out_halve = Halve(False, attn_all, cot_for, grad_scale)
     after = jnp.zeros(state_shape, f32)
     got = scan_send(gtotal, 1)
@@ -643,7 +640,7 @@
     out_got = flip(out_odd, "tensor", 1)
     mask = 1
     while got is not None:
-        cover = [out_odd, *cot_for] if mask == 1 else [kept] if mask == 2 else [dv]
+        cover = [out_odd, *tokens_for] if mask == 1 else [kept] if mask == 2 else [dv]
         after, gtotal = scan_take(after, gtotal, held(got, *cover), mask, True)
         mask *= 2
         got = scan_send(gtotal, mask)

time: 200 us -> 194 us (0.970)
  starting transfers between devices: 28.9 us -> 32.6 us
  local copies, waits for them, and re-layouts: 12.6 us -> 9 us
  other arithmetic: 20.2 us -> 16.7 us
  waiting for transfers between devices: 48.5 us -> 46.2 us
    ppermute x25, starting transfers between devices: 24.9 us -> 28.5 us  [flip(): return lax.ppermute(x, axis, [(i, i ^ mask) for i in range(n)])]
    unnamed x93 -> x89, local copies, waits for them, and re-layouts: 7.73 us -> 4.18 us
    ppermute x25, waiting for transfers between devices: 48.5 us -> 46.2 us  [flip(): return lax.ppermute(x, axis, [(i, i ^ mask) for i in range(n)])]
  transfers between devices with their start and end apart: 30 -> 30, of which waited for: 9 -> 11; matrix products, arithmetic and copies ran while one was open for 25% -> 24% of each run, Pallas kernels for 23% -> 24%
where the time goes in v2:
time: 194 us; the launch traced here: 193 us
  Pallas kernels  53 us (27%)
  waiting for transfers between devices  46.2 us (24%)
  matrix products  34 us (18%)
  starting transfers between devices  32.6 us (17%)
  other arithmetic  16.7 us (9%)
  local copies, waits for them, and re-layouts  9 us (5%)
    pallas_call x7, Pallas kernels, call(): pl.pallas_call(kernel, out_shape=out_shapes, grid_spec=pltpu.PrefetchScal...  53 us
    ppermute x25, waiting for transfers between devices, flip(): return lax.ppermute(x, axis, [(i, i ^ mask) for i in range(n)])  46.2 us
    ppermute x25, starting transfers between devices, flip(): return lax.ppermute(x, axis, [(i, i ^ mask) for i in range(n)])  28.5 us
    dot_general x6, matrix products, mm_nt(): return lax.dot_general(a, b, CONTRACT_COLS, preferred_element_type=f32)  13.1 us
    dot_general x7, matrix products, mm(): return jnp.dot(a, b, preferred_element_type=f32)  11.8 us
    dot_general x8, matrix products, mm_tn(): return lax.dot_general(a, b, CONTRACT_ROWS, preferred_element_type=f32)  9.11 us
    unnamed x89, local copies, waits for them, and re-layouts  4.18 us
  transfers between devices with their start and end apart: 30, of which 11 were waited for; matrix products, arithmetic and copies ran while one was open for 24% of the time, Pallas kernels for 24%

profile of v2, /device:TPU:0, one launch (start us, length us, event | category | flops | bytes accessed | tf_op | source)
XLA Modules:
  0.0 193.0 jit_solution(15058521323703696458)
XLA Ops:
  1.2 2.6 %collective-permute-start.1 = (bf16[256,2048]{1,0:T(8,128)(2,1)}, bf16[256,2048]{1,0:T(8,128)(2,1)}, u32[]{:S(2)}, u32[]{:S(2)}) collective-permute-start(bf16[256,2048]{1,0:T(8,128)(2,1)} %refs_1_.1), channel_id=1, source_target_pairs={{0,2},{1,3},{2,0},{3,1},{4,6},{5,7},{6,4},{7,5},{8,10},{9,11},{10,... | collective-permute-start | bytes 3145736 | tf_op jit(solution)/shard_map/ppermute | solution.py:362
  3.9 2.7 %convolution_convert_fusion.9 = bf16[256,512]{1,0:T(8,128)(2,1)} fusion(bf16[256,2048]{1,0:T(8,128)(2,1)} %refs_1_, bf16[512,2048]{1,0:T(8,128)(2,1)S(1)} %copy-done), kind=kOutput, calls=%fused_computation.26 | convolution fusion | flops 537001984 | bytes 3407872 | tf_op jit(solution)/shard_map/dot_general | solution.py:29
  9.6 2.0 %copy.28 = bf16[2048,64]{1,0:T(8,128)(2,1)} copy(bf16[2048,64]{0,1:T(8,128)(2,1)} %param.16) | data formatting | bytes 524288 | tf_op jit(solution)/shard_map/optimization_barrier | solution.py:366
  11.6 2.3 %pad_maximum_fusion = bf16[2048,640]{1,0:T(8,128)(2,1)S(1)} fusion(bf16[2048,64]{1,0:T(8,128)(2,1)} %copy.28, bf16[2048,64]{1,0:T(8,128)(2,1)} %copy.27, bf16[2048,512]{1,0:T(8,128)(2,1)} %param.17), kind=kLoop, calls=%fused_computation.4 | loop fusion | flops 7864320 | bytes 5242880 | tf_op jit(solution)/shard_map/concatenate | solution.py:514
  13.9 1.7 fusion.4.refs_1_
  15.6 2.9 %fusion.5.refs_2_ = bf16[256,640]{1,0:T(8,128)(2,1)} fusion(bf16[256,2048]{1,0:T(8,128)(2,1)} %collective-permute-done.refs_3_, bf16[2048,640]{1,0:T(8,128)(2,1)S(1)} %pad_maximum_fusion), kind=kOutput, calls=%fused_computation.28 | convolution fusion | flops 671252480 | bytes 3997696 | tf_op jit(solution)/shard_map/dot_general | solution.py:25
  19.4 2.7 %convolution_convert_fusion.8 = bf16[256,512]{1,0:T(8,128)(2,1)} fusion(bf16[256,2048]{1,0:T(8,128)(2,1)} %collective-permute-done.6.refs_3_, bf16[512,2048]{1,0:T(8,128)(2,1)S(1)} %copy-done), kind=kOutput, calls=%fused_computation.25 | convolution fusion | flops 537001984 | bytes 3407872 | tf_op jit(solution)/shard_map/dot_general | solution.py:29
  22.5 5.5 %collective-permute-done.1.refs_2_ = bf16[256,2048]{1,0:T(8,128)(2,1)} collective-permute-done((bf16[256,2048]{1,0:T(8,128)(2,1)}, bf16[256,2048]{1,0:T(8,128)(2,1)}, u32[]{:S(2)}, u32[]{:S(2)}) %collective-permute-start.1) | collective-permute-done | bytes 1048608 | tf_op jit(solution)/shard_map/ppermute | solution.py:362
  28.0 3.2 %convolution_convert_fusion.5.refs_3_ = bf16[256,640]{1,0:T(8,128)(2,1)S(1)} fusion(bf16[256,2048]{1,0:T(8,128)(2,1)} %collective-permute-done.1.refs_2_, bf16[2048,640]{1,0:T(8,128)(2,1)} %copy-done.25), kind=kOutput, calls=%fused_computation.18 | convolution fusion | flops 671252480 | bytes 3997696 | tf_op jit(solution)/shard_map/dot_general | solution.py:25
  33.9 5.6 %shard_map.197 = (bf16[1024,128]{1,0:T(8,128)(2,1)S(1)}, bf16[1024,512]{1,0:T(8,128)(2,1)S(1)}, bf16[1024,512]{1,0:T(8,128)(2,1)S(1)}, bf16[4,4,160,128]{3,2,1,0:T(8,128)(2,1)S(1)}, bf16[4,160,128]{2,1,0:T(8,128)(2,1)S(1)}) custom-call(s32[1]{0:T(128)} %bitcast.refs_0_, bf16[256,640]{1,0:T(8,128)(2,1)S(1)} %copy-done.19, bf16[256,640]{1,0:T(8,128)(2,1)S(1)} %copy-done.20, ...), custom_call_target="tpu_custom_call" | custom-call | tf_op jit(solution)/shard_map/pallas_call | solution.py:338
  42.0 7.7 %shard_map.198 = (bf16[1024,512]{1,0:T(8,128)(2,1)}, bf16[1024,1024]{1,0:T(8,128)(2,1)}, bf16[4,256,1024]{2,1,0:T(8,128)(2,1)}, bf16[4,1024,256]{2,1,0:T(8,128)(...) custom-call(s32[1]{0:T(128)} %bitcast.refs_0_, ...), custom_call_target="tpu_custom_call" | custom-call | tf_op jit(solution)/shard_map/pallas_call | solution.py:338
  51.4 4.5 %collective-permute-done.9 = bf16[4,160,128]{2,1,0:T(8,128)(2,1)S(1)} collective-permute-done((bf16[4,160,128]{2,1,0:T(8,128)(2,1)S(1)}, bf16[4,160,128]{2,1,0:T(8,128)(2,1)S(1)}, u32[]{:S(2)}, u32[]{:S(2)}) %collective-permute-start.9) | collective-permute-done | bytes 163872 | tf_op jit(solution)/shard_map/ppermute | solution.py:362
  57.1 2.9 %collective-permute-start.10 = (bf16[4,160,128]{2,1,0:T(8,128)(2,1)}, bf16[4,160,128]{2,1,0:T(8,128)(2,1)S(1)}, u32[]{:S(2)}, u32[]{:S(2)}) collective-permute-start(bf16[4,160,128]{2,1,0:T(8,128)(2,1)} %convert_add_fusion.3), channel_id=1, source_target_pairs={{0,16},{4,20},{8,24},{12,28},{16,0},{20,4},{24,8},{28,12},{1,17},{... | collective-permute-start | bytes 491528 | tf_op jit(solution)/shard_map/ppermute | solution.py:362
  60.0 2.0 %fusion.6 = bf16[1,256,512]{2,1,0:T(8,128)(2,1)S(1)} fusion(bf16[256,2048]{1,0:T(8,128)(2,1)} %collective-permute-done.11.refs_2_, bf16[512,2048]{1,0:T(8,128)(2,1)S(1)} %copy-done), kind=kOutput, calls=%fused_computation.29 | convolution fusion | flops 537001984 | bytes 3407872 | tf_op jit(solution)/shard_map/dot_general | solution.py:29
  62.1 2.1 %fusion.7 = bf16[1,256,512]{2,1,0:T(8,128)(2,1)S(1)} fusion(bf16[256,2048]{1,0:T(8,128)(2,1)} %collective-permute-done.12.refs_4_, bf16[512,2048]{1,0:T(8,128)(2,1)S(1)} %copy-done), kind=kOutput, calls=%fused_computation.30 | convolution fusion | flops 537001984 | bytes 3407872 | tf_op jit(solution)/shard_map/dot_general | solution.py:29
  64.4 7.9 %shard_map.199 = (bf16[1024,1024]{1,0:T(8,128)(2,1)}, bf16[1024,1024]{1,0:T(8,128)(2,1)}) custom-call(s32[8]{0:T(128)S(1)} %broadcast_xor_fusion.refs_0_, bf16[256,2048]{1,0:T(8,128)(2,1)S(1)} %copy-done.10, bf16[256,2048]{1,0:T(8,128)(2,1)} %collective-permute-done.11.refs_2_, bf16[256,2048]{1,0:T(8,128)(2,1)} %collective-permute-done.6.refs_3_, ...), custom_call_target="tpu_custom_call" | custom-call | tf_op jit(solution)/shard_map/pallas_call | solution.py:338
  72.5 7.2 %shard_map.200 = (bf16[2,256,512]{2,1,0:T(8,128)(2,1)S(1)}, bf16[2,256,512]{2,1,0:T(8,128)(2,1)S(1)}, bf16[1024,512]{1,0:T(8,128)(2,1)S(1)}, bf16[4,4,160,128]{3...) custom-call(s32[1]{0:T(128)} %bitcast.refs_0_, ...), custom_call_target="tpu_custom_call" | custom-call | tf_op jit(solution)/shard_map/pallas_call | solution.py:338
  82.8 7.2 %shard_map.201 = (bf16[1024,1024]{1,0:T(8,128)(2,1)}, bf16[1024,1024]{1,0:T(8,128)(2,1)}) custom-call(s32[8]{0:T(128)S(1)} %broadcast_xor_fusion.refs_0_, bf16[256,2048]{1,0:T(8,128)(2,1)S(1)} %copy-done.8, bf16[256,2048]{1,0:T(8,128)(2,1)} %collective-permute-done.1.refs_2_, bf16[256,2048]{1,0:T(8,128)(2,1)} %collective-permute-done.refs_3_, ...), custom_call_target="tpu_custom_call" | custom-call | tf_op jit(solution)/shard_map/pallas_call | solution.py:338
  91.7 2.2 %multiply_convert_fusion.1 = bf16[512,1024]{1,0:T(8,128)(2,1)} fusion(bf16[1024,512]{1,0:T(8,128)(2,1)S(1)} %pad_maximum_fusion.2, bf16[1024,1024]{1,0:T(8,128)(2,1)S(1)} %copy-done.33), kind=kOutput, calls=%fused_computation.8 | convolution fusion | flops 1074790400 | bytes 4194304 | tf_op jit(solution)/shard_map/dot_general | solution.py:33
  103.3 9.9 %shard_map.202 = (f32[1024,128]{1,0:T(8,128)S(1)}, bf16[1024,512]{1,0:T(8,128)(2,1)S(1)}) custom-call(s32[1]{0:T(128)} %bitcast.refs_0_, bf16[1024,128]{1,0:T(8,128)(2,1)S(1)} %get-tuple-element.105.refs_1_.refs_7_.refs_2_, bf16[1024,512]{1,0:T(8,128)(2,1)} %copy-done.2, bf16[1024,512]{1,0:T(8,128)(2,1)S(1)} %copy-done.15, ...), custom_call_target="tpu_custom_call" | custom-call | tf_op jit(solution)/shard_map/pallas_call | solution.py:338
  114.4 5.3 %collective-permute-done.16 = bf16[512,1024]{1,0:T(8,128)(2,1)} collective-permute-done((bf16[512,1024]{1,0:T(8,128)(2,1)}, bf16[512,1024]{1,0:T(8,128)(2,1)}, u32[]{:S(2)}, u32[]{:S(2)}) %collective-permute-start.16) | collective-permute-done | bytes 1048608 | tf_op jit(solution)/shard_map/ppermute | solution.py:362
  119.6 2.0 %add_convert_fusion.4 = bf16[512,512]{1,0:T(8,128)(2,1)} fusion(bf16[512,1024]{1,0:T(8,128)(2,1)S(1)} %multiply_convert_fusion, bf16[512,1024]{1,0:T(8,128)(2,1)} %collective-permute-done.16), kind=kLoop, calls=%fused_computation.38 | loop fusion | flops 1048576 | bytes 1572864 | tf_op jit(solution)/shard_map/convert_element_type | solution.py:467
  123.2 7.5 %shard_map.203 = (bf16[4,256,384]{2,1,0:T(8,128)(2,1)S(1)}, bf16[4,256,256]{2,1,0:T(8,128)(2,1)S(1)}, bf16[2,256,640]{2,1,0:T(8,128)(2,1)S(1)}, bf16[2,256,640]{2,1,0:T(8,128)(2,1)S(1)}, f32[8,512]{1,0:T(8,128)S(1)}) custom-call(s32[1]{0:T(128)} %bitcast.refs_0_, f32[1024,128]{1,0:T(8,128)S(1)} %get-tuple-element.113.refs_1_, ...), custom_call_target="tpu_custom_call" | custom-call | tf_op jit(solution)/shard_map/pallas_call | solution.py:338
  131.6 2.7 %multiply_convert_fusion.3 = bf16[384,1024]{1,0:T(8,128)(2,1)S(1)} fusion(bf16[1024,384]{1,0:T(8,128)(2,1)S(1)} %bitcast.68, bf16[1024,1024]{1,0:T(8,128)(2,1)} %get-tuple-element.99), kind=kOutput, calls=%fused_computation.10 | convolution fusion | flops 806092800 | bytes 3670016 | tf_op jit(solution)/shard_map/dot_general | solution.py:33
  138.4 1.8 convolution_convert_fusion.1
  144.5 1.8 add_convert_fusion
  147.3 13.0 %collective-permute-done.22 = bf16[384,1024]{1,0:T(8,128)(2,1)S(1)} collective-permute-done((bf16[384,1024]{1,0:T(8,128)(2,1)S(1)}, bf16[384,1024]{1,0:T(8,128)(2,1)S(1)}, u32[]{:S(2)}, u32[]{:S(2)}) %collective-permute-start.22) | collective-permute-done | bytes 786464 | tf_op jit(solution)/shard_map/ppermute | solution.py:362
  161.7 2.1 %collective-permute-start.25 = (bf16[264,512]{1,0:T(8,128)(2,1)S(1)}, bf16[264,512]{1,0:T(8,128)(2,1)S(1)}, u32[]{:S(2)}, u32[]{:S(2)}) collective-permute-start(bf16[264,512]{1,0:T(8,128)(2,1)S(1)} %add_convert_fusion.6), channel_id=1, source_target_pairs={{0,16},{4,20},{8,24},{12,28},{16,0},{20,4},{24,8},{28,12},{1,17},{... | collective-permute-start | bytes 811016 | tf_op jit(solution)/shard_map/ppermute | solution.py:362
  166.5 2.6 %add_convert_fusion.3 = bf16[256,2048]{1,0:T(8,128)(2,1)} fusion(bf16[256,2048]{1,0:T(8,128)(2,1)} %collective-permute-done.20, bf16[512,2048]{1,0:T(8,128)(2,1)S(1)} %copy-done.29), kind=kLoop, calls=%fused_computation.6 | loop fusion | flops 2097152 | bytes 3145728 | tf_op jit(solution)/shard_map/convert_element_type | solution.py:726
  169.1 1.9 %convert_add_fusion = bf16[512,256]{1,0:T(8,128)(2,1)} fusion(bf16[512,256]{1,0:T(8,128)(2,1)S(1)} %collective-permute-done.27, bf16[512,1024]{1,0:T(8,128)(2,1)} %copy-done.24, bf16[512,512]{1,0:T(8,128)(2,1)} %collective-permute-done.19, bf16[512,1024]{1,0:T(8,128)(2,1)} %collective-permute-done.16), kind=kLoop, calls=%fused_computation.43 | loop fusion | flops 1048576 | bytes 1310720 | tf_op jit(solution)/shard_map/add | solution.py:464
  171.1 8.1 %collective-permute-done.26 = bf16[384,512]{1,0:T(8,128)(2,1)S(1)} collective-permute-done((bf16[384,512]{1,0:T(8,128)(2,1)S(1)}, bf16[384,512]{1,0:T(8,128)(2,1)S(1)}, u32[]{:S(2)}, u32[]{:S(2)}) %collective-permute-start.26) | collective-permute-done | bytes 393248 | tf_op jit(solution)/shard_map/ppermute | solution.py:362
  181.8 6.9 %collective-permute-done.24 = bf16[256,2048]{1,0:T(8,128)(2,1)S(1)} collective-permute-done((bf16[256,2048]{1,0:T(8,128)(2,1)S(1)}, bf16[256,2048]{1,0:T(8,128)(2,1)S(1)}, u32[]{:S(2)}, u32[]{:S(2)}) %collective-permute-start.24) | collective-permute-done | bytes 1048608 | tf_op jit(solution)/shard_map/ppermute | solution.py:362
  (187 shorter events, 51.1 us)
Async XLA Ops:
  0.7 5.9 %collective-permute-start = (bf16[256,2048]{1,0:T(8,128)(2,1)}, bf16[256,2048]{1,0:T(8,128)(2,1)}, u32[]{:S(2)}, u32[]{:S(2)}) collective-permute-start(bf16[256,2048]{1,0:T(8,128)(2,1)} %refs_1_.1), channel_id=1, source_target_pairs={{0,1},{1,0},{2,3},{3,2},{4,5},{5,4},{6,7},{7,6},{8,9},{9,8},{10,11... | collective-permute-start | bytes 3145736 | tf_op jit(solution)/shard_map/ppermute | solution.py:362
  1.2 26.8 %collective-permute-start.1 = (bf16[256,2048]{1,0:T(8,128)(2,1)}, bf16[256,2048]{1,0:T(8,128)(2,1)}, u32[]{:S(2)}, u32[]{:S(2)}) collective-permute-start(bf16[256,2048]{1,0:T(8,128)(2,1)} %refs_1_.1), channel_id=1, source_target_pairs={{0,2},{1,3},{2,0},{3,1},{4,6},{5,7},{6,4},{7,5},{8,10},{9,11},{10,... | collective-permute-start | bytes 3145736 | tf_op jit(solution)/shard_map/ppermute | solution.py:362
  3.8 14.8 %collective-permute-start.6 = (bf16[256,2048]{1,0:T(8,128)(2,1)}, bf16[256,2048]{1,0:T(8,128)(2,1)}, u32[]{:S(2)}, u32[]{:S(2)}) collective-permute-start(bf16[256,2048]{1,0:T(8,128)(2,1)} %refs_1_), channel_id=1, source_target_pairs={{0,1},{1,0},{2,3},{3,2},{4,5},{5,4},{6,7},{7,6},{8,9},{9,8},{10,11... | collective-permute-start | bytes 3145736 | tf_op jit(solution)/shard_map/ppermute | solution.py:362
  6.6 15.4 %collective-permute-start.5 = (bf16[2,2048]{1,0:T(2,128)(2,1)S(1)}, bf16[2,2048]{1,0:T(2,128)(2,1)S(1)}, u32[]{:S(2)}, u32[]{:S(2)}) collective-permute-start(bf16[2,2048]{1,0:T(2,128)(2,1)S(1)} %slice.171), channel_id=1, source_target_pairs={{3,7},{7,11},{11,15},{15,19},{19,23},{23,27},{27,31}} | collective-permute-start | bytes 24584 | tf_op jit(solution)/shard_map/ppermute | solution.py:507
  7.3 14.8 %collective-permute-start.4 = (bf16[2,2048]{1,0:T(2,128)(2,1)S(1)}, bf16[2,2048]{1,0:T(2,128)(2,1)S(1)}, u32[]{:S(2)}, u32[]{:S(2)}) collective-permute-start(bf16[2,2048]{1,0:T(2,128)(2,1)S(1)} %slice.171), channel_id=1, source_target_pairs={{3,6},{7,10},{11,14},{15,18},{19,22},{23,26},{27,30}} | collective-permute-start | bytes 24584 | tf_op jit(solution)/shard_map/ppermute | solution.py:507
  8.0 14.1 %collective-permute-start.3 = (bf16[2,2048]{1,0:T(2,128)(2,1)S(1)}, bf16[2,2048]{1,0:T(2,128)(2,1)S(1)}, u32[]{:S(2)}, u32[]{:S(2)}) collective-permute-start(bf16[2,2048]{1,0:T(2,128)(2,1)S(1)} %slice.171), channel_id=1, source_target_pairs={{3,5},{7,9},{11,13},{15,17},{19,21},{23,25},{27,29}} | collective-permute-start | bytes 24584 | tf_op jit(solution)/shard_map/ppermute | solution.py:507
  18.6 3.5 %collective-permute-start.2 = (bf16[2,2048]{1,0:T(2,128)(2,1)S(1)}, bf16[2,2048]{1,0:T(2,128)(2,1)S(1)}, u32[]{:S(2)}, u32[]{:S(2)}) collective-permute-start(bf16[2,2048]{1,0:T(2,128)(2,1)S(1)} %slice.171), channel_id=1, source_target_pairs={{3,4},{7,8},{11,12},{15,16},{19,20},{23,24},{27,28}} | collective-permute-start | bytes 24584 | tf_op jit(solution)/shard_map/ppermute | solution.py:507
  28.0 4.9 %collective-permute-start.7 = (bf16[256,2048]{1,0:T(8,128)(2,1)}, bf16[256,2048]{1,0:T(8,128)(2,1)S(1)}, u32[]{:S(2)}, u32[]{:S(2)}) collective-permute-start(bf16[256,2048]{1,0:T(8,128)(2,1)} %collective-permute-done.1.refs_2_), channel_id=1, source_target_pairs={{0,1},{1,0},{2,3},{3,2},{4,5},{5,4},{6,7},{7,6},{8,9},{9,8},{10,11... | collective-permute-start | bytes 3145736 | tf_op jit(solution)/shard_map/ppermute | solution.py:362
  31.2 25.7 %collective-permute-start.11 = (bf16[256,2048]{1,0:T(8,128)(2,1)S(1)}, bf16[256,2048]{1,0:T(8,128)(2,1)}, u32[]{:S(2)}, u32[]{:S(2)}) collective-permute-start(bf16[256,2048]{1,0:T(8,128)(2,1)S(1)} %copy-done.9), channel_id=1, source_target_pairs={{0,2},{1,3},{2,0},{3,1},{4,6},{5,7},{6,4},{7,5},{8,10},{9,11},{10,... | collective-permute-start | bytes 3145736 | tf_op jit(solution)/shard_map/ppermute | solution.py:362
  40.5 21.5 %copy-start.2 = (bf16[1024,512]{1,0:T(8,128)(2,1)}, bf16[1024,512]{1,0:T(8,128)(2,1)S(1)}, u32[]{:S(2)}) copy-start(bf16[1024,512]{1,0:T(8,128)(2,1)S(1)} %get-tuple-element.80.refs_2_.refs_4_) | copy-start | bytes 3145732
  40.5 9.2 %collective-permute-start.8 = (bf16[4,160,128]{2,1,0:T(8,128)(2,1)S(1)}, bf16[4,160,128]{2,1,0:T(8,128)(2,1)S(1)}, u32[]{:S(2)}, u32[]{:S(2)}) collective-permute-start(bf16[4,160,128]{2,1,0:T(8,128)(2,1)S(1)} %get-tuple-element.85), channel_id=1, source_target_pairs={{0,4},{4,0},{8,12},{12,8},{16,20},{20,16},{24,28},{28,24},{1,5},{5... | collective-permute-start | bytes 491528 | tf_op jit(solution)/shard_map/ppermute | solution.py:362
  49.8 6.1 %collective-permute-start.9 = (bf16[4,160,128]{2,1,0:T(8,128)(2,1)S(1)}, bf16[4,160,128]{2,1,0:T(8,128)(2,1)S(1)}, u32[]{:S(2)}, u32[]{:S(2)}) collective-permute-start(bf16[4,160,128]{2,1,0:T(8,128)(2,1)S(1)} %fusion.18), channel_id=1, source_target_pairs={{0,8},{4,12},{8,0},{12,4},{16,24},{20,28},{24,16},{28,20},{1,9},{5... | collective-permute-start | bytes 491528 | tf_op jit(solution)/shard_map/ppermute | solution.py:362
  57.0 5.1 %collective-permute-start.12 = (bf16[256,2048]{1,0:T(8,128)(2,1)}, bf16[256,2048]{1,0:T(8,128)(2,1)}, u32[]{:S(2)}, u32[]{:S(2)}) collective-permute-start(bf16[256,2048]{1,0:T(8,128)(2,1)} %collective-permute-done.11.refs_2_), channel_id=1, source_target_pairs={{0,1},{1,0},{2,3},{3,2},{4,5},{5,4},{6,7},{7,6},{8,9},{9,8},{10,11... | collective-permute-start | bytes 3145736 | tf_op jit(solution)/shard_map/ppermute | solution.py:362
  57.1 15.2 %collective-permute-start.10 = (bf16[4,160,128]{2,1,0:T(8,128)(2,1)}, bf16[4,160,128]{2,1,0:T(8,128)(2,1)S(1)}, u32[]{:S(2)}, u32[]{:S(2)}) collective-permute-start(bf16[4,160,128]{2,1,0:T(8,128)(2,1)} %convert_add_fusion.3), channel_id=1, source_target_pairs={{0,16},{4,20},{8,24},{12,28},{16,0},{20,4},{24,8},{28,12},{1,17},{... | collective-permute-start | bytes 491528 | tf_op jit(solution)/shard_map/ppermute | solution.py:362
  81.0 9.1 %collective-permute-start.13 = (bf16[512,2048]{1,0:T(8,128)(2,1)S(1)}, bf16[512,2048]{1,0:T(8,128)(2,1)S(1)}, u32[]{:S(2)}, u32[]{:S(2)}) collective-permute-start(bf16[512,2048]{1,0:T(8,128)(2,1)S(1)} %convolution_convert_fusion), channel_id=1, source_target_pairs={{0,1},{1,0},{2,3},{3,2},{4,5},{5,4},{6,7},{7,6},{8,9},{9,8},{10,11... | collective-permute-start | bytes 6291464 | tf_op jit(solution)/shard_map/ppermute | solution.py:362
  81.3 8.9 %collective-permute-start.14 = (bf16[4,160,128]{2,1,0:T(8,128)(2,1)S(1)}, bf16[4,160,128]{2,1,0:T(8,128)(2,1)S(1)}, u32[]{:S(2)}, u32[]{:S(2)}) collective-permute-start(bf16[4,160,128]{2,1,0:T(8,128)(2,1)S(1)} %get-tuple-element.96), channel_id=1, source_target_pairs={{0,4},{4,0},{8,12},{12,8},{16,20},{20,16},{24,28},{28,24},{1,5},{5... | collective-permute-start | bytes 491528 | tf_op jit(solution)/shard_map/ppermute | solution.py:362
  94.0 25.7 %collective-permute-start.16 = (bf16[512,1024]{1,0:T(8,128)(2,1)}, bf16[512,1024]{1,0:T(8,128)(2,1)}, u32[]{:S(2)}, u32[]{:S(2)}) collective-permute-start(bf16[512,1024]{1,0:T(8,128)(2,1)} %multiply_convert_fusion.1), channel_id=1, source_target_pairs={{0,4},{4,0},{8,12},{12,8},{16,20},{20,16},{24,28},{28,24},{1,5},{5... | collective-permute-start | bytes 3145736 | tf_op jit(solution)/shard_map/ppermute | solution.py:362
  94.5 6.0 %collective-permute-start.15 = (bf16[4,160,128]{2,1,0:T(8,128)(2,1)S(1)}, bf16[4,160,128]{2,1,0:T(8,128)(2,1)S(1)}, u32[]{:S(2)}, u32[]{:S(2)}) collective-permute-start(bf16[4,160,128]{2,1,0:T(8,128)(2,1)S(1)} %fusion.23), channel_id=1, source_target_pairs={{0,8},{4,12},{8,0},{12,4},{16,24},{20,28},{24,16},{28,20},{1,9},{5... | collective-permute-start | bytes 491528 | tf_op jit(solution)/shard_map/ppermute | solution.py:362
  97.2 34.4 %collective-permute-start.20 = (bf16[256,2048]{1,0:T(8,128)(2,1)}, bf16[256,2048]{1,0:T(8,128)(2,1)}, u32[]{:S(2)}, u32[]{:S(2)}) collective-permute-start(bf16[256,2048]{1,0:T(8,128)(2,1)} %slice.221), channel_id=1, source_target_pairs={{0,2},{1,3},{2,0},{3,1},{4,6},{5,7},{6,4},{7,5},{8,10},{9,11},{10,... | collective-permute-start | bytes 3145736 | tf_op jit(solution)/shard_map/ppermute | solution.py:362
  99.8 23.5 %copy-start.24 = (bf16[512,1024]{1,0:T(8,128)(2,1)}, bf16[512,1024]{1,0:T(8,128)(2,1)S(1)}, u32[]{:S(2)}) copy-start(bf16[512,1024]{1,0:T(8,128)(2,1)S(1)} %multiply_convert_fusion) | copy-start | bytes 3145732
  101.2 12.0 %collective-permute-start.17 = (bf16[4,160,128]{2,1,0:T(8,128)(2,1)}, bf16[4,160,128]{2,1,0:T(8,128)(2,1)}, u32[]{:S(2)}, u32[]{:S(2)}) collective-permute-start(bf16[4,160,128]{2,1,0:T(8,128)(2,1)} %convert_add_fusion.1), channel_id=1, source_target_pairs={{0,16},{4,20},{8,24},{12,28},{16,0},{20,4},{24,8},{28,12},{1,17},{... | collective-permute-start | bytes 491528 | tf_op jit(solution)/shard_map/ppermute | solution.py:362
  102.0 21.2 %collective-permute-start.18 = (f32[8,640]{1,0:T(8,128)S(1)}, f32[8,640]{1,0:T(8,128)S(1)}, u32[]{:S(2)}, u32[]{:S(2)}) collective-permute-start(f32[8,640]{1,0:T(8,128)S(1)} %get-tuple-element.116), channel_id=1, source_target_pairs={{4,0},{8,4},{12,8},{16,12},{20,16},{24,20},{28,24},{5,1},{9,5},{13... | collective-permute-start | bytes 61448 | tf_op jit(solution)/shard_map/ppermute | solution.py:638
  121.6 13.2 %collective-permute-start.19 = (bf16[512,512]{1,0:T(8,128)(2,1)}, bf16[512,512]{1,0:T(8,128)(2,1)}, u32[]{:S(2)}, u32[]{:S(2)}) collective-permute-start(bf16[512,512]{1,0:T(8,128)(2,1)} %add_convert_fusion.4), channel_id=1, source_target_pairs={{0,8},{4,12},{8,0},{12,4},{16,24},{20,28},{24,16},{28,20},{1,9},{5... | collective-permute-start | bytes 1572872 | tf_op jit(solution)/shard_map/ppermute | solution.py:362
  140.3 4.2 %collective-permute-start.21 = (bf16[512,2048]{1,0:T(8,128)(2,1)S(1)}, bf16[512,2048]{1,0:T(8,128)(2,1)S(1)}, u32[]{:S(2)}, u32[]{:S(2)}) collective-permute-start(bf16[512,2048]{1,0:T(8,128)(2,1)S(1)} %convolution_convert_fusion.1), channel_id=1, source_target_pairs={{0,1},{1,0},{2,3},{3,2},{4,5},{5,4},{6,7},{7,6},{8,9},{9,8},{10,11... | collective-permute-start | bytes 6291464 | tf_op jit(solution)/shard_map/ppermute | solution.py:362
  140.3 20.0 %collective-permute-start.22 = (bf16[384,1024]{1,0:T(8,128)(2,1)S(1)}, bf16[384,1024]{1,0:T(8,128)(2,1)S(1)}, u32[]{:S(2)}, u32[]{:S(2)}) collective-permute-start(bf16[384,1024]{1,0:T(8,128)(2,1)S(1)} %multiply_convert_fusion.3), channel_id=1, source_target_pairs={{0,4},{4,0},{8,12},{12,8},{16,20},{20,16},{24,28},{28,24},{1,5},{5... | collective-permute-start | bytes 2359304 | tf_op jit(solution)/shard_map/ppermute | solution.py:362
  141.1 28.0 %collective-permute-start.27 = (bf16[512,256]{1,0:T(8,128)(2,1)S(1)}, bf16[512,256]{1,0:T(8,128)(2,1)S(1)}, u32[]{:S(2)}, u32[]{:S(2)}) collective-permute-start(bf16[512,256]{1,0:T(8,128)(2,1)S(1)} %add_convert_fusion.7), channel_id=1, source_target_pairs={{0,16},{4,20},{8,24},{12,28},{16,0},{20,4},{24,8},{28,12},{1,17},{... | collective-permute-start | bytes 786440 | tf_op jit(solution)/shard_map/ppermute | solution.py:362
  142.0 19.7 %collective-permute-start.23 = (bf16[264,1024]{1,0:T(8,128)(2,1)S(1)}, bf16[264,1024]{1,0:T(8,128)(2,1)S(1)}, u32[]{:S(2)}, u32[]{:S(2)}) collective-permute-start(bf16[264,1024]{1,0:T(8,128)(2,1)S(1)} %pad_maximum_fusion.4), channel_id=1, source_target_pairs={{0,8},{4,12},{8,0},{12,4},{16,24},{20,28},{24,16},{28,20},{1,9},{5... | collective-permute-start | bytes 1622024 | tf_op jit(solution)/shard_map/ppermute | solution.py:362
  161.7 19.0 %collective-permute-start.25 = (bf16[264,512]{1,0:T(8,128)(2,1)S(1)}, bf16[264,512]{1,0:T(8,128)(2,1)S(1)}, u32[]{:S(2)}, u32[]{:S(2)}) collective-permute-start(bf16[264,512]{1,0:T(8,128)(2,1)S(1)} %add_convert_fusion.6), channel_id=1, source_target_pairs={{0,16},{4,20},{8,24},{12,28},{16,0},{20,4},{24,8},{28,12},{1,17},{... | collective-permute-start | bytes 811016 | tf_op jit(solution)/shard_map/ppermute | solution.py:362
  163.8 15.4 %collective-permute-start.26 = (bf16[384,512]{1,0:T(8,128)(2,1)S(1)}, bf16[384,512]{1,0:T(8,128)(2,1)S(1)}, u32[]{:S(2)}, u32[]{:S(2)}) collective-permute-start(bf16[384,512]{1,0:T(8,128)(2,1)S(1)} %add_convert_fusion.5), channel_id=1, source_target_pairs={{0,8},{4,12},{8,0},{12,4},{16,24},{20,28},{24,16},{28,20},{1,9},{5... | collective-permute-start | bytes 1179656 | tf_op jit(solution)/shard_map/ppermute | solution.py:362
  165.1 23.6 %collective-permute-start.24 = (bf16[256,2048]{1,0:T(8,128)(2,1)S(1)}, bf16[256,2048]{1,0:T(8,128)(2,1)S(1)}, u32[]{:S(2)}, u32[]{:S(2)}) collective-permute-start(bf16[256,2048]{1,0:T(8,128)(2,1)S(1)} %slice.233), channel_id=1, source_target_pairs={{0,2},{1,3},{2,0},{3,1},{4,6},{5,7},{6,4},{7,5},{8,10},{9,11},{10,... | collective-permute-start | bytes 3145736 | tf_op jit(solution)/shard_map/ppermute | solution.py:362
  179.3 12.8 %collective-permute-start.29 = (bf16[384,256]{1,0:T(8,128)(2,1)S(1)}, bf16[384,256]{1,0:T(8,128)(2,1)S(1)}, u32[]{:S(2)}, u32[]{:S(2)}) collective-permute-start(bf16[384,256]{1,0:T(8,128)(2,1)S(1)} %add_convert_fusion.9), channel_id=1, source_target_pairs={{0,16},{4,20},{8,24},{12,28},{16,0},{20,4},{24,8},{28,12},{1,17},{... | collective-permute-start | bytes 589832 | tf_op jit(solution)/shard_map/ppermute | solution.py:362
  180.8 9.3 %collective-permute-start.28 = (bf16[264,256]{1,0:T(8,128)(2,1)S(1)}, bf16[264,256]{1,0:T(8,128)(2,1)S(1)}, u32[]{:S(2)}, u32[]{:S(2)}) collective-permute-start(bf16[264,256]{1,0:T(8,128)(2,1)S(1)} %add_convert_fusion.10), channel_id=1, source_target_pairs={{0,4},{4,0},{8,12},{12,8},{16,20},{20,16},{24,28},{28,24},{1,5},{5... | collective-permute-start | bytes 405512 | tf_op jit(solution)/shard_map/ppermute | solution.py:362
  (42 other events, 212.7 us)

commit v3 on v2

--- a/solution.py
+++ b/solution.py
@@ -469,6 +469,29 @@
         self.at += 1
         self.kept = [t[:, :half] for t in self.kept]
         return send
+
+
+def product_kernel(_, left_ref, right_ref, *refs):
+    total = mm_nt(left_ref[...], right_ref[...])
+    if len(refs) > 1:
+        total += refs[0][...].astype(f32)
+    refs[-1][...] = total.astype(bf16)
+
+
+def product_nt(left, right, place, *more):
+    height, width = left.shape[0], right.shape[0]
+    tile = min(width, 1024)
+    columns = pl.BlockSpec((height, tile), lambda i, p: (0, i))
+    return call(
+        product_kernel,
+        place,
+        [left, right, *more],
+        [whole(left.shape), pl.BlockSpec((tile, right.shape[1]), lambda i, p: (i, 0))]
+        + [columns] * len(more),
+        [jax.ShapeDtypeStruct((height, width), bf16)],
+        [columns],
+        [], width // tile, 0,
+    )[0]
 
 
 def masks_of(first):
@@ -709,7 +732,7 @@
     second = Halve(True, late.reshape(length, cw - cut), tokens_for, grad_scale, sums)
     done = out_halve.step(first.first) if steps > 2 else first.first
     second.begin(done)
-    in_odd = mm_nt(held(cols_odd, second.first).reshape(-1, cw), weights).astype(bf16)
+    in_odd = product_nt(held(cols_odd, second.first).reshape(-1, cw), weights, place)
     in_got = held(flip(in_odd, "tensor", 1), in_odd)
     in_rows = mm_nt(cols_even.reshape(-1, cw), weights) + in_got.astype(f32)
     in_rows = in_rows.astype(bf16)
@@ -725,10 +748,10 @@
         layer_out += got.astype(f32)
     done = layer_out = layer_out.astype(bf16)
     for k in range(1, steps):
+        done = first.step(done) if k < steps - 1 else done
+        done = second.step(done)
         if k < steps - 1 or steps == 2:
             done = out_halve.step(done)
-        done = first.step(done) if k < steps - 1 else done
-        done = second.step(done)
         if k == steps - 2 or steps == 2:
             grad_in = in_rows[:rows].astype(f32)
             for got in in_flips:

time: 194 us -> 194 us (level)
  other arithmetic: 16.7 us -> 13.8 us
  Pallas kernels: 53 us -> 55.3 us
  starting transfers between devices: 32.6 us -> 30.6 us
  waiting for transfers between devices: 46.2 us -> 48.2 us
    pallas_call x7 -> x8, Pallas kernels: 53 us -> 55.3 us  [call(): pl.pallas_call(kernel, out_shape=out_shapes, grid_spec=pltpu.PrefetchScal...]
    ppermute x25, waiting for transfers between devices: 46.2 us -> 48.2 us  [flip(): return lax.ppermute(x, axis, [(i, i ^ mask) for i in range(n)])]
    ppermute x25, starting transfers between devices: 28.5 us -> 26.6 us  [flip(): return lax.ppermute(x, axis, [(i, i ^ mask) for i in range(n)])]
    dot_general x6 -> x5, matrix products: 13.1 us -> 11.3 us  [mm_nt(): return lax.dot_general(a, b, CONTRACT_COLS, preferred_element_type=f32)]
    unnamed x89 -> x99, local copies, waits for them, and re-layouts: 4.18 us -> 5.05 us
  transfers between devices with their start and end apart: 30 -> 30, of which waited for: 11 -> 8; matrix products, arithmetic and copies ran while one was open for 24% -> 23% of each run, Pallas kernels for 24% -> 24%
where the time goes in v3:
time: 194 us; the launch traced here: 193 us
  Pallas kernels  55.3 us (29%)
  waiting for transfers between devices  48.2 us (25%)
  matrix products  33.2 us (17%)
  starting transfers between devices  30.6 us (16%)
  other arithmetic  13.8 us (7%)
  local copies, waits for them, and re-layouts  9.87 us (5%)
    pallas_call x8, Pallas kernels, call(): pl.pallas_call(kernel, out_shape=out_shapes, grid_spec=pltpu.PrefetchScal...  55.3 us
    ppermute x25, waiting for transfers between devices, flip(): return lax.ppermute(x, axis, [(i, i ^ mask) for i in range(n)])  48.2 us
    ppermute x25, starting transfers between devices, flip(): return lax.ppermute(x, axis, [(i, i ^ mask) for i in range(n)])  26.6 us
    dot_general x7, matrix products, mm(): return jnp.dot(a, b, preferred_element_type=f32)  11.8 us
    dot_general x5, matrix products, mm_nt(): return lax.dot_general(a, b, CONTRACT_COLS, preferred_element_type=f32)  11.3 us
    dot_general x8, matrix products, mm_tn(): return lax.dot_general(a, b, CONTRACT_ROWS, preferred_element_type=f32)  10.2 us
    unnamed x99, local copies, waits for them, and re-layouts  5.05 us
  transfers between devices with their start and end apart: 30, of which 8 were waited for; matrix products, arithmetic and copies ran while one was open for 23% of the time, Pallas kernels for 24%

profile of v3, /device:TPU:0, one launch (start us, length us, event | category | flops | bytes accessed | tf_op | source)
XLA Modules:
  0.0 192.7 jit_solution(9087825243508445984)
XLA Ops:
  1.2 2.6 %collective-permute-start.1 = (bf16[256,2048]{1,0:T(8,128)(2,1)}, bf16[256,2048]{1,0:T(8,128)(2,1)}, u32[]{:S(2)}, u32[]{:S(2)}) collective-permute-start(bf16[256,2048]{1,0:T(8,128)(2,1)} %refs_1_.1), channel_id=1, source_target_pairs={{0,2},{1,3},{2,0},{3,1},{4,6},{5,7},{6,4},{7,5},{8,10},{9,11},{10,... | collective-permute-start | bytes 3145736 | tf_op jit(solution)/shard_map/ppermute | solution.py:362
  3.9 2.7 %convolution_convert_fusion.8 = bf16[256,512]{1,0:T(8,128)(2,1)} fusion(bf16[256,2048]{1,0:T(8,128)(2,1)} %refs_1_, bf16[512,2048]{1,0:T(8,128)(2,1)S(1)} %copy-done), kind=kOutput, calls=%fused_computation.25 | convolution fusion | flops 537001984 | bytes 3407872 | tf_op jit(solution)/shard_map/dot_general | solution.py:29
  9.6 2.0 %copy.28 = bf16[2048,64]{1,0:T(8,128)(2,1)} copy(bf16[2048,64]{0,1:T(8,128)(2,1)} %param.16) | data formatting | bytes 524288 | tf_op jit(solution)/shard_map/optimization_barrier | solution.py:366
  11.6 2.3 %pad_maximum_fusion.right_ref = bf16[2048,640]{1,0:T(8,128)(2,1)S(1)} fusion(bf16[2048,64]{1,0:T(8,128)(2,1)} %copy.28, bf16[2048,64]{1,0:T(8,128)(2,1)} %copy.27, bf16[2048,512]{1,0:T(8,128)(2,1)} %param.17), kind=kLoop, calls=%fused_computation.3 | loop fusion | flops 7864320 | bytes 5242880 | tf_op jit(solution)/shard_map/concatenate | solution.py:537
  13.9 1.7 fusion.4.refs_1_
  15.6 2.9 %fusion.5.refs_2_ = bf16[256,640]{1,0:T(8,128)(2,1)} fusion(bf16[256,2048]{1,0:T(8,128)(2,1)} %collective-permute-done.refs_3_, bf16[2048,640]{1,0:T(8,128)(2,1)S(1)} %pad_maximum_fusion.right_ref), kind=kOutput, calls=%fused_computation.27 | convolution fusion | flops 671252480 | bytes 3997696 | tf_op jit(solution)/shard_map/dot_general | solution.py:25
  19.4 2.7 %convolution_convert_fusion.7 = bf16[256,512]{1,0:T(8,128)(2,1)} fusion(bf16[256,2048]{1,0:T(8,128)(2,1)} %collective-permute-done.6.refs_3_, bf16[512,2048]{1,0:T(8,128)(2,1)S(1)} %copy-done), kind=kOutput, calls=%fused_computation.24 | convolution fusion | flops 537001984 | bytes 3407872 | tf_op jit(solution)/shard_map/dot_general | solution.py:29
  22.5 5.5 %collective-permute-done.1.refs_2_ = bf16[256,2048]{1,0:T(8,128)(2,1)} collective-permute-done((bf16[256,2048]{1,0:T(8,128)(2,1)}, bf16[256,2048]{1,0:T(8,128)(2,1)}, u32[]{:S(2)}, u32[]{:S(2)}) %collective-permute-start.1) | collective-permute-done | bytes 1048608 | tf_op jit(solution)/shard_map/ppermute | solution.py:362
  28.0 3.2 %convolution_convert_fusion.4.refs_3_ = bf16[256,640]{1,0:T(8,128)(2,1)S(1)} fusion(bf16[256,2048]{1,0:T(8,128)(2,1)} %collective-permute-done.1.refs_2_, bf16[2048,640]{1,0:T(8,128)(2,1)} %copy-done.2), kind=kOutput, calls=%fused_computation.17 | convolution fusion | flops 671252480 | bytes 3997696 | tf_op jit(solution)/shard_map/dot_general | solution.py:25
  33.9 5.6 %shard_map.197 = (bf16[1024,128]{1,0:T(8,128)(2,1)S(1)}, bf16[1024,512]{1,0:T(8,128)(2,1)S(1)}, bf16[1024,512]{1,0:T(8,128)(2,1)S(1)}, bf16[4,4,160,128]{3,2,1,0:T(8,128)(2,1)S(1)}, bf16[4,160,128]{2,1,0:T(8,128)(2,1)S(1)}) custom-call(s32[1]{0:T(128)} %bitcast.refs_0_._, bf16[256,640]{1,0:T(8,128)(2,1)S(1)} %copy-done.26, bf16[256,640]{1,0:T(8,128)(2,1)S(1)} %copy-done.27, ...), custom_call_target="tpu_custom_call" | custom-call | tf_op jit(solution)/shard_map/pallas_call | solution.py:338
  41.1 7.7 %shard_map.198 = (bf16[1024,512]{1,0:T(8,128)(2,1)}, bf16[1024,1024]{1,0:T(8,128)(2,1)}, bf16[4,256,1024]{2,1,0:T(8,128)(2,1)}, bf16[4,1024,256]{2,1,0:T(8,128)(...) custom-call(s32[1]{0:T(128)} %bitcast.refs_0_._, ...), custom_call_target="tpu_custom_call" | custom-call | tf_op jit(solution)/shard_map/pallas_call | solution.py:338
  50.5 4.5 %collective-permute-done.9 = bf16[4,160,128]{2,1,0:T(8,128)(2,1)S(1)} collective-permute-done((bf16[4,160,128]{2,1,0:T(8,128)(2,1)S(1)}, bf16[4,160,128]{2,1,0:T(8,128)(2,1)S(1)}, u32[]{:S(2)}, u32[]{:S(2)}) %collective-permute-start.9) | collective-permute-done | bytes 163872 | tf_op jit(solution)/shard_map/ppermute | solution.py:362
  57.1 2.9 %collective-permute-start.10 = (bf16[4,160,128]{2,1,0:T(8,128)(2,1)}, bf16[4,160,128]{2,1,0:T(8,128)(2,1)S(1)}, u32[]{:S(2)}, u32[]{:S(2)}) collective-permute-start(bf16[4,160,128]{2,1,0:T(8,128)(2,1)} %convert_add_fusion.3), channel_id=1, source_target_pairs={{0,16},{4,20},{8,24},{12,28},{16,0},{20,4},{24,8},{28,12},{1,17},{... | collective-permute-start | bytes 491528 | tf_op jit(solution)/shard_map/ppermute | solution.py:362
  60.0 2.0 %fusion.6 = bf16[1,256,512]{2,1,0:T(8,128)(2,1)S(1)} fusion(bf16[256,2048]{1,0:T(8,128)(2,1)} %collective-permute-done.11.refs_2_, bf16[512,2048]{1,0:T(8,128)(2,1)S(1)} %copy-done), kind=kOutput, calls=%fused_computation.28 | convolution fusion | flops 537001984 | bytes 3407872 | tf_op jit(solution)/shard_map/dot_general | solution.py:29
  62.1 2.1 %fusion.7 = bf16[1,256,512]{2,1,0:T(8,128)(2,1)S(1)} fusion(bf16[256,2048]{1,0:T(8,128)(2,1)} %collective-permute-done.12.refs_4_, bf16[512,2048]{1,0:T(8,128)(2,1)S(1)} %copy-done), kind=kOutput, calls=%fused_computation.29 | convolution fusion | flops 537001984 | bytes 3407872 | tf_op jit(solution)/shard_map/dot_general | solution.py:29
  64.4 7.9 %shard_map.199 = (bf16[1024,1024]{1,0:T(8,128)(2,1)}, bf16[1024,1024]{1,0:T(8,128)(2,1)}) custom-call(s32[8]{0:T(128)S(1)} %broadcast_xor_fusion.refs_0_, bf16[256,2048]{1,0:T(8,128)(2,1)S(1)} %copy-done.13, bf16[256,2048]{1,0:T(8,128)(2,1)} %collective-permute-done.11.refs_2_, bf16[256,2048]{1,0:T(8,128)(2,1)} %collective-permute-done.6.refs_3_, ...), custom_call_target="tpu_custom_call" | custom-call | tf_op jit(solution)/shard_map/pallas_call | solution.py:338
  72.5 7.2 %shard_map.200 = (bf16[2,256,512]{2,1,0:T(8,128)(2,1)S(1)}, bf16[2,256,512]{2,1,0:T(8,128)(2,1)S(1)}, bf16[1024,512]{1,0:T(8,128)(2,1)S(1)}, bf16[4,4,160,128]{3...) custom-call(s32[1]{0:T(128)} %bitcast.refs_0_._, ...), custom_call_target="tpu_custom_call" | custom-call | tf_op jit(solution)/shard_map/pallas_call | solution.py:338
  82.9 7.3 %shard_map.201 = (bf16[1024,1024]{1,0:T(8,128)(2,1)}, bf16[1024,1024]{1,0:T(8,128)(2,1)}) custom-call(s32[8]{0:T(128)S(1)} %broadcast_xor_fusion.refs_0_, bf16[256,2048]{1,0:T(8,128)(2,1)S(1)} %copy-done.11, bf16[256,2048]{1,0:T(8,128)(2,1)} %collective-permute-done.1.refs_2_, bf16[256,2048]{1,0:T(8,128)(2,1)} %collective-permute-done.refs_3_, ...), custom_call_target="tpu_custom_call" | custom-call | tf_op jit(solution)/shard_map/pallas_call | solution.py:338
  91.8 2.3 %multiply_convert_fusion.1 = bf16[512,1024]{1,0:T(8,128)(2,1)} fusion(bf16[1024,512]{1,0:T(8,128)(2,1)S(1)} %pad_maximum_fusion.2, bf16[1024,1024]{1,0:T(8,128)(2,1)S(1)} %copy-done.40), kind=kOutput, calls=%fused_computation.7 | convolution fusion | flops 1074790400 | bytes 4194304 | tf_op jit(solution)/shard_map/dot_general | solution.py:33
  98.7 2.3 %multiply_convert_fusion = bf16[512,1024]{1,0:T(8,128)(2,1)} fusion(bf16[1024,512]{1,0:T(8,128)(2,1)S(1)} %pad_maximum_fusion.2, bf16[1024,1024]{1,0:T(8,128)(2,1)S(1)} %copy-done.39), kind=kOutput, calls=%fused_computation.6 | convolution fusion | flops 1074790400 | bytes 4194304 | tf_op jit(solution)/shard_map/dot_general | solution.py:33
  103.3 10.1 %shard_map.202 = (f32[1024,128]{1,0:T(8,128)S(1)}, bf16[1024,512]{1,0:T(8,128)(2,1)S(1)}) custom-call(s32[1]{0:T(128)} %bitcast.refs_0_._, bf16[1024,128]{1,0:T(8,128)(2,1)S(1)} %get-tuple-element.105.refs_1_.refs_7_.refs_2_, bf16[1024,512]{1,0:T(8,128)(2,1)} %copy-done.5, bf16[1024,512]{1,0:T(8,128)(2,1)S(1)} %copy-done.18, ...), custom_call_target="tpu_custom_call" | custom-call | tf_op jit(solution)/shard_map/pallas_call | solution.py:338
  113.5 6.3 %collective-permute-done.16 = bf16[512,1024]{1,0:T(8,128)(2,1)} collective-permute-done((bf16[512,1024]{1,0:T(8,128)(2,1)}, bf16[512,1024]{1,0:T(8,128)(2,1)}, u32[]{:S(2)}, u32[]{:S(2)}) %collective-permute-start.16) | collective-permute-done | bytes 1048608 | tf_op jit(solution)/shard_map/ppermute | solution.py:362
  122.7 7.4 %shard_map.203 = (bf16[4,256,384]{2,1,0:T(8,128)(2,1)S(1)}, bf16[4,256,256]{2,1,0:T(8,128)(2,1)S(1)}, bf16[2,256,640]{2,1,0:T(8,128)(2,1)S(1)}, bf16[2,256,640]{2,1,0:T(8,128)(2,1)S(1)}, f32[8,512]{1,0:T(8,128)S(1)}) custom-call(s32[1]{0:T(128)} %bitcast.refs_0_._, f32[1024,128]{1,0:T(8,128)S(1)} %get-tuple-element.113.refs_1_, ...), custom_call_target="tpu_custom_call" | custom-call | tf_op jit(solution)/shard_map/pallas_call | solution.py:338
  132.7 2.7 %multiply_convert_fusion.3 = bf16[384,1024]{1,0:T(8,128)(2,1)S(1)} fusion(bf16[1024,384]{1,0:T(8,128)(2,1)S(1)} %bitcast.66, bf16[1024,1024]{1,0:T(8,128)(2,1)} %get-tuple-element.99), kind=kOutput, calls=%fused_computation.9 | convolution fusion | flops 806092800 | bytes 3670016 | tf_op jit(solution)/shard_map/dot_general | solution.py:33
  139.0 2.2 %shard_map.204 = bf16[512,2048]{1,0:T(8,128)(2,1)S(1)} custom-call(s32[1]{0:T(128)} %bitcast.refs_0_._, bf16[512,640]{1,0:T(8,128)(2,1)S(1)} %bitcast.68, bf16[2048,640]{1,0:T(8,128)(2,1)S(1)} %copy-done.4), custom_call_target="tpu_custom_call" | custom-call | tf_op jit(solution)/shard_map/pallas_call | solution.py:338
  143.4 2.0 %collective-permute-done.21 = bf16[512,2048]{1,0:T(8,128)(2,1)S(1)} collective-permute-done((bf16[512,2048]{1,0:T(8,128)(2,1)S(1)}, bf16[512,2048]{1,0:T(8,128)(2,1)S(1)}, u32[]{:S(2)}, u32[]{:S(2)}) %collective-permute-start.21) | collective-permute-done | bytes 2097184 | tf_op jit(solution)/shard_map/ppermute | solution.py:362
  145.4 1.8 add_convert_fusion
  148.3 13.0 %collective-permute-done.22 = bf16[384,1024]{1,0:T(8,128)(2,1)S(1)} collective-permute-done((bf16[384,1024]{1,0:T(8,128)(2,1)S(1)}, bf16[384,1024]{1,0:T(8,128)(2,1)S(1)}, u32[]{:S(2)}, u32[]{:S(2)}) %collective-permute-start.22) | collective-permute-done | bytes 786464 | tf_op jit(solution)/shard_map/ppermute | solution.py:362
  166.2 2.6 %add_convert_fusion.3 = bf16[256,2048]{1,0:T(8,128)(2,1)} fusion(bf16[256,2048]{1,0:T(8,128)(2,1)} %collective-permute-done.20, bf16[512,2048]{1,0:T(8,128)(2,1)S(1)} %copy-done.36), kind=kLoop, calls=%fused_computation.5 | loop fusion | flops 2097152 | bytes 3145728 | tf_op jit(solution)/shard_map/convert_element_type | solution.py:749
  168.8 10.8 %collective-permute-done.27 = bf16[384,512]{1,0:T(8,128)(2,1)S(1)} collective-permute-done((bf16[384,512]{1,0:T(8,128)(2,1)S(1)}, bf16[384,512]{1,0:T(8,128)(2,1)S(1)}, u32[]{:S(2)}, u32[]{:S(2)}) %collective-permute-start.27) | collective-permute-done | bytes 393248 | tf_op jit(solution)/shard_map/ppermute | solution.py:362
  181.7 1.8 convert_add_fusion
  183.5 4.9 %collective-permute-done.24 = bf16[256,2048]{1,0:T(8,128)(2,1)S(1)} collective-permute-done((bf16[256,2048]{1,0:T(8,128)(2,1)S(1)}, bf16[256,2048]{1,0:T(8,128)(2,1)S(1)}, u32[]{:S(2)}, u32[]{:S(2)}) %collective-permute-start.24) | collective-permute-done | bytes 1048608 | tf_op jit(solution)/shard_map/ppermute | solution.py:362
  (197 shorter events, 48.3 us)
Async XLA Ops:
  0.7 5.9 %collective-permute-start = (bf16[256,2048]{1,0:T(8,128)(2,1)}, bf16[256,2048]{1,0:T(8,128)(2,1)}, u32[]{:S(2)}, u32[]{:S(2)}) collective-permute-start(bf16[256,2048]{1,0:T(8,128)(2,1)} %refs_1_.1), channel_id=1, source_target_pairs={{0,1},{1,0},{2,3},{3,2},{4,5},{5,4},{6,7},{7,6},{8,9},{9,8},{10,11... | collective-permute-start | bytes 3145736 | tf_op jit(solution)/shard_map/ppermute | solution.py:362
  1.2 26.8 %collective-permute-start.1 = (bf16[256,2048]{1,0:T(8,128)(2,1)}, bf16[256,2048]{1,0:T(8,128)(2,1)}, u32[]{:S(2)}, u32[]{:S(2)}) collective-permute-start(bf16[256,2048]{1,0:T(8,128)(2,1)} %refs_1_.1), channel_id=1, source_target_pairs={{0,2},{1,3},{2,0},{3,1},{4,6},{5,7},{6,4},{7,5},{8,10},{9,11},{10,... | collective-permute-start | bytes 3145736 | tf_op jit(solution)/shard_map/ppermute | solution.py:362
  3.8 14.8 %collective-permute-start.6 = (bf16[256,2048]{1,0:T(8,128)(2,1)}, bf16[256,2048]{1,0:T(8,128)(2,1)}, u32[]{:S(2)}, u32[]{:S(2)}) collective-permute-start(bf16[256,2048]{1,0:T(8,128)(2,1)} %refs_1_), channel_id=1, source_target_pairs={{0,1},{1,0},{2,3},{3,2},{4,5},{5,4},{6,7},{7,6},{8,9},{9,8},{10,11... | collective-permute-start | bytes 3145736 | tf_op jit(solution)/shard_map/ppermute | solution.py:362
  6.6 15.4 %collective-permute-start.5 = (bf16[2,2048]{1,0:T(2,128)(2,1)S(1)}, bf16[2,2048]{1,0:T(2,128)(2,1)S(1)}, u32[]{:S(2)}, u32[]{:S(2)}) collective-permute-start(bf16[2,2048]{1,0:T(2,128)(2,1)S(1)} %slice.171), channel_id=1, source_target_pairs={{3,7},{7,11},{11,15},{15,19},{19,23},{23,27},{27,31}} | collective-permute-start | bytes 24584 | tf_op jit(solution)/shard_map/ppermute | solution.py:530
  7.3 14.7 %collective-permute-start.4 = (bf16[2,2048]{1,0:T(2,128)(2,1)S(1)}, bf16[2,2048]{1,0:T(2,128)(2,1)S(1)}, u32[]{:S(2)}, u32[]{:S(2)}) collective-permute-start(bf16[2,2048]{1,0:T(2,128)(2,1)S(1)} %slice.171), channel_id=1, source_target_pairs={{3,6},{7,10},{11,14},{15,18},{19,22},{23,26},{27,30}} | collective-permute-start | bytes 24584 | tf_op jit(solution)/shard_map/ppermute | solution.py:530
  8.0 14.1 %collective-permute-start.3 = (bf16[2,2048]{1,0:T(2,128)(2,1)S(1)}, bf16[2,2048]{1,0:T(2,128)(2,1)S(1)}, u32[]{:S(2)}, u32[]{:S(2)}) collective-permute-start(bf16[2,2048]{1,0:T(2,128)(2,1)S(1)} %slice.171), channel_id=1, source_target_pairs={{3,5},{7,9},{11,13},{15,17},{19,21},{23,25},{27,29}} | collective-permute-start | bytes 24584 | tf_op jit(solution)/shard_map/ppermute | solution.py:530
  18.6 3.5 %collective-permute-start.2 = (bf16[2,2048]{1,0:T(2,128)(2,1)S(1)}, bf16[2,2048]{1,0:T(2,128)(2,1)S(1)}, u32[]{:S(2)}, u32[]{:S(2)}) collective-permute-start(bf16[2,2048]{1,0:T(2,128)(2,1)S(1)} %slice.171), channel_id=1, source_target_pairs={{3,4},{7,8},{11,12},{15,16},{19,20},{23,24},{27,28}} | collective-permute-start | bytes 24584 | tf_op jit(solution)/shard_map/ppermute | solution.py:530
  28.0 4.9 %collective-permute-start.7 = (bf16[256,2048]{1,0:T(8,128)(2,1)}, bf16[256,2048]{1,0:T(8,128)(2,1)S(1)}, u32[]{:S(2)}, u32[]{:S(2)}) collective-permute-start(bf16[256,2048]{1,0:T(8,128)(2,1)} %collective-permute-done.1.refs_2_), channel_id=1, source_target_pairs={{0,1},{1,0},{2,3},{3,2},{4,5},{5,4},{6,7},{7,6},{8,9},{9,8},{10,11... | collective-permute-start | bytes 3145736 | tf_op jit(solution)/shard_map/ppermute | solution.py:362
  31.2 25.7 %collective-permute-start.11 = (bf16[256,2048]{1,0:T(8,128)(2,1)S(1)}, bf16[256,2048]{1,0:T(8,128)(2,1)}, u32[]{:S(2)}, u32[]{:S(2)}) collective-permute-start(bf16[256,2048]{1,0:T(8,128)(2,1)S(1)} %copy-done.12), channel_id=1, source_target_pairs={{0,2},{1,3},{2,0},{3,1},{4,6},{5,7},{6,4},{7,5},{8,10},{9,11},{10,... | collective-permute-start | bytes 3145736 | tf_op jit(solution)/shard_map/ppermute | solution.py:362
  39.5 22.5 %copy-start.5 = (bf16[1024,512]{1,0:T(8,128)(2,1)}, bf16[1024,512]{1,0:T(8,128)(2,1)S(1)}, u32[]{:S(2)}) copy-start(bf16[1024,512]{1,0:T(8,128)(2,1)S(1)} %get-tuple-element.80.refs_2_.refs_4_) | copy-start | bytes 3145732
  39.5 9.3 %collective-permute-start.8 = (bf16[4,160,128]{2,1,0:T(8,128)(2,1)S(1)}, bf16[4,160,128]{2,1,0:T(8,128)(2,1)S(1)}, u32[]{:S(2)}, u32[]{:S(2)}) collective-permute-start(bf16[4,160,128]{2,1,0:T(8,128)(2,1)S(1)} %get-tuple-element.85), channel_id=1, source_target_pairs={{0,4},{4,0},{8,12},{12,8},{16,20},{20,16},{24,28},{28,24},{1,5},{5... | collective-permute-start | bytes 491528 | tf_op jit(solution)/shard_map/ppermute | solution.py:362
  48.9 6.1 %collective-permute-start.9 = (bf16[4,160,128]{2,1,0:T(8,128)(2,1)S(1)}, bf16[4,160,128]{2,1,0:T(8,128)(2,1)S(1)}, u32[]{:S(2)}, u32[]{:S(2)}) collective-permute-start(bf16[4,160,128]{2,1,0:T(8,128)(2,1)S(1)} %fusion.18), channel_id=1, source_target_pairs={{0,8},{4,12},{8,0},{12,4},{16,24},{20,28},{24,16},{28,20},{1,9},{5... | collective-permute-start | bytes 491528 | tf_op jit(solution)/shard_map/ppermute | solution.py:362
  57.0 5.1 %collective-permute-start.12 = (bf16[256,2048]{1,0:T(8,128)(2,1)}, bf16[256,2048]{1,0:T(8,128)(2,1)}, u32[]{:S(2)}, u32[]{:S(2)}) collective-permute-start(bf16[256,2048]{1,0:T(8,128)(2,1)} %collective-permute-done.11.refs_2_), channel_id=1, source_target_pairs={{0,1},{1,0},{2,3},{3,2},{4,5},{5,4},{6,7},{7,6},{8,9},{9,8},{10,11... | collective-permute-start | bytes 3145736 | tf_op jit(solution)/shard_map/ppermute | solution.py:362
  57.1 15.2 %collective-permute-start.10 = (bf16[4,160,128]{2,1,0:T(8,128)(2,1)}, bf16[4,160,128]{2,1,0:T(8,128)(2,1)S(1)}, u32[]{:S(2)}, u32[]{:S(2)}) collective-permute-start(bf16[4,160,128]{2,1,0:T(8,128)(2,1)} %convert_add_fusion.3), channel_id=1, source_target_pairs={{0,16},{4,20},{8,24},{12,28},{16,0},{20,4},{24,8},{28,12},{1,17},{... | collective-permute-start | bytes 491528 | tf_op jit(solution)/shard_map/ppermute | solution.py:362
  81.1 9.1 %collective-permute-start.13 = (bf16[512,2048]{1,0:T(8,128)(2,1)S(1)}, bf16[512,2048]{1,0:T(8,128)(2,1)S(1)}, u32[]{:S(2)}, u32[]{:S(2)}) collective-permute-start(bf16[512,2048]{1,0:T(8,128)(2,1)S(1)} %convolution_convert_fusion), channel_id=1, source_target_pairs={{0,1},{1,0},{2,3},{3,2},{4,5},{5,4},{6,7},{7,6},{8,9},{9,8},{10,11... | collective-permute-start | bytes 6291464 | tf_op jit(solution)/shard_map/ppermute | solution.py:362
  81.3 8.9 %collective-permute-start.14 = (bf16[4,160,128]{2,1,0:T(8,128)(2,1)S(1)}, bf16[4,160,128]{2,1,0:T(8,128)(2,1)S(1)}, u32[]{:S(2)}, u32[]{:S(2)}) collective-permute-start(bf16[4,160,128]{2,1,0:T(8,128)(2,1)S(1)} %get-tuple-element.96), channel_id=1, source_target_pairs={{0,4},{4,0},{8,12},{12,8},{16,20},{20,16},{24,28},{28,24},{1,5},{5... | collective-permute-start | bytes 491528 | tf_op jit(solution)/shard_map/ppermute | solution.py:362
  94.1 25.7 %collective-permute-start.16 = (bf16[512,1024]{1,0:T(8,128)(2,1)}, bf16[512,1024]{1,0:T(8,128)(2,1)}, u32[]{:S(2)}, u32[]{:S(2)}) collective-permute-start(bf16[512,1024]{1,0:T(8,128)(2,1)} %multiply_convert_fusion.1), channel_id=1, source_target_pairs={{0,4},{4,0},{8,12},{12,8},{16,20},{20,16},{24,28},{28,24},{1,5},{5... | collective-permute-start | bytes 3145736 | tf_op jit(solution)/shard_map/ppermute | solution.py:362
  94.7 6.3 %collective-permute-start.15 = (bf16[4,160,128]{2,1,0:T(8,128)(2,1)S(1)}, bf16[4,160,128]{2,1,0:T(8,128)(2,1)S(1)}, u32[]{:S(2)}, u32[]{:S(2)}) collective-permute-start(bf16[4,160,128]{2,1,0:T(8,128)(2,1)S(1)} %fusion.23), channel_id=1, source_target_pairs={{0,8},{4,12},{8,0},{12,4},{16,24},{20,28},{24,16},{28,20},{1,9},{5... | collective-permute-start | bytes 491528 | tf_op jit(solution)/shard_map/ppermute | solution.py:362
  97.4 35.2 %collective-permute-start.20 = (bf16[256,2048]{1,0:T(8,128)(2,1)}, bf16[256,2048]{1,0:T(8,128)(2,1)}, u32[]{:S(2)}, u32[]{:S(2)}) collective-permute-start(bf16[256,2048]{1,0:T(8,128)(2,1)} %slice.221), channel_id=1, source_target_pairs={{0,2},{1,3},{2,0},{3,1},{4,6},{5,7},{6,4},{7,5},{8,10},{9,11},{10,... | collective-permute-start | bytes 3145736 | tf_op jit(solution)/shard_map/ppermute | solution.py:362
  101.1 12.3 %collective-permute-start.17 = (bf16[4,160,128]{2,1,0:T(8,128)(2,1)S(1)}, bf16[4,160,128]{2,1,0:T(8,128)(2,1)S(1)}, u32[]{:S(2)}, u32[]{:S(2)}) collective-permute-start(bf16[4,160,128]{2,1,0:T(8,128)(2,1)S(1)} %convert_add_fusion.1), channel_id=1, source_target_pairs={{0,16},{4,20},{8,24},{12,28},{16,0},{20,4},{24,8},{28,12},{1,17},{... | collective-permute-start | bytes 491528 | tf_op jit(solution)/shard_map/ppermute | solution.py:362
  101.9 20.7 %collective-permute-start.18 = (f32[8,640]{1,0:T(8,128)S(1)}, f32[8,640]{1,0:T(8,128)S(1)}, u32[]{:S(2)}, u32[]{:S(2)}) collective-permute-start(f32[8,640]{1,0:T(8,128)S(1)} %get-tuple-element.116), channel_id=1, source_target_pairs={{4,0},{8,4},{12,8},{16,12},{20,16},{24,20},{28,24},{5,1},{9,5},{13... | collective-permute-start | bytes 61448 | tf_op jit(solution)/shard_map/ppermute | solution.py:661
  103.2 19.4 %copy-start.23 = (bf16[4,4,160,128]{3,2,1,0:T(8,128)(2,1)S(1)}, bf16[4,4,160,128]{3,2,1,0:T(8,128)(2,1)}, u32[]{:S(2)}) copy-start(bf16[4,4,160,128]{3,2,1,0:T(8,128)(2,1)} %copy-done.22) | copy-start | bytes 1966084
  121.0 14.4 %collective-permute-start.19 = (bf16[512,512]{1,0:T(8,128)(2,1)S(1)}, bf16[512,512]{1,0:T(8,128)(2,1)S(1)}, u32[]{:S(2)}, u32[]{:S(2)}) collective-permute-start(bf16[512,512]{1,0:T(8,128)(2,1)S(1)} %add_convert_fusion.4), channel_id=1, source_target_pairs={{0,8},{4,12},{8,0},{12,4},{16,24},{20,28},{24,16},{28,20},{1,9},{5... | collective-permute-start | bytes 1572872 | tf_op jit(solution)/shard_map/ppermute | solution.py:362
  141.2 4.2 %collective-permute-start.21 = (bf16[512,2048]{1,0:T(8,128)(2,1)S(1)}, bf16[512,2048]{1,0:T(8,128)(2,1)S(1)}, u32[]{:S(2)}, u32[]{:S(2)}) collective-permute-start(bf16[512,2048]{1,0:T(8,128)(2,1)S(1)} %shard_map.204), channel_id=1, source_target_pairs={{0,1},{1,0},{2,3},{3,2},{4,5},{5,4},{6,7},{7,6},{8,9},{9,8},{10,11... | collective-permute-start | bytes 6291464 | tf_op jit(solution)/shard_map/ppermute | solution.py:362
  141.3 20.0 %collective-permute-start.22 = (bf16[384,1024]{1,0:T(8,128)(2,1)S(1)}, bf16[384,1024]{1,0:T(8,128)(2,1)S(1)}, u32[]{:S(2)}, u32[]{:S(2)}) collective-permute-start(bf16[384,1024]{1,0:T(8,128)(2,1)S(1)} %multiply_convert_fusion.3), channel_id=1, source_target_pairs={{0,4},{4,0},{8,12},{12,8},{16,20},{20,16},{24,28},{28,24},{1,5},{5... | collective-permute-start | bytes 2359304 | tf_op jit(solution)/shard_map/ppermute | solution.py:362
  142.2 39.5 %collective-permute-start.25 = (bf16[512,256]{1,0:T(8,128)(2,1)S(1)}, bf16[512,256]{1,0:T(8,128)(2,1)S(1)}, u32[]{:S(2)}, u32[]{:S(2)}) collective-permute-start(bf16[512,256]{1,0:T(8,128)(2,1)S(1)} %add_convert_fusion.7), channel_id=1, source_target_pairs={{0,16},{4,20},{8,24},{12,28},{16,0},{20,4},{24,8},{28,12},{1,17},{... | collective-permute-start | bytes 786440 | tf_op jit(solution)/shard_map/ppermute | solution.py:362
  142.5 19.9 %collective-permute-start.23 = (bf16[264,1024]{1,0:T(8,128)(2,1)S(1)}, bf16[264,1024]{1,0:T(8,128)(2,1)S(1)}, u32[]{:S(2)}, u32[]{:S(2)}) collective-permute-start(bf16[264,1024]{1,0:T(8,128)(2,1)S(1)} %pad_maximum_fusion.4), channel_id=1, source_target_pairs={{0,8},{4,12},{8,0},{12,4},{16,24},{20,28},{24,16},{28,20},{1,9},{5... | collective-permute-start | bytes 1622024 | tf_op jit(solution)/shard_map/ppermute | solution.py:362
  162.6 18.1 %collective-permute-start.26 = (bf16[264,512]{1,0:T(8,128)(2,1)S(1)}, bf16[264,512]{1,0:T(8,128)(2,1)S(1)}, u32[]{:S(2)}, u32[]{:S(2)}) collective-permute-start(bf16[264,512]{1,0:T(8,128)(2,1)S(1)} %add_convert_fusion.6), channel_id=1, source_target_pairs={{0,16},{4,20},{8,24},{12,28},{16,0},{20,4},{24,8},{28,12},{1,17},{... | collective-permute-start | bytes 811016 | tf_op jit(solution)/shard_map/ppermute | solution.py:362
  163.7 15.9 %collective-permute-start.27 = (bf16[384,512]{1,0:T(8,128)(2,1)S(1)}, bf16[384,512]{1,0:T(8,128)(2,1)S(1)}, u32[]{:S(2)}, u32[]{:S(2)}) collective-permute-start(bf16[384,512]{1,0:T(8,128)(2,1)S(1)} %add_convert_fusion.5), channel_id=1, source_target_pairs={{0,8},{4,12},{8,0},{12,4},{16,24},{20,28},{24,16},{28,20},{1,9},{5... | collective-permute-start | bytes 1179656 | tf_op jit(solution)/shard_map/ppermute | solution.py:362
  164.8 23.6 %collective-permute-start.24 = (bf16[256,2048]{1,0:T(8,128)(2,1)S(1)}, bf16[256,2048]{1,0:T(8,128)(2,1)S(1)}, u32[]{:S(2)}, u32[]{:S(2)}) collective-permute-start(bf16[256,2048]{1,0:T(8,128)(2,1)S(1)} %slice.233), channel_id=1, source_target_pairs={{0,2},{1,3},{2,0},{3,1},{4,6},{5,7},{6,4},{7,5},{8,10},{9,11},{10,... | collective-permute-start | bytes 3145736 | tf_op jit(solution)/shard_map/ppermute | solution.py:362
  179.7 12.0 %collective-permute-start.29 = (bf16[384,256]{1,0:T(8,128)(2,1)S(1)}, bf16[384,256]{1,0:T(8,128)(2,1)S(1)}, u32[]{:S(2)}, u32[]{:S(2)}) collective-permute-start(bf16[384,256]{1,0:T(8,128)(2,1)S(1)} %add_convert_fusion.9), channel_id=1, source_target_pairs={{0,16},{4,20},{8,24},{12,28},{16,0},{20,4},{24,8},{28,12},{1,17},{... | collective-permute-start | bytes 589832 | tf_op jit(solution)/shard_map/ppermute | solution.py:362
  180.8 9.0 %collective-permute-start.28 = (bf16[264,256]{1,0:T(8,128)(2,1)S(1)}, bf16[264,256]{1,0:T(8,128)(2,1)S(1)}, u32[]{:S(2)}, u32[]{:S(2)}) collective-permute-start(bf16[264,256]{1,0:T(8,128)(2,1)S(1)} %add_convert_fusion.10), channel_id=1, source_target_pairs={{0,4},{4,0},{8,12},{12,8},{16,20},{20,16},{24,28},{28,24},{1,5},{5... | collective-permute-start | bytes 405512 | tf_op jit(solution)/shard_map/ppermute | solution.py:362
  (47 other events, 242.0 us)

commit v4 on v3

--- a/solution.py
+++ b/solution.py
@@ -347,7 +347,7 @@
         ),
         input_output_aliases=alias or {},
         compiler_params=pltpu.CompilerParams(
-            dimension_semantics=("arbitrary",), vmem_limit_bytes=16 << 20
+            dimension_semantics=("arbitrary",), vmem_limit_bytes=28 << 20
         ),
         cost_estimate=pl.CostEstimate(flops=0, bytes_accessed=0, transcendentals=0),
     )(place, *inputs)

time: 194 us -> 194 us (level)
  no operation moved by 1% of the time
where the time goes in v4:
time: 194 us; the launch traced here: 193 us
  Pallas kernels  55.3 us (29%)
  waiting for transfers between devices  48.3 us (25%)
  matrix products  33.2 us (17%)
  starting transfers between devices  30.7 us (16%)
  other arithmetic  13.8 us (7%)
  local copies, waits for them, and re-layouts  9.87 us (5%)
    pallas_call x8, Pallas kernels, call(): pl.pallas_call(kernel, out_shape=out_shapes, grid_spec=pltpu.PrefetchScal...  55.3 us
    ppermute x25, waiting for transfers between devices, flip(): return lax.ppermute(x, axis, [(i, i ^ mask) for i in range(n)])  48.3 us
    ppermute x25, starting transfers between devices, flip(): return lax.ppermute(x, axis, [(i, i ^ mask) for i in range(n)])  26.6 us
    dot_general x7, matrix products, mm(): return jnp.dot(a, b, preferred_element_type=f32)  11.8 us
    dot_general x5, matrix products, mm_nt(): return lax.dot_general(a, b, CONTRACT_COLS, preferred_element_type=f32)  11.3 us
    dot_general x8, matrix products, mm_tn(): return lax.dot_general(a, b, CONTRACT_ROWS, preferred_element_type=f32)  10.1 us
    unnamed x99, local copies, waits for them, and re-layouts  5.05 us
  transfers between devices with their start and end apart: 30, of which 8 were waited for; matrix products, arithmetic and copies ran while one was open for 23% of the time, Pallas kernels for 24%

profile of v4, /device:TPU:0, one launch (start us, length us, event | category | flops | bytes accessed | tf_op | source)
XLA Modules:
  0.0 192.8 jit_solution(1465568123591351250)
XLA Ops:
  1.2 2.6 %collective-permute-start.1 = (bf16[256,2048]{1,0:T(8,128)(2,1)}, bf16[256,2048]{1,0:T(8,128)(2,1)}, u32[]{:S(2)}, u32[]{:S(2)}) collective-permute-start(bf16[256,2048]{1,0:T(8,128)(2,1)} %refs_1_.1), channel_id=1, source_target_pairs={{0,2},{1,3},{2,0},{3,1},{4,6},{5,7},{6,4},{7,5},{8,10},{9,11},{10,... | collective-permute-start | bytes 3145736 | tf_op jit(solution)/shard_map/ppermute | solution.py:362
  3.9 2.7 %convolution_convert_fusion.8 = bf16[256,512]{1,0:T(8,128)(2,1)} fusion(bf16[256,2048]{1,0:T(8,128)(2,1)} %refs_1_, bf16[512,2048]{1,0:T(8,128)(2,1)S(1)} %copy-done), kind=kOutput, calls=%fused_computation.25 | convolution fusion | flops 537001984 | bytes 3407872 | tf_op jit(solution)/shard_map/dot_general | solution.py:29
  9.6 2.0 %copy.28 = bf16[2048,64]{1,0:T(8,128)(2,1)} copy(bf16[2048,64]{0,1:T(8,128)(2,1)} %param.16) | data formatting | bytes 524288 | tf_op jit(solution)/shard_map/optimization_barrier | solution.py:366
  11.6 2.3 %pad_maximum_fusion.right_ref = bf16[2048,640]{1,0:T(8,128)(2,1)S(1)} fusion(bf16[2048,64]{1,0:T(8,128)(2,1)} %copy.28, bf16[2048,64]{1,0:T(8,128)(2,1)} %copy.27, bf16[2048,512]{1,0:T(8,128)(2,1)} %param.17), kind=kLoop, calls=%fused_computation.3 | loop fusion | flops 7864320 | bytes 5242880 | tf_op jit(solution)/shard_map/concatenate | solution.py:537
  13.9 1.7 fusion.4.refs_1_
  15.6 2.9 %fusion.5.refs_2_ = bf16[256,640]{1,0:T(8,128)(2,1)} fusion(bf16[256,2048]{1,0:T(8,128)(2,1)} %collective-permute-done.refs_3_, bf16[2048,640]{1,0:T(8,128)(2,1)S(1)} %pad_maximum_fusion.right_ref), kind=kOutput, calls=%fused_computation.27 | convolution fusion | flops 671252480 | bytes 3997696 | tf_op jit(solution)/shard_map/dot_general | solution.py:25
  19.4 2.7 %convolution_convert_fusion.7 = bf16[256,512]{1,0:T(8,128)(2,1)} fusion(bf16[256,2048]{1,0:T(8,128)(2,1)} %collective-permute-done.6.refs_3_, bf16[512,2048]{1,0:T(8,128)(2,1)S(1)} %copy-done), kind=kOutput, calls=%fused_computation.24 | convolution fusion | flops 537001984 | bytes 3407872 | tf_op jit(solution)/shard_map/dot_general | solution.py:29
  22.5 5.5 %collective-permute-done.1.refs_2_ = bf16[256,2048]{1,0:T(8,128)(2,1)} collective-permute-done((bf16[256,2048]{1,0:T(8,128)(2,1)}, bf16[256,2048]{1,0:T(8,128)(2,1)}, u32[]{:S(2)}, u32[]{:S(2)}) %collective-permute-start.1) | collective-permute-done | bytes 1048608 | tf_op jit(solution)/shard_map/ppermute | solution.py:362
  28.0 3.2 %convolution_convert_fusion.4.refs_3_ = bf16[256,640]{1,0:T(8,128)(2,1)S(1)} fusion(bf16[256,2048]{1,0:T(8,128)(2,1)} %collective-permute-done.1.refs_2_, bf16[2048,640]{1,0:T(8,128)(2,1)} %copy-done.2), kind=kOutput, calls=%fused_computation.17 | convolution fusion | flops 671252480 | bytes 3997696 | tf_op jit(solution)/shard_map/dot_general | solution.py:25
  33.9 5.6 %shard_map.197 = (bf16[1024,128]{1,0:T(8,128)(2,1)S(1)}, bf16[1024,512]{1,0:T(8,128)(2,1)S(1)}, bf16[1024,512]{1,0:T(8,128)(2,1)S(1)}, bf16[4,4,160,128]{3,2,1,0:T(8,128)(2,1)S(1)}, bf16[4,160,128]{2,1,0:T(8,128)(2,1)S(1)}) custom-call(s32[1]{0:T(128)} %bitcast.refs_0_._, bf16[256,640]{1,0:T(8,128)(2,1)S(1)} %copy-done.26, bf16[256,640]{1,0:T(8,128)(2,1)S(1)} %copy-done.27, ...), custom_call_target="tpu_custom_call" | custom-call | tf_op jit(solution)/shard_map/pallas_call | solution.py:338
  41.1 7.7 %shard_map.198 = (bf16[1024,512]{1,0:T(8,128)(2,1)}, bf16[1024,1024]{1,0:T(8,128)(2,1)}, bf16[4,256,1024]{2,1,0:T(8,128)(2,1)}, bf16[4,1024,256]{2,1,0:T(8,128)(...) custom-call(s32[1]{0:T(128)} %bitcast.refs_0_._, ...), custom_call_target="tpu_custom_call" | custom-call | tf_op jit(solution)/shard_map/pallas_call | solution.py:338
  50.5 4.5 %collective-permute-done.9 = bf16[4,160,128]{2,1,0:T(8,128)(2,1)S(1)} collective-permute-done((bf16[4,160,128]{2,1,0:T(8,128)(2,1)S(1)}, bf16[4,160,128]{2,1,0:T(8,128)(2,1)S(1)}, u32[]{:S(2)}, u32[]{:S(2)}) %collective-permute-start.9) | collective-permute-done | bytes 163872 | tf_op jit(solution)/shard_map/ppermute | solution.py:362
  57.1 2.9 %collective-permute-start.10 = (bf16[4,160,128]{2,1,0:T(8,128)(2,1)}, bf16[4,160,128]{2,1,0:T(8,128)(2,1)S(1)}, u32[]{:S(2)}, u32[]{:S(2)}) collective-permute-start(bf16[4,160,128]{2,1,0:T(8,128)(2,1)} %convert_add_fusion.3), channel_id=1, source_target_pairs={{0,16},{4,20},{8,24},{12,28},{16,0},{20,4},{24,8},{28,12},{1,17},{... | collective-permute-start | bytes 491528 | tf_op jit(solution)/shard_map/ppermute | solution.py:362
  60.0 2.0 %fusion.6 = bf16[1,256,512]{2,1,0:T(8,128)(2,1)S(1)} fusion(bf16[256,2048]{1,0:T(8,128)(2,1)} %collective-permute-done.11.refs_2_, bf16[512,2048]{1,0:T(8,128)(2,1)S(1)} %copy-done), kind=kOutput, calls=%fused_computation.28 | convolution fusion | flops 537001984 | bytes 3407872 | tf_op jit(solution)/shard_map/dot_general | solution.py:29
  62.1 2.1 %fusion.7 = bf16[1,256,512]{2,1,0:T(8,128)(2,1)S(1)} fusion(bf16[256,2048]{1,0:T(8,128)(2,1)} %collective-permute-done.12.refs_4_, bf16[512,2048]{1,0:T(8,128)(2,1)S(1)} %copy-done), kind=kOutput, calls=%fused_computation.29 | convolution fusion | flops 537001984 | bytes 3407872 | tf_op jit(solution)/shard_map/dot_general | solution.py:29
  64.4 7.9 %shard_map.199 = (bf16[1024,1024]{1,0:T(8,128)(2,1)}, bf16[1024,1024]{1,0:T(8,128)(2,1)}) custom-call(s32[8]{0:T(128)S(1)} %broadcast_xor_fusion.refs_0_, bf16[256,2048]{1,0:T(8,128)(2,1)S(1)} %copy-done.13, bf16[256,2048]{1,0:T(8,128)(2,1)} %collective-permute-done.11.refs_2_, bf16[256,2048]{1,0:T(8,128)(2,1)} %collective-permute-done.6.refs_3_, ...), custom_call_target="tpu_custom_call" | custom-call | tf_op jit(solution)/shard_map/pallas_call | solution.py:338
  72.5 7.2 %shard_map.200 = (bf16[2,256,512]{2,1,0:T(8,128)(2,1)S(1)}, bf16[2,256,512]{2,1,0:T(8,128)(2,1)S(1)}, bf16[1024,512]{1,0:T(8,128)(2,1)S(1)}, bf16[4,4,160,128]{3...) custom-call(s32[1]{0:T(128)} %bitcast.refs_0_._, ...), custom_call_target="tpu_custom_call" | custom-call | tf_op jit(solution)/shard_map/pallas_call | solution.py:338
  82.9 7.3 %shard_map.201 = (bf16[1024,1024]{1,0:T(8,128)(2,1)}, bf16[1024,1024]{1,0:T(8,128)(2,1)}) custom-call(s32[8]{0:T(128)S(1)} %broadcast_xor_fusion.refs_0_, bf16[256,2048]{1,0:T(8,128)(2,1)S(1)} %copy-done.11, bf16[256,2048]{1,0:T(8,128)(2,1)} %collective-permute-done.1.refs_2_, bf16[256,2048]{1,0:T(8,128)(2,1)} %collective-permute-done.refs_3_, ...), custom_call_target="tpu_custom_call" | custom-call | tf_op jit(solution)/shard_map/pallas_call | solution.py:338
  91.8 2.3 %multiply_convert_fusion.1 = bf16[512,1024]{1,0:T(8,128)(2,1)} fusion(bf16[1024,512]{1,0:T(8,128)(2,1)S(1)} %pad_maximum_fusion.2, bf16[1024,1024]{1,0:T(8,128)(2,1)S(1)} %copy-done.40), kind=kOutput, calls=%fused_computation.7 | convolution fusion | flops 1074790400 | bytes 4194304 | tf_op jit(solution)/shard_map/dot_general | solution.py:33
  98.7 2.2 %multiply_convert_fusion = bf16[512,1024]{1,0:T(8,128)(2,1)} fusion(bf16[1024,512]{1,0:T(8,128)(2,1)S(1)} %pad_maximum_fusion.2, bf16[1024,1024]{1,0:T(8,128)(2,1)S(1)} %copy-done.39), kind=kOutput, calls=%fused_computation.6 | convolution fusion | flops 1074790400 | bytes 4194304 | tf_op jit(solution)/shard_map/dot_general | solution.py:33
  103.2 10.1 %shard_map.202 = (f32[1024,128]{1,0:T(8,128)S(1)}, bf16[1024,512]{1,0:T(8,128)(2,1)S(1)}) custom-call(s32[1]{0:T(128)} %bitcast.refs_0_._, bf16[1024,128]{1,0:T(8,128)(2,1)S(1)} %get-tuple-element.105.refs_1_.refs_7_.refs_2_, bf16[1024,512]{1,0:T(8,128)(2,1)} %copy-done.5, bf16[1024,512]{1,0:T(8,128)(2,1)S(1)} %copy-done.18, ...), custom_call_target="tpu_custom_call" | custom-call | tf_op jit(solution)/shard_map/pallas_call | solution.py:338
  113.4 6.3 %collective-permute-done.16 = bf16[512,1024]{1,0:T(8,128)(2,1)} collective-permute-done((bf16[512,1024]{1,0:T(8,128)(2,1)}, bf16[512,1024]{1,0:T(8,128)(2,1)}, u32[]{:S(2)}, u32[]{:S(2)}) %collective-permute-start.16) | collective-permute-done | bytes 1048608 | tf_op jit(solution)/shard_map/ppermute | solution.py:362
  122.7 7.4 %shard_map.203 = (bf16[4,256,384]{2,1,0:T(8,128)(2,1)S(1)}, bf16[4,256,256]{2,1,0:T(8,128)(2,1)S(1)}, bf16[2,256,640]{2,1,0:T(8,128)(2,1)S(1)}, bf16[2,256,640]{2,1,0:T(8,128)(2,1)S(1)}, f32[8,512]{1,0:T(8,128)S(1)}) custom-call(s32[1]{0:T(128)} %bitcast.refs_0_._, f32[1024,128]{1,0:T(8,128)S(1)} %get-tuple-element.113.refs_1_, ...), custom_call_target="tpu_custom_call" | custom-call | tf_op jit(solution)/shard_map/pallas_call | solution.py:338
  132.6 2.7 %multiply_convert_fusion.3 = bf16[384,1024]{1,0:T(8,128)(2,1)S(1)} fusion(bf16[1024,384]{1,0:T(8,128)(2,1)S(1)} %bitcast.66, bf16[1024,1024]{1,0:T(8,128)(2,1)} %get-tuple-element.99), kind=kOutput, calls=%fused_computation.9 | convolution fusion | flops 806092800 | bytes 3670016 | tf_op jit(solution)/shard_map/dot_general | solution.py:33
  139.0 2.2 %shard_map.204 = bf16[512,2048]{1,0:T(8,128)(2,1)S(1)} custom-call(s32[1]{0:T(128)} %bitcast.refs_0_._, bf16[512,640]{1,0:T(8,128)(2,1)S(1)} %bitcast.68, bf16[2048,640]{1,0:T(8,128)(2,1)S(1)} %copy-done.4), custom_call_target="tpu_custom_call" | custom-call | tf_op jit(solution)/shard_map/pallas_call | solution.py:338
  143.4 2.0 %collective-permute-done.21 = bf16[512,2048]{1,0:T(8,128)(2,1)S(1)} collective-permute-done((bf16[512,2048]{1,0:T(8,128)(2,1)S(1)}, bf16[512,2048]{1,0:T(8,128)(2,1)S(1)}, u32[]{:S(2)}, u32[]{:S(2)}) %collective-permute-start.21) | collective-permute-done | bytes 2097184 | tf_op jit(solution)/shard_map/ppermute | solution.py:362
  145.4 1.8 add_convert_fusion
  148.2 13.0 %collective-permute-done.22 = bf16[384,1024]{1,0:T(8,128)(2,1)S(1)} collective-permute-done((bf16[384,1024]{1,0:T(8,128)(2,1)S(1)}, bf16[384,1024]{1,0:T(8,128)(2,1)S(1)}, u32[]{:S(2)}, u32[]{:S(2)}) %collective-permute-start.22) | collective-permute-done | bytes 786464 | tf_op jit(solution)/shard_map/ppermute | solution.py:362
  166.2 2.6 %add_convert_fusion.3 = bf16[256,2048]{1,0:T(8,128)(2,1)} fusion(bf16[256,2048]{1,0:T(8,128)(2,1)} %collective-permute-done.20, bf16[512,2048]{1,0:T(8,128)(2,1)S(1)} %copy-done.36), kind=kLoop, calls=%fused_computation.5 | loop fusion | flops 2097152 | bytes 3145728 | tf_op jit(solution)/shard_map/convert_element_type | solution.py:749
  168.8 10.8 %collective-permute-done.27 = bf16[384,512]{1,0:T(8,128)(2,1)S(1)} collective-permute-done((bf16[384,512]{1,0:T(8,128)(2,1)S(1)}, bf16[384,512]{1,0:T(8,128)(2,1)S(1)}, u32[]{:S(2)}, u32[]{:S(2)}) %collective-permute-start.27) | collective-permute-done | bytes 393248 | tf_op jit(solution)/shard_map/ppermute | solution.py:362
  181.7 1.8 convert_add_fusion
  183.5 4.9 %collective-permute-done.24 = bf16[256,2048]{1,0:T(8,128)(2,1)S(1)} collective-permute-done((bf16[256,2048]{1,0:T(8,128)(2,1)S(1)}, bf16[256,2048]{1,0:T(8,128)(2,1)S(1)}, u32[]{:S(2)}, u32[]{:S(2)}) %collective-permute-start.24) | collective-permute-done | bytes 1048608 | tf_op jit(solution)/shard_map/ppermute | solution.py:362
  (197 shorter events, 48.3 us)
Async XLA Ops:
  0.7 5.9 %collective-permute-start = (bf16[256,2048]{1,0:T(8,128)(2,1)}, bf16[256,2048]{1,0:T(8,128)(2,1)}, u32[]{:S(2)}, u32[]{:S(2)}) collective-permute-start(bf16[256,2048]{1,0:T(8,128)(2,1)} %refs_1_.1), channel_id=1, source_target_pairs={{0,1},{1,0},{2,3},{3,2},{4,5},{5,4},{6,7},{7,6},{8,9},{9,8},{10,11... | collective-permute-start | bytes 3145736 | tf_op jit(solution)/shard_map/ppermute | solution.py:362
  1.2 26.8 %collective-permute-start.1 = (bf16[256,2048]{1,0:T(8,128)(2,1)}, bf16[256,2048]{1,0:T(8,128)(2,1)}, u32[]{:S(2)}, u32[]{:S(2)}) collective-permute-start(bf16[256,2048]{1,0:T(8,128)(2,1)} %refs_1_.1), channel_id=1, source_target_pairs={{0,2},{1,3},{2,0},{3,1},{4,6},{5,7},{6,4},{7,5},{8,10},{9,11},{10,... | collective-permute-start | bytes 3145736 | tf_op jit(solution)/shard_map/ppermute | solution.py:362
  3.8 14.8 %collective-permute-start.6 = (bf16[256,2048]{1,0:T(8,128)(2,1)}, bf16[256,2048]{1,0:T(8,128)(2,1)}, u32[]{:S(2)}, u32[]{:S(2)}) collective-permute-start(bf16[256,2048]{1,0:T(8,128)(2,1)} %refs_1_), channel_id=1, source_target_pairs={{0,1},{1,0},{2,3},{3,2},{4,5},{5,4},{6,7},{7,6},{8,9},{9,8},{10,11... | collective-permute-start | bytes 3145736 | tf_op jit(solution)/shard_map/ppermute | solution.py:362
  6.6 15.4 %collective-permute-start.5 = (bf16[2,2048]{1,0:T(2,128)(2,1)S(1)}, bf16[2,2048]{1,0:T(2,128)(2,1)S(1)}, u32[]{:S(2)}, u32[]{:S(2)}) collective-permute-start(bf16[2,2048]{1,0:T(2,128)(2,1)S(1)} %slice.171), channel_id=1, source_target_pairs={{3,7},{7,11},{11,15},{15,19},{19,23},{23,27},{27,31}} | collective-permute-start | bytes 24584 | tf_op jit(solution)/shard_map/ppermute | solution.py:530
  7.3 14.7 %collective-permute-start.4 = (bf16[2,2048]{1,0:T(2,128)(2,1)S(1)}, bf16[2,2048]{1,0:T(2,128)(2,1)S(1)}, u32[]{:S(2)}, u32[]{:S(2)}) collective-permute-start(bf16[2,2048]{1,0:T(2,128)(2,1)S(1)} %slice.171), channel_id=1, source_target_pairs={{3,6},{7,10},{11,14},{15,18},{19,22},{23,26},{27,30}} | collective-permute-start | bytes 24584 | tf_op jit(solution)/shard_map/ppermute | solution.py:530
  8.0 14.1 %collective-permute-start.3 = (bf16[2,2048]{1,0:T(2,128)(2,1)S(1)}, bf16[2,2048]{1,0:T(2,128)(2,1)S(1)}, u32[]{:S(2)}, u32[]{:S(2)}) collective-permute-start(bf16[2,2048]{1,0:T(2,128)(2,1)S(1)} %slice.171), channel_id=1, source_target_pairs={{3,5},{7,9},{11,13},{15,17},{19,21},{23,25},{27,29}} | collective-permute-start | bytes 24584 | tf_op jit(solution)/shard_map/ppermute | solution.py:530
  18.6 3.5 %collective-permute-start.2 = (bf16[2,2048]{1,0:T(2,128)(2,1)S(1)}, bf16[2,2048]{1,0:T(2,128)(2,1)S(1)}, u32[]{:S(2)}, u32[]{:S(2)}) collective-permute-start(bf16[2,2048]{1,0:T(2,128)(2,1)S(1)} %slice.171), channel_id=1, source_target_pairs={{3,4},{7,8},{11,12},{15,16},{19,20},{23,24},{27,28}} | collective-permute-start | bytes 24584 | tf_op jit(solution)/shard_map/ppermute | solution.py:530
  28.0 4.9 %collective-permute-start.7 = (bf16[256,2048]{1,0:T(8,128)(2,1)}, bf16[256,2048]{1,0:T(8,128)(2,1)S(1)}, u32[]{:S(2)}, u32[]{:S(2)}) collective-permute-start(bf16[256,2048]{1,0:T(8,128)(2,1)} %collective-permute-done.1.refs_2_), channel_id=1, source_target_pairs={{0,1},{1,0},{2,3},{3,2},{4,5},{5,4},{6,7},{7,6},{8,9},{9,8},{10,11... | collective-permute-start | bytes 3145736 | tf_op jit(solution)/shard_map/ppermute | solution.py:362
  31.2 25.7 %collective-permute-start.11 = (bf16[256,2048]{1,0:T(8,128)(2,1)S(1)}, bf16[256,2048]{1,0:T(8,128)(2,1)}, u32[]{:S(2)}, u32[]{:S(2)}) collective-permute-start(bf16[256,2048]{1,0:T(8,128)(2,1)S(1)} %copy-done.12), channel_id=1, source_target_pairs={{0,2},{1,3},{2,0},{3,1},{4,6},{5,7},{6,4},{7,5},{8,10},{9,11},{10,... | collective-permute-start | bytes 3145736 | tf_op jit(solution)/shard_map/ppermute | solution.py:362
  39.5 22.5 %copy-start.5 = (bf16[1024,512]{1,0:T(8,128)(2,1)}, bf16[1024,512]{1,0:T(8,128)(2,1)S(1)}, u32[]{:S(2)}) copy-start(bf16[1024,512]{1,0:T(8,128)(2,1)S(1)} %get-tuple-element.80.refs_2_.refs_4_) | copy-start | bytes 3145732
  39.5 9.3 %collective-permute-start.8 = (bf16[4,160,128]{2,1,0:T(8,128)(2,1)S(1)}, bf16[4,160,128]{2,1,0:T(8,128)(2,1)S(1)}, u32[]{:S(2)}, u32[]{:S(2)}) collective-permute-start(bf16[4,160,128]{2,1,0:T(8,128)(2,1)S(1)} %get-tuple-element.85), channel_id=1, source_target_pairs={{0,4},{4,0},{8,12},{12,8},{16,20},{20,16},{24,28},{28,24},{1,5},{5... | collective-permute-start | bytes 491528 | tf_op jit(solution)/shard_map/ppermute | solution.py:362
  48.9 6.1 %collective-permute-start.9 = (bf16[4,160,128]{2,1,0:T(8,128)(2,1)S(1)}, bf16[4,160,128]{2,1,0:T(8,128)(2,1)S(1)}, u32[]{:S(2)}, u32[]{:S(2)}) collective-permute-start(bf16[4,160,128]{2,1,0:T(8,128)(2,1)S(1)} %fusion.18), channel_id=1, source_target_pairs={{0,8},{4,12},{8,0},{12,4},{16,24},{20,28},{24,16},{28,20},{1,9},{5... | collective-permute-start | bytes 491528 | tf_op jit(solution)/shard_map/ppermute | solution.py:362
  57.0 5.1 %collective-permute-start.12 = (bf16[256,2048]{1,0:T(8,128)(2,1)}, bf16[256,2048]{1,0:T(8,128)(2,1)}, u32[]{:S(2)}, u32[]{:S(2)}) collective-permute-start(bf16[256,2048]{1,0:T(8,128)(2,1)} %collective-permute-done.11.refs_2_), channel_id=1, source_target_pairs={{0,1},{1,0},{2,3},{3,2},{4,5},{5,4},{6,7},{7,6},{8,9},{9,8},{10,11... | collective-permute-start | bytes 3145736 | tf_op jit(solution)/shard_map/ppermute | solution.py:362
  57.1 15.2 %collective-permute-start.10 = (bf16[4,160,128]{2,1,0:T(8,128)(2,1)}, bf16[4,160,128]{2,1,0:T(8,128)(2,1)S(1)}, u32[]{:S(2)}, u32[]{:S(2)}) collective-permute-start(bf16[4,160,128]{2,1,0:T(8,128)(2,1)} %convert_add_fusion.3), channel_id=1, source_target_pairs={{0,16},{4,20},{8,24},{12,28},{16,0},{20,4},{24,8},{28,12},{1,17},{... | collective-permute-start | bytes 491528 | tf_op jit(solution)/shard_map/ppermute | solution.py:362
  81.1 9.1 %collective-permute-start.13 = (bf16[512,2048]{1,0:T(8,128)(2,1)S(1)}, bf16[512,2048]{1,0:T(8,128)(2,1)S(1)}, u32[]{:S(2)}, u32[]{:S(2)}) collective-permute-start(bf16[512,2048]{1,0:T(8,128)(2,1)S(1)} %convolution_convert_fusion), channel_id=1, source_target_pairs={{0,1},{1,0},{2,3},{3,2},{4,5},{5,4},{6,7},{7,6},{8,9},{9,8},{10,11... | collective-permute-start | bytes 6291464 | tf_op jit(solution)/shard_map/ppermute | solution.py:362
  81.3 8.9 %collective-permute-start.14 = (bf16[4,160,128]{2,1,0:T(8,128)(2,1)S(1)}, bf16[4,160,128]{2,1,0:T(8,128)(2,1)S(1)}, u32[]{:S(2)}, u32[]{:S(2)}) collective-permute-start(bf16[4,160,128]{2,1,0:T(8,128)(2,1)S(1)} %get-tuple-element.96), channel_id=1, source_target_pairs={{0,4},{4,0},{8,12},{12,8},{16,20},{20,16},{24,28},{28,24},{1,5},{5... | collective-permute-start | bytes 491528 | tf_op jit(solution)/shard_map/ppermute | solution.py:362
  94.1 25.7 %collective-permute-start.16 = (bf16[512,1024]{1,0:T(8,128)(2,1)}, bf16[512,1024]{1,0:T(8,128)(2,1)}, u32[]{:S(2)}, u32[]{:S(2)}) collective-permute-start(bf16[512,1024]{1,0:T(8,128)(2,1)} %multiply_convert_fusion.1), channel_id=1, source_target_pairs={{0,4},{4,0},{8,12},{12,8},{16,20},{20,16},{24,28},{28,24},{1,5},{5... | collective-permute-start | bytes 3145736 | tf_op jit(solution)/shard_map/ppermute | solution.py:362
  94.7 6.2 %collective-permute-start.15 = (bf16[4,160,128]{2,1,0:T(8,128)(2,1)S(1)}, bf16[4,160,128]{2,1,0:T(8,128)(2,1)S(1)}, u32[]{:S(2)}, u32[]{:S(2)}) collective-permute-start(bf16[4,160,128]{2,1,0:T(8,128)(2,1)S(1)} %fusion.23), channel_id=1, source_target_pairs={{0,8},{4,12},{8,0},{12,4},{16,24},{20,28},{24,16},{28,20},{1,9},{5... | collective-permute-start | bytes 491528 | tf_op jit(solution)/shard_map/ppermute | solution.py:362
  97.4 35.2 %collective-permute-start.20 = (bf16[256,2048]{1,0:T(8,128)(2,1)}, bf16[256,2048]{1,0:T(8,128)(2,1)}, u32[]{:S(2)}, u32[]{:S(2)}) collective-permute-start(bf16[256,2048]{1,0:T(8,128)(2,1)} %slice.221), channel_id=1, source_target_pairs={{0,2},{1,3},{2,0},{3,1},{4,6},{5,7},{6,4},{7,5},{8,10},{9,11},{10,... | collective-permute-start | bytes 3145736 | tf_op jit(solution)/shard_map/ppermute | solution.py:362
  101.0 12.3 %collective-permute-start.17 = (bf16[4,160,128]{2,1,0:T(8,128)(2,1)S(1)}, bf16[4,160,128]{2,1,0:T(8,128)(2,1)S(1)}, u32[]{:S(2)}, u32[]{:S(2)}) collective-permute-start(bf16[4,160,128]{2,1,0:T(8,128)(2,1)S(1)} %convert_add_fusion.1), channel_id=1, source_target_pairs={{0,16},{4,20},{8,24},{12,28},{16,0},{20,4},{24,8},{28,12},{1,17},{... | collective-permute-start | bytes 491528 | tf_op jit(solution)/shard_map/ppermute | solution.py:362
  101.9 20.7 %collective-permute-start.18 = (f32[8,640]{1,0:T(8,128)S(1)}, f32[8,640]{1,0:T(8,128)S(1)}, u32[]{:S(2)}, u32[]{:S(2)}) collective-permute-start(f32[8,640]{1,0:T(8,128)S(1)} %get-tuple-element.116), channel_id=1, source_target_pairs={{4,0},{8,4},{12,8},{16,12},{20,16},{24,20},{28,24},{5,1},{9,5},{13... | collective-permute-start | bytes 61448 | tf_op jit(solution)/shard_map/ppermute | solution.py:661
  103.2 19.4 %copy-start.23 = (bf16[4,4,160,128]{3,2,1,0:T(8,128)(2,1)S(1)}, bf16[4,4,160,128]{3,2,1,0:T(8,128)(2,1)}, u32[]{:S(2)}) copy-start(bf16[4,4,160,128]{3,2,1,0:T(8,128)(2,1)} %copy-done.22) | copy-start | bytes 1966084
  121.0 14.4 %collective-permute-start.19 = (bf16[512,512]{1,0:T(8,128)(2,1)S(1)}, bf16[512,512]{1,0:T(8,128)(2,1)S(1)}, u32[]{:S(2)}, u32[]{:S(2)}) collective-permute-start(bf16[512,512]{1,0:T(8,128)(2,1)S(1)} %add_convert_fusion.4), channel_id=1, source_target_pairs={{0,8},{4,12},{8,0},{12,4},{16,24},{20,28},{24,16},{28,20},{1,9},{5... | collective-permute-start | bytes 1572872 | tf_op jit(solution)/shard_map/ppermute | solution.py:362
  141.2 4.2 %collective-permute-start.21 = (bf16[512,2048]{1,0:T(8,128)(2,1)S(1)}, bf16[512,2048]{1,0:T(8,128)(2,1)S(1)}, u32[]{:S(2)}, u32[]{:S(2)}) collective-permute-start(bf16[512,2048]{1,0:T(8,128)(2,1)S(1)} %shard_map.204), channel_id=1, source_target_pairs={{0,1},{1,0},{2,3},{3,2},{4,5},{5,4},{6,7},{7,6},{8,9},{9,8},{10,11... | collective-permute-start | bytes 6291464 | tf_op jit(solution)/shard_map/ppermute | solution.py:362
  141.3 20.0 %collective-permute-start.22 = (bf16[384,1024]{1,0:T(8,128)(2,1)S(1)}, bf16[384,1024]{1,0:T(8,128)(2,1)S(1)}, u32[]{:S(2)}, u32[]{:S(2)}) collective-permute-start(bf16[384,1024]{1,0:T(8,128)(2,1)S(1)} %multiply_convert_fusion.3), channel_id=1, source_target_pairs={{0,4},{4,0},{8,12},{12,8},{16,20},{20,16},{24,28},{28,24},{1,5},{5... | collective-permute-start | bytes 2359304 | tf_op jit(solution)/shard_map/ppermute | solution.py:362
  142.2 39.5 %collective-permute-start.25 = (bf16[512,256]{1,0:T(8,128)(2,1)S(1)}, bf16[512,256]{1,0:T(8,128)(2,1)S(1)}, u32[]{:S(2)}, u32[]{:S(2)}) collective-permute-start(bf16[512,256]{1,0:T(8,128)(2,1)S(1)} %add_convert_fusion.7), channel_id=1, source_target_pairs={{0,16},{4,20},{8,24},{12,28},{16,0},{20,4},{24,8},{28,12},{1,17},{... | collective-permute-start | bytes 786440 | tf_op jit(solution)/shard_map/ppermute | solution.py:362
  142.5 19.9 %collective-permute-start.23 = (bf16[264,1024]{1,0:T(8,128)(2,1)S(1)}, bf16[264,1024]{1,0:T(8,128)(2,1)S(1)}, u32[]{:S(2)}, u32[]{:S(2)}) collective-permute-start(bf16[264,1024]{1,0:T(8,128)(2,1)S(1)} %pad_maximum_fusion.4), channel_id=1, source_target_pairs={{0,8},{4,12},{8,0},{12,4},{16,24},{20,28},{24,16},{28,20},{1,9},{5... | collective-permute-start | bytes 1622024 | tf_op jit(solution)/shard_map/ppermute | solution.py:362
  162.6 18.1 %collective-permute-start.26 = (bf16[264,512]{1,0:T(8,128)(2,1)S(1)}, bf16[264,512]{1,0:T(8,128)(2,1)S(1)}, u32[]{:S(2)}, u32[]{:S(2)}) collective-permute-start(bf16[264,512]{1,0:T(8,128)(2,1)S(1)} %add_convert_fusion.6), channel_id=1, source_target_pairs={{0,16},{4,20},{8,24},{12,28},{16,0},{20,4},{24,8},{28,12},{1,17},{... | collective-permute-start | bytes 811016 | tf_op jit(solution)/shard_map/ppermute | solution.py:362
  163.7 15.9 %collective-permute-start.27 = (bf16[384,512]{1,0:T(8,128)(2,1)S(1)}, bf16[384,512]{1,0:T(8,128)(2,1)S(1)}, u32[]{:S(2)}, u32[]{:S(2)}) collective-permute-start(bf16[384,512]{1,0:T(8,128)(2,1)S(1)} %add_convert_fusion.5), channel_id=1, source_target_pairs={{0,8},{4,12},{8,0},{12,4},{16,24},{20,28},{24,16},{28,20},{1,9},{5... | collective-permute-start | bytes 1179656 | tf_op jit(solution)/shard_map/ppermute | solution.py:362
  164.8 23.6 %collective-permute-start.24 = (bf16[256,2048]{1,0:T(8,128)(2,1)S(1)}, bf16[256,2048]{1,0:T(8,128)(2,1)S(1)}, u32[]{:S(2)}, u32[]{:S(2)}) collective-permute-start(bf16[256,2048]{1,0:T(8,128)(2,1)S(1)} %slice.233), channel_id=1, source_target_pairs={{0,2},{1,3},{2,0},{3,1},{4,6},{5,7},{6,4},{7,5},{8,10},{9,11},{10,... | collective-permute-start | bytes 3145736 | tf_op jit(solution)/shard_map/ppermute | solution.py:362
  179.7 12.0 %collective-permute-start.29 = (bf16[384,256]{1,0:T(8,128)(2,1)S(1)}, bf16[384,256]{1,0:T(8,128)(2,1)S(1)}, u32[]{:S(2)}, u32[]{:S(2)}) collective-permute-start(bf16[384,256]{1,0:T(8,128)(2,1)S(1)} %add_convert_fusion.9), channel_id=1, source_target_pairs={{0,16},{4,20},{8,24},{12,28},{16,0},{20,4},{24,8},{28,12},{1,17},{... | collective-permute-start | bytes 589832 | tf_op jit(solution)/shard_map/ppermute | solution.py:362
  180.8 9.0 %collective-permute-start.28 = (bf16[264,256]{1,0:T(8,128)(2,1)S(1)}, bf16[264,256]{1,0:T(8,128)(2,1)S(1)}, u32[]{:S(2)}, u32[]{:S(2)}) collective-permute-start(bf16[264,256]{1,0:T(8,128)(2,1)S(1)} %add_convert_fusion.10), channel_id=1, source_target_pairs={{0,4},{4,0},{8,12},{12,8},{16,20},{20,16},{24,28},{28,24},{1,5},{5... | collective-permute-start | bytes 405512 | tf_op jit(solution)/shard_map/ppermute | solution.py:362
  (47 other events, 242.1 us)
